TPU v7x, 512 devices: a whole 4x4x16 slice. The times are simulated.
512 devices in a mesh: blk: 64 (over z, x_lo, core), rep: 8 (over y, x_hi).
Axes of the slice: x: 4 (x_hi: 2, x_lo: 2; x = x_hi * 2 + x_lo), y: 4, z: 16, core: 2. Of those that a mesh axis runs over, the one named last changes fastest.
Arguments:
- features: bfloat16 [65536, 256], P(('blk', 'rep')), may hold values from -6 to 6
- out_grad: bfloat16 [65536, 256], P('blk'), may hold values from -4 to 4
- weight: bfloat16 [256, 256], replicated, may hold values from -0.375 to 0.375
- block_words: int32 [64, 64, 8, 16, 128], P('blk', 'rep'), may hold values from 0 to 255
- block_coords: int32 [64, 64, 2, 8], P('blk', 'rep'), may hold values from 0 to 7, as said below
- block_counts: int32 [64, 64], P('blk', 'rep'), may hold values from 1 to 8, as said below
- degrees: int32 [65536], P('blk'), may hold values from 1 to 127
Outputs:
- input_grad: bfloat16 [65536, 256], P(('blk', 'rep'))
- weight_grad: float32 [256, 256], replicated
Inputs may be any that keep to these rules, and one draw needn't show every extreme that they name: `block_coords`: within one slab pair the 8 slots name distinct pairs of row block and column block. `block_counts`: the 8 slab pairs of one device include one in which all 8 slots are live.
All inputs are finite; a program needn't handle non-finite values.
Results may differ from a plain program's by a relative error of at most 0.015.
Values may be sent and summed in bfloat16 or wider, within the bound.
A program may use at most 64 MiB of HBM per device.

v0:
```python
import math

import jax
import jax.numpy as jnp
from jax import lax
from jax.sharding import PartitionSpec as P


def from_behind(block, axis, distance):
    devices = range(lax.axis_size(axis))
    route = [((i - distance) % len(devices), i) for i in devices]
    return lax.ppermute(block, axis, route)


def unpack_block(slot_words):
    shifts = jnp.arange(8, dtype=jnp.int32)
    bit_values = jnp.bitwise_and(
        jnp.right_shift(slot_words[:, :, None, :], shifts[None, None, :, None]), 1
    )
    return bit_values.reshape(slot_words.shape[0], 128, 128).astype(jnp.bfloat16)


def per_device(features, out_grad, weight, block_words, block_coords, block_counts, degrees):
    slab_rows, width = out_grad.shape
    row_blocks = slab_rows // 128
    group_size = lax.axis_size("rep")
    step_count = lax.axis_size("blk") // group_size
    rep_index = lax.axis_index("rep")
    inverse_root = lax.rsqrt(degrees.astype(jnp.float32))
    scaled = (out_grad.astype(jnp.float32) * inverse_root[:, None]).astype(jnp.bfloat16)
    column_ids = jnp.arange(row_blocks, dtype=jnp.int32)
    slot_total = block_words.shape[2]
    slot_ids = jnp.arange(slot_total, dtype=jnp.int32)

    def add_slot(accumulated, source_slab, slot_index):
        slot_words = lax.dynamic_index_in_dim(block_words[0], slot_index, 0, keepdims=False)
        coords = lax.dynamic_index_in_dim(block_coords[0], slot_index, 0, keepdims=False)
        live_count = lax.dynamic_index_in_dim(block_counts[0], slot_index, 0, keepdims=False)
        picked = jnp.take(source_slab.reshape(row_blocks, 128, width), coords[0], axis=0)
        transposed = unpack_block(slot_words)
        contrib = jnp.einsum("bvu,buf->bvf", transposed, picked, preferred_element_type=jnp.float32)
        live_slots = slot_ids < live_count
        placement = ((coords[1][:, None] == column_ids[None, :]) & live_slots[:, None]).astype(
            jnp.float32
        )
        return accumulated + jnp.einsum("bc,bvf->cvf", placement, contrib)

    empty = jnp.zeros((row_blocks, 128, width), jnp.float32)
    current = scaled
    for bit in range(group_size.bit_length() - 1):
        shifted = from_behind(current, "blk", -(1 << bit) * step_count)
        current = jnp.where(
            jnp.bitwise_and(jnp.right_shift(rep_index, bit), 1) == 1, shifted, current
        )
    accumulated = add_slot(empty, current, 0)

    def advance(step_index, state_tuple):
        current, accumulated = state_tuple
        current = from_behind(current, "blk", -1)
        return (current, add_slot(accumulated, current, step_index))

    current, accumulated = lax.fori_loop(1, step_count, advance, (current, accumulated))
    partial_sums = accumulated.reshape(slab_rows, width)
    share_rows = slab_rows // group_size
    share_root = lax.dynamic_slice_in_dim(inverse_root, rep_index * share_rows, share_rows, 0)
    whole_sums = lax.psum(partial_sums, "rep")
    own_sums = lax.dynamic_slice_in_dim(whole_sums, rep_index * share_rows, share_rows, 0)
    aggregated = (own_sums * share_root[:, None]).astype(jnp.bfloat16)
    input_grad = lax.dot_general(
        aggregated, weight, (((1,), (1,)), ((), ())), preferred_element_type=jnp.float32
    ).astype(jnp.bfloat16)
    weight_term = lax.dot_general(
        features, aggregated, (((0,), (0,)), ((), ())), preferred_element_type=jnp.float32
    )
    node_total = slab_rows * lax.axis_size("blk")
    weight_grad = lax.psum(weight_term, ("blk", "rep")) * (1.0 / math.sqrt(node_total))
    return (input_grad, weight_grad)


def solution(mesh):
    return jax.shard_map(
        per_device,
        mesh=mesh,
        in_specs=(
            P(("blk", "rep"), None),
            P("blk", None),
            P(),
            P("blk", "rep", None, None, None),
            P("blk", "rep", None, None),
            P("blk", "rep"),
            P("blk"),
        ),
        out_specs=(P(("blk", "rep"), None), P()),
        check_vma=False,
    )
```

profile of v0, /device:TPU:1, one launch (start us, length us, event | category | flops | bytes accessed | tf_op | source)
XLA Modules:
  0.0 820.6 jit_solution(11861567313591803345)
XLA Ops:
  7.2 0.7 convert_rsqrt_fusion
  7.9 1.3 multiply_convert_fusion
  9.3 12.4 %collective-permute-start.1 = (bf16[1024,256]{1,0:T(8,128)(2,1)S(1)}, bf16[1024,256]{1,0:T(8,128)(2,1)S(1)}, u32[]{:S(2)}, u32[]{:S(2)}) collective-permute-start(bf16[1024,256]{1,0:T(8,128)(2,1)S(1)} %multiply_convert_fusion), channel_id=1, source_target_pairs={{64,0},{72,8},{80,16},{88,24},{96,32},{104,40},{112,48},{120,56},{... | collective-permute-start | bytes 1572872 | tf_op jit(solution)/shard_map/ppermute | solution.py:12
  21.7 21.9 %collective-permute-done.1 = bf16[1024,256]{1,0:T(8,128)(2,1)S(1)} collective-permute-done((bf16[1024,256]{1,0:T(8,128)(2,1)S(1)}, bf16[1024,256]{1,0:T(8,128)(2,1)S(1)}, u32[]{:S(2)}, u32[]{:S(2)}) %collective-permute-start.1) | collective-permute-done | bytes 524320 | tf_op jit(solution)/shard_map/ppermute | solution.py:12
  43.9 6.5 collective-permute-start.2
  50.5 0.7 compare_and_fusion.1
  51.2 40.6 %collective-permute-done.2 = bf16[1024,256]{1,0:T(8,128)(2,1)S(1)} collective-permute-done((bf16[1024,256]{1,0:T(8,128)(2,1)S(1)}, bf16[1024,256]{1,0:T(8,128)(2,1)S(1)}, u32[]{:S(2)}, u32[]{:S(2)}) %collective-permute-start.2) | collective-permute-done | bytes 524320 | tf_op jit(solution)/shard_map/ppermute | solution.py:12
  91.9 4.8 collective-permute-start.3
  97.3 0.7 slice_bitcast_fusion.2
  98.0 0.8 slice_bitcast_fusion.1
  98.9 27.5 %collective-permute-done.3 = bf16[1024,256]{1,0:T(8,128)(2,1)S(1)} collective-permute-done((bf16[1024,256]{1,0:T(8,128)(2,1)S(1)}, bf16[1024,256]{1,0:T(8,128)(2,1)S(1)}, u32[]{:S(2)}, u32[]{:S(2)}) %collective-permute-start.3) | collective-permute-done | bytes 524320 | tf_op jit(solution)/shard_map/ppermute | solution.py:12
  127.8 115.9 %while.20 = (s32[]{:T(128)}, bf16[1024,256]{1,0:T(8,128)(2,1)S(1)}, f32[8,128,256]{2,0,1:T(8,128)S(1)}, s32[1,8,2,8]{3,2,1,0:T(2,128)}, s32[1,8]{1,0:T(1,128)S(1...) while((s32[]{:T(128)}, bf16[1024,256]{1,0:T(8,128)(2,1)S(1)}, ...), condition=%wide.region_1.3_spmd.clone.clone, body=%wide.region_0.2_spmd.clone.clone.sunk | while | flops 72221880 | bytes 8067647 | solution.py:62
  127.8 3.7 collective-permute-start
  132.2 0.7 constant_dynamic-slice_fusion.4
  132.9 0.7 iota_compare_fusion.5
  133.6 0.9 dynamic-slice_bitcast_fusion.2
  134.5 5.0 collective-permute-done
  141.0 28.1 %collective-permute-start = (bf16[1024,256]{1,0:T(8,128)(2,1)S(1)}, bf16[1024,256]{1,0:T(8,128)(2,1)S(1)}, u32[]{:S(2)}, u32[]{:S(2)}) collective-permute-start(bf16[1024,256]{1,0:T(8,128)(2,1)S(1)} %get-tuple-element.308), channel_id=1, source_target_pairs={{8,0},{16,8},{24,16},{32,24},{40,32},{48,40},{56,48},{64,56},{72,6... | collective-permute-start | bytes 1572872 | tf_op jit(solution)/shard_map/while/body/eval_jaxpr/ppermute | solution.py:12
  169.6 0.7 constant_dynamic-slice_fusion.4
  170.4 0.7 iota_compare_fusion.5
  171.1 0.9 dynamic-slice_bitcast_fusion.2
  173.4 9.7 %collective-permute-start = (bf16[1024,256]{1,0:T(8,128)(2,1)S(1)}, bf16[1024,256]{1,0:T(8,128)(2,1)S(1)}, u32[]{:S(2)}, u32[]{:S(2)}) collective-permute-start(bf16[1024,256]{1,0:T(8,128)(2,1)S(1)} %get-tuple-element.308), channel_id=1, source_target_pairs={{8,0},{16,8},{24,16},{32,24},{40,32},{48,40},{56,48},{64,56},{72,6... | collective-permute-start | bytes 1572872 | tf_op jit(solution)/shard_map/while/body/eval_jaxpr/ppermute | solution.py:12
  183.7 0.7 constant_dynamic-slice_fusion.4
  184.5 0.7 iota_compare_fusion.5
  185.1 0.9 dynamic-slice_bitcast_fusion.2
  187.4 9.7 %collective-permute-start = (bf16[1024,256]{1,0:T(8,128)(2,1)S(1)}, bf16[1024,256]{1,0:T(8,128)(2,1)S(1)}, u32[]{:S(2)}, u32[]{:S(2)}) collective-permute-start(bf16[1024,256]{1,0:T(8,128)(2,1)S(1)} %get-tuple-element.308), channel_id=1, source_target_pairs={{8,0},{16,8},{24,16},{32,24},{40,32},{48,40},{56,48},{64,56},{72,6... | collective-permute-start | bytes 1572872 | tf_op jit(solution)/shard_map/while/body/eval_jaxpr/ppermute | solution.py:12
  197.7 0.7 constant_dynamic-slice_fusion.4
  198.5 0.7 iota_compare_fusion.5
  199.2 0.9 dynamic-slice_bitcast_fusion.2
  201.5 9.7 %collective-permute-start = (bf16[1024,256]{1,0:T(8,128)(2,1)S(1)}, bf16[1024,256]{1,0:T(8,128)(2,1)S(1)}, u32[]{:S(2)}, u32[]{:S(2)}) collective-permute-start(bf16[1024,256]{1,0:T(8,128)(2,1)S(1)} %get-tuple-element.308), channel_id=1, source_target_pairs={{8,0},{16,8},{24,16},{32,24},{40,32},{48,40},{56,48},{64,56},{72,6... | collective-permute-start | bytes 1572872 | tf_op jit(solution)/shard_map/while/body/eval_jaxpr/ppermute | solution.py:12
  211.8 0.7 constant_dynamic-slice_fusion.4
  212.6 0.7 iota_compare_fusion.5
  213.3 0.9 dynamic-slice_bitcast_fusion.2
  215.6 9.7 %collective-permute-start = (bf16[1024,256]{1,0:T(8,128)(2,1)S(1)}, bf16[1024,256]{1,0:T(8,128)(2,1)S(1)}, u32[]{:S(2)}, u32[]{:S(2)}) collective-permute-start(bf16[1024,256]{1,0:T(8,128)(2,1)S(1)} %get-tuple-element.308), channel_id=1, source_target_pairs={{8,0},{16,8},{24,16},{32,24},{40,32},{48,40},{56,48},{64,56},{72,6... | collective-permute-start | bytes 1572872 | tf_op jit(solution)/shard_map/while/body/eval_jaxpr/ppermute | solution.py:12
  225.9 0.7 constant_dynamic-slice_fusion.4
  226.7 0.7 iota_compare_fusion.5
  227.3 0.9 dynamic-slice_bitcast_fusion.2
  229.6 9.7 %collective-permute-start = (bf16[1024,256]{1,0:T(8,128)(2,1)S(1)}, bf16[1024,256]{1,0:T(8,128)(2,1)S(1)}, u32[]{:S(2)}, u32[]{:S(2)}) collective-permute-start(bf16[1024,256]{1,0:T(8,128)(2,1)S(1)} %get-tuple-element.308), channel_id=1, source_target_pairs={{8,0},{16,8},{24,16},{32,24},{40,32},{48,40},{56,48},{64,56},{72,6... | collective-permute-start | bytes 1572872 | tf_op jit(solution)/shard_map/while/body/eval_jaxpr/ppermute | solution.py:12
  239.9 0.7 constant_dynamic-slice_fusion.4
  240.7 0.7 iota_compare_fusion.5
  241.4 0.9 dynamic-slice_bitcast_fusion.2
  243.7 1.3 copy.10
  245.2 101.7 %all-reduce.3.cloned.1.call-done = f32[1024,256]{1,0:T(8,128)} async-done(((f32[1024,256]{1,0:T(8,128)}), f32[1024,256]{1,0:T(8,128)}) %all-reduce.3.cloned.1.call-update) | async-done | bytes 1048592 | tf_op jit(solution)/shard_map/psum | solution.py:66
  346.9 1.9 convolution_bitcast_fusion
  348.8 1.8 convolution_convert_fusion
  350.6 461.4 %all-reduce.5.cloned.1.call-done = f32[256,256]{0,1:T(8,128)} async-done(((f32[256,256]{0,1:T(8,128)}), f32[256,256]{0,1:T(8,128)}) %all-reduce.5.cloned.1.call-update) | async-done | bytes 262160 | tf_op jit(solution)/shard_map/psum | solution.py:76
  812.0 1.0 broadcast_multiply_fusion
  813.0 0.8 copy.11
  (99 shorter events, 17.5 us)
Async XLA Ops:
  7.2 341.6 %copy-start = (bf16[256,256]{1,0:T(8,128)(2,1)S(1)}, bf16[256,256]{1,0:T(8,128)(2,1)}, u32[]{:S(2)}) copy-start(bf16[256,256]{1,0:T(8,128)(2,1)} %param.13) | copy-start | bytes 393220
  7.2 339.7 %all-reduce.3.cloned.1.call-start = ((), (), s32[]{:S(2)}) async-start(), calls=%async_computation | async-start | bytes 2097152 | tf_op jit(solution)/shard_map/psum | solution.py:66
  7.9 35.6 %copy-start.1 = (bf16[1024,256]{1,0:T(8,128)(2,1)S(1)}, bf16[1024,256]{1,0:T(8,128)(2,1)}, u32[]{:S(2)}) copy-start(bf16[1024,256]{1,0:T(8,128)(2,1)} %param.12) | copy-start | bytes 1572868
  9.3 34.3 %collective-permute-start.1 = (bf16[1024,256]{1,0:T(8,128)(2,1)S(1)}, bf16[1024,256]{1,0:T(8,128)(2,1)S(1)}, u32[]{:S(2)}, u32[]{:S(2)}) collective-permute-start(bf16[1024,256]{1,0:T(8,128)(2,1)S(1)} %multiply_convert_fusion), channel_id=1, source_target_pairs={{64,0},{72,8},{80,16},{88,24},{96,32},{104,40},{112,48},{120,56},{... | collective-permute-start | bytes 1572872 | tf_op jit(solution)/shard_map/ppermute | solution.py:12
  43.9 48.0 %collective-permute-start.2 = (bf16[1024,256]{1,0:T(8,128)(2,1)S(1)}, bf16[1024,256]{1,0:T(8,128)(2,1)S(1)}, u32[]{:S(2)}, u32[]{:S(2)}) collective-permute-start(bf16[1024,256]{1,0:T(8,128)(2,1)S(1)} %broadcast_select_fusion), channel_id=1, source_target_pairs={{128,0},{136,8},{144,16},{152,24},{160,32},{168,40},{176,48},{184,... | collective-permute-start | bytes 1572872 | tf_op jit(solution)/shard_map/ppermute | solution.py:12
  91.9 34.5 %collective-permute-start.3 = (bf16[1024,256]{1,0:T(8,128)(2,1)S(1)}, bf16[1024,256]{1,0:T(8,128)(2,1)S(1)}, u32[]{:S(2)}, u32[]{:S(2)}) collective-permute-start(bf16[1024,256]{1,0:T(8,128)(2,1)S(1)} %broadcast_select_fusion.1), channel_id=1, source_target_pairs={{256,0},{264,8},{272,16},{280,24},{288,32},{296,40},{304,48},{312,... | collective-permute-start | bytes 1572872 | tf_op jit(solution)/shard_map/ppermute | solution.py:12
  96.6 0.7 copy-start.3
  127.8 11.7 %collective-permute-start = (bf16[1024,256]{1,0:T(8,128)(2,1)S(1)}, bf16[1024,256]{1,0:T(8,128)(2,1)S(1)}, u32[]{:S(2)}, u32[]{:S(2)}) collective-permute-start(bf16[1024,256]{1,0:T(8,128)(2,1)S(1)} %get-tuple-element.308), channel_id=1, source_target_pairs={{8,0},{16,8},{24,16},{32,24},{40,32},{48,40},{56,48},{64,56},{72,6... | collective-permute-start | bytes 1572872 | tf_op jit(solution)/shard_map/while/body/eval_jaxpr/ppermute | solution.py:12
  141.0 31.0 %collective-permute-start = (bf16[1024,256]{1,0:T(8,128)(2,1)S(1)}, bf16[1024,256]{1,0:T(8,128)(2,1)S(1)}, u32[]{:S(2)}, u32[]{:S(2)}) collective-permute-start(bf16[1024,256]{1,0:T(8,128)(2,1)S(1)} %get-tuple-element.308), channel_id=1, source_target_pairs={{8,0},{16,8},{24,16},{32,24},{40,32},{48,40},{56,48},{64,56},{72,6... | collective-permute-start | bytes 1572872 | tf_op jit(solution)/shard_map/while/body/eval_jaxpr/ppermute | solution.py:12
  173.4 12.6 %collective-permute-start = (bf16[1024,256]{1,0:T(8,128)(2,1)S(1)}, bf16[1024,256]{1,0:T(8,128)(2,1)S(1)}, u32[]{:S(2)}, u32[]{:S(2)}) collective-permute-start(bf16[1024,256]{1,0:T(8,128)(2,1)S(1)} %get-tuple-element.308), channel_id=1, source_target_pairs={{8,0},{16,8},{24,16},{32,24},{40,32},{48,40},{56,48},{64,56},{72,6... | collective-permute-start | bytes 1572872 | tf_op jit(solution)/shard_map/while/body/eval_jaxpr/ppermute | solution.py:12
  187.4 12.6 %collective-permute-start = (bf16[1024,256]{1,0:T(8,128)(2,1)S(1)}, bf16[1024,256]{1,0:T(8,128)(2,1)S(1)}, u32[]{:S(2)}, u32[]{:S(2)}) collective-permute-start(bf16[1024,256]{1,0:T(8,128)(2,1)S(1)} %get-tuple-element.308), channel_id=1, source_target_pairs={{8,0},{16,8},{24,16},{32,24},{40,32},{48,40},{56,48},{64,56},{72,6... | collective-permute-start | bytes 1572872 | tf_op jit(solution)/shard_map/while/body/eval_jaxpr/ppermute | solution.py:12
  201.5 12.6 %collective-permute-start = (bf16[1024,256]{1,0:T(8,128)(2,1)S(1)}, bf16[1024,256]{1,0:T(8,128)(2,1)S(1)}, u32[]{:S(2)}, u32[]{:S(2)}) collective-permute-start(bf16[1024,256]{1,0:T(8,128)(2,1)S(1)} %get-tuple-element.308), channel_id=1, source_target_pairs={{8,0},{16,8},{24,16},{32,24},{40,32},{48,40},{56,48},{64,56},{72,6... | collective-permute-start | bytes 1572872 | tf_op jit(solution)/shard_map/while/body/eval_jaxpr/ppermute | solution.py:12
  215.6 12.6 %collective-permute-start = (bf16[1024,256]{1,0:T(8,128)(2,1)S(1)}, bf16[1024,256]{1,0:T(8,128)(2,1)S(1)}, u32[]{:S(2)}, u32[]{:S(2)}) collective-permute-start(bf16[1024,256]{1,0:T(8,128)(2,1)S(1)} %get-tuple-element.308), channel_id=1, source_target_pairs={{8,0},{16,8},{24,16},{32,24},{40,32},{48,40},{56,48},{64,56},{72,6... | collective-permute-start | bytes 1572872 | tf_op jit(solution)/shard_map/while/body/eval_jaxpr/ppermute | solution.py:12
  229.6 12.6 %collective-permute-start = (bf16[1024,256]{1,0:T(8,128)(2,1)S(1)}, bf16[1024,256]{1,0:T(8,128)(2,1)S(1)}, u32[]{:S(2)}, u32[]{:S(2)}) collective-permute-start(bf16[1024,256]{1,0:T(8,128)(2,1)S(1)} %get-tuple-element.308), channel_id=1, source_target_pairs={{8,0},{16,8},{24,16},{32,24},{40,32},{48,40},{56,48},{64,56},{72,6... | collective-permute-start | bytes 1572872 | tf_op jit(solution)/shard_map/while/body/eval_jaxpr/ppermute | solution.py:12
  245.0 101.9 %copy-start.2 = (bf16[128,256]{1,0:T(8,128)(2,1)S(1)}, bf16[128,256]{1,0:T(8,128)(2,1)}, u32[]{:S(2)}) copy-start(bf16[128,256]{1,0:T(8,128)(2,1)} %param.11) | copy-start | bytes 196612
  245.1 566.9 %all-reduce.5.cloned.1.call-start = ((), (), s32[]{:S(2)}) async-start(), calls=%async_computation.1 | async-start | bytes 524288 | tf_op jit(solution)/shard_map/psum | solution.py:76
Sparse Core Ops, SparseCore 0:
  245.2 101.6 all-reduce.2
  352.9 459.0 all-reduce.4
where the time goes:
time: 822 us; the launch traced here: 821 us
  waiting for transfers between devices  658 us (80%)
  starting transfers between devices  104 us (13%)
  local copies, waits for them, and re-layouts  24.9 us (3%)
  between operations  14.2 us (2%)
  matrix products  9.98 us (1%)
  other arithmetic  8.83 us (1%)
    psum x1, waiting for transfers between devices, per_device(): lax.psum(weight_term, ('blk', 'rep')) * (1.0 / math.sqrt(node_total))  461 us
    ppermute x10, starting transfers between devices, from_behind(): return lax.ppermute(block, axis, route)  104 us
    psum x1, waiting for transfers between devices, per_device(): whole_sums = lax.psum(partial_sums, 'rep')  102 us
    ppermute x10, waiting for transfers between devices, from_behind(): return lax.ppermute(block, axis, route)  95.1 us
  transfers between devices with their start and end apart: 12, of which 6 were waited for; matrix products, arithmetic and copies ran while one was open for 3% of the time, Pallas kernels for 0%

commit v1 on v0

--- a/solution.py
+++ b/solution.py
@@ -10,6 +10,23 @@
     devices = range(lax.axis_size(axis))
     route = [((i - distance) % len(devices), i) for i in devices]
     return lax.ppermute(block, axis, route)
+
+
+def scatter_sum(flat, axis):
+    size = lax.axis_size(axis)
+    pieces = lax.all_to_all(flat.reshape(size, -1), axis, 0, 0, tiled=False)
+    return pieces.sum(0)
+
+
+def gather_all(piece, axis):
+    size = lax.axis_size(axis)
+    copies = jnp.broadcast_to(piece[None], (size,) + piece.shape)
+    return lax.all_to_all(copies, axis, 0, 0, tiled=False).reshape(-1)
+
+
+def all_reduce_by_exchange(term):
+    flat = scatter_sum(scatter_sum(term.reshape(-1), "rep"), "blk")
+    return gather_all(gather_all(flat, "blk"), "rep").reshape(term.shape)
 
 
 def unpack_block(slot_words):
@@ -63,8 +80,10 @@
     partial_sums = accumulated.reshape(slab_rows, width)
     share_rows = slab_rows // group_size
     share_root = lax.dynamic_slice_in_dim(inverse_root, rep_index * share_rows, share_rows, 0)
-    whole_sums = lax.psum(partial_sums, "rep")
-    own_sums = lax.dynamic_slice_in_dim(whole_sums, rep_index * share_rows, share_rows, 0)
+    exchanged = lax.all_to_all(
+        partial_sums.reshape(group_size, share_rows, width), "rep", 0, 0, tiled=False
+    )
+    own_sums = exchanged.sum(0)
     aggregated = (own_sums * share_root[:, None]).astype(jnp.bfloat16)
     input_grad = lax.dot_general(
         aggregated, weight, (((1,), (1,)), ((), ())), preferred_element_type=jnp.float32
@@ -73,7 +92,7 @@
         features, aggregated, (((0,), (0,)), ((), ())), preferred_element_type=jnp.float32
     )
     node_total = slab_rows * lax.axis_size("blk")
-    weight_grad = lax.psum(weight_term, ("blk", "rep")) * (1.0 / math.sqrt(node_total))
+    weight_grad = all_reduce_by_exchange(weight_term) * (1.0 / math.sqrt(node_total))
     return (input_grad, weight_grad)
 
 

time: 822 us -> 327 us (0.40)
  waiting for transfers between devices: 658 us -> 114 us
  blocking collectives: 0 us -> 54.5 us
  between operations: 14.2 us -> 0.82 us
  starting transfers between devices: 104 us -> 114 us
    psum x2 -> x0, waiting for transfers between devices: 563 us -> none  [the longest x1 461 us: per_device(): lax.psum(weight_term, ('blk', 'rep')) * (1.0 / math.sqrt(node_total))]
    all_to_all x0 -> x3, blocking collectives: none -> 54.5 us  [the longest x2 37.4 us: scatter_sum(): pieces = lax.all_to_all(flat.reshape(size, -1), axis, 0, 0, tiled=False)]
    all_to_all x0 -> x2, waiting for transfers between devices: none -> 18.8 us  [the longest x1 11.8 us: per_device(): lax.all_to_all(partial_sums.reshape(group_size, share_rows, width), 'rep'...]
    all_to_all x0 -> x2, starting transfers between devices: none -> 9.77 us  [the longest x1 6.35 us: per_device(): lax.all_to_all(partial_sums.reshape(group_size, share_rows, width), 'rep'...]
  transfers between devices with their start and end apart: 12 -> 12, of which waited for: 6 -> 6; matrix products, arithmetic and copies ran while one was open for 3% -> 7% of each run, Pallas kernels for 0% -> 0%
where the time goes in v1:
time: 327 us; the launch traced here: 326 us
  starting transfers between devices  114 us (35%)
  waiting for transfers between devices  114 us (35%)
  blocking collectives  54.5 us (17%)
  local copies, waits for them, and re-layouts  26 us (8%)
  other arithmetic  8.88 us (3%)
  matrix products  7.45 us (2%)
    ppermute x10, starting transfers between devices, from_behind(): return lax.ppermute(block, axis, route)  104 us
    ppermute x10, waiting for transfers between devices, from_behind(): return lax.ppermute(block, axis, route)  95.1 us
    all_to_all x2, blocking collectives, scatter_sum(): pieces = lax.all_to_all(flat.reshape(size, -1), axis, 0, 0, tiled=False)  37.4 us
    all_to_all x1, blocking collectives, gather_all(): return lax.all_to_all(copies, axis, 0, 0, tiled=False).reshape(-1)  17.2 us
    all_to_all x1, waiting for transfers between devices, per_device(): lax.all_to_all(partial_sums.reshape(group_size, share_rows, width), 'rep'...  11.8 us
    shift_right_arithmetic x24, local copies, waits for them, and re-layouts, unpack_block(): jnp.right_shift(slot_words[:, :, None, :], shifts[None, None, :, None])  7.51 us
    all_to_all x1, waiting for transfers between devices, gather_all(): return lax.all_to_all(copies, axis, 0, 0, tiled=False).reshape(-1)  7.03 us
  transfers between devices with their start and end apart: 12, of which 6 were waited for; matrix products, arithmetic and copies ran while one was open for 7% of the time, Pallas kernels for 0%

profile of v1, /device:TPU:1, one launch (start us, length us, event | category | flops | bytes accessed | tf_op | source)
XLA Modules:
  0.0 325.8 jit_solution(9909862133719982775)
XLA Ops:
  0.6 0.7 convert_rsqrt_fusion
  1.4 1.3 multiply_convert_fusion
  2.7 12.4 %collective-permute-start.1 = (bf16[1024,256]{1,0:T(8,128)(2,1)S(1)}, bf16[1024,256]{1,0:T(8,128)(2,1)S(1)}, u32[]{:S(2)}, u32[]{:S(2)}) collective-permute-start(bf16[1024,256]{1,0:T(8,128)(2,1)S(1)} %multiply_convert_fusion), channel_id=1, source_target_pairs={{64,0},{72,8},{80,16},{88,24},{96,32},{104,40},{112,48},{120,56},{... | collective-permute-start | bytes 1572872 | tf_op jit(solution)/shard_map/ppermute | solution.py:12
  15.1 21.9 %collective-permute-done.1 = bf16[1024,256]{1,0:T(8,128)(2,1)S(1)} collective-permute-done((bf16[1024,256]{1,0:T(8,128)(2,1)S(1)}, bf16[1024,256]{1,0:T(8,128)(2,1)S(1)}, u32[]{:S(2)}, u32[]{:S(2)}) %collective-permute-start.1) | collective-permute-done | bytes 524320 | tf_op jit(solution)/shard_map/ppermute | solution.py:12
  37.3 6.5 %collective-permute-start.2 = (bf16[1024,256]{1,0:T(8,128)(2,1)S(1)}, bf16[1024,256]{1,0:T(8,128)(2,1)S(1)}, u32[]{:S(2)}, u32[]{:S(2)}) collective-permute-start(bf16[1024,256]{1,0:T(8,128)(2,1)S(1)} %broadcast_select_fusion), channel_id=1, source_target_pairs={{128,0},{136,8},{144,16},{152,24},{160,32},{168,40},{176,48},{184,... | collective-permute-start | bytes 1572872 | tf_op jit(solution)/shard_map/ppermute | solution.py:12
  43.9 0.7 compare_and_fusion.1
  44.6 40.6 %collective-permute-done.2 = bf16[1024,256]{1,0:T(8,128)(2,1)S(1)} collective-permute-done((bf16[1024,256]{1,0:T(8,128)(2,1)S(1)}, bf16[1024,256]{1,0:T(8,128)(2,1)S(1)}, u32[]{:S(2)}, u32[]{:S(2)}) %collective-permute-start.2) | collective-permute-done | bytes 524320 | tf_op jit(solution)/shard_map/ppermute | solution.py:12
  85.3 4.8 %collective-permute-start.3 = (bf16[1024,256]{1,0:T(8,128)(2,1)S(1)}, bf16[1024,256]{1,0:T(8,128)(2,1)S(1)}, u32[]{:S(2)}, u32[]{:S(2)}) collective-permute-start(bf16[1024,256]{1,0:T(8,128)(2,1)S(1)} %broadcast_select_fusion.1), channel_id=1, source_target_pairs={{256,0},{264,8},{272,16},{280,24},{288,32},{296,40},{304,48},{312,... | collective-permute-start | bytes 1572872 | tf_op jit(solution)/shard_map/ppermute | solution.py:12
  90.8 0.7 slice_bitcast_fusion.2
  91.4 0.8 slice_bitcast_fusion.1
  92.3 27.5 %collective-permute-done.3 = bf16[1024,256]{1,0:T(8,128)(2,1)S(1)} collective-permute-done((bf16[1024,256]{1,0:T(8,128)(2,1)S(1)}, bf16[1024,256]{1,0:T(8,128)(2,1)S(1)}, u32[]{:S(2)}, u32[]{:S(2)}) %collective-permute-start.3) | collective-permute-done | bytes 524320 | tf_op jit(solution)/shard_map/ppermute | solution.py:12
  121.2 115.9 %while.20 = (s32[]{:T(128)}, bf16[1024,256]{1,0:T(8,128)(2,1)S(1)}, f32[8,128,256]{2,0,1:T(8,128)S(1)}, s32[1,8,2,8]{3,2,1,0:T(2,128)}, s32[1,8]{1,0:T(1,128)S(1...) while((s32[]{:T(128)}, bf16[1024,256]{1,0:T(8,128)(2,1)S(1)}, ...), condition=%wide.region_1.3_spmd.clone.clone, body=%wide.region_0.2_spmd.clone.clone.sunk | while | flops 72221880 | bytes 8067647 | solution.py:79
  121.2 3.7 %collective-permute-start = (bf16[1024,256]{1,0:T(8,128)(2,1)S(1)}, bf16[1024,256]{1,0:T(8,128)(2,1)S(1)}, u32[]{:S(2)}, u32[]{:S(2)}) collective-permute-start(bf16[1024,256]{1,0:T(8,128)(2,1)S(1)} %get-tuple-element.304), channel_id=1, source_target_pairs={{8,0},{16,8},{24,16},{32,24},{40,32},{48,40},{56,48},{64,56},{72,6... | collective-permute-start | bytes 1572872 | tf_op jit(solution)/shard_map/while/body/eval_jaxpr/ppermute | solution.py:12
  125.6 0.7 constant_dynamic-slice_fusion.4
  126.4 0.7 iota_compare_fusion.5
  127.0 0.9 dynamic-slice_bitcast_fusion.2
  127.9 5.0 %collective-permute-done = bf16[1024,256]{1,0:T(8,128)(2,1)S(1)} collective-permute-done((bf16[1024,256]{1,0:T(8,128)(2,1)S(1)}, bf16[1024,256]{1,0:T(8,128)(2,1)S(1)}, u32[]{:S(2)}, u32[]{:S(2)}) %collective-permute-start) | collective-permute-done | bytes 524320 | tf_op jit(solution)/shard_map/while/body/eval_jaxpr/ppermute | solution.py:12
  134.4 28.1 %collective-permute-start = (bf16[1024,256]{1,0:T(8,128)(2,1)S(1)}, bf16[1024,256]{1,0:T(8,128)(2,1)S(1)}, u32[]{:S(2)}, u32[]{:S(2)}) collective-permute-start(bf16[1024,256]{1,0:T(8,128)(2,1)S(1)} %get-tuple-element.304), channel_id=1, source_target_pairs={{8,0},{16,8},{24,16},{32,24},{40,32},{48,40},{56,48},{64,56},{72,6... | collective-permute-start | bytes 1572872 | tf_op jit(solution)/shard_map/while/body/eval_jaxpr/ppermute | solution.py:12
  163.1 0.7 constant_dynamic-slice_fusion.4
  164.5 0.9 dynamic-slice_bitcast_fusion.2
  166.8 9.7 %collective-permute-start = (bf16[1024,256]{1,0:T(8,128)(2,1)S(1)}, bf16[1024,256]{1,0:T(8,128)(2,1)S(1)}, u32[]{:S(2)}, u32[]{:S(2)}) collective-permute-start(bf16[1024,256]{1,0:T(8,128)(2,1)S(1)} %get-tuple-element.304), channel_id=1, source_target_pairs={{8,0},{16,8},{24,16},{32,24},{40,32},{48,40},{56,48},{64,56},{72,6... | collective-permute-start | bytes 1572872 | tf_op jit(solution)/shard_map/while/body/eval_jaxpr/ppermute | solution.py:12
  177.1 0.7 constant_dynamic-slice_fusion.4
  178.6 0.9 dynamic-slice_bitcast_fusion.2
  180.9 9.7 %collective-permute-start = (bf16[1024,256]{1,0:T(8,128)(2,1)S(1)}, bf16[1024,256]{1,0:T(8,128)(2,1)S(1)}, u32[]{:S(2)}, u32[]{:S(2)}) collective-permute-start(bf16[1024,256]{1,0:T(8,128)(2,1)S(1)} %get-tuple-element.304), channel_id=1, source_target_pairs={{8,0},{16,8},{24,16},{32,24},{40,32},{48,40},{56,48},{64,56},{72,6... | collective-permute-start | bytes 1572872 | tf_op jit(solution)/shard_map/while/body/eval_jaxpr/ppermute | solution.py:12
  191.2 0.7 constant_dynamic-slice_fusion.4
  192.0 0.7 iota_compare_fusion.5
  192.6 0.9 dynamic-slice_bitcast_fusion.2
  194.9 9.7 %collective-permute-start = (bf16[1024,256]{1,0:T(8,128)(2,1)S(1)}, bf16[1024,256]{1,0:T(8,128)(2,1)S(1)}, u32[]{:S(2)}, u32[]{:S(2)}) collective-permute-start(bf16[1024,256]{1,0:T(8,128)(2,1)S(1)} %get-tuple-element.304), channel_id=1, source_target_pairs={{8,0},{16,8},{24,16},{32,24},{40,32},{48,40},{56,48},{64,56},{72,6... | collective-permute-start | bytes 1572872 | tf_op jit(solution)/shard_map/while/body/eval_jaxpr/ppermute | solution.py:12
  205.2 0.7 constant_dynamic-slice_fusion.4
  206.7 0.9 dynamic-slice_bitcast_fusion.2
  209.0 9.7 %collective-permute-start = (bf16[1024,256]{1,0:T(8,128)(2,1)S(1)}, bf16[1024,256]{1,0:T(8,128)(2,1)S(1)}, u32[]{:S(2)}, u32[]{:S(2)}) collective-permute-start(bf16[1024,256]{1,0:T(8,128)(2,1)S(1)} %get-tuple-element.304), channel_id=1, source_target_pairs={{8,0},{16,8},{24,16},{32,24},{40,32},{48,40},{56,48},{64,56},{72,6... | collective-permute-start | bytes 1572872 | tf_op jit(solution)/shard_map/while/body/eval_jaxpr/ppermute | solution.py:12
  219.3 0.7 constant_dynamic-slice_fusion.4
  220.8 0.9 dynamic-slice_bitcast_fusion.2
  223.1 9.7 %collective-permute-start = (bf16[1024,256]{1,0:T(8,128)(2,1)S(1)}, bf16[1024,256]{1,0:T(8,128)(2,1)S(1)}, u32[]{:S(2)}, u32[]{:S(2)}) collective-permute-start(bf16[1024,256]{1,0:T(8,128)(2,1)S(1)} %get-tuple-element.304), channel_id=1, source_target_pairs={{8,0},{16,8},{24,16},{32,24},{40,32},{48,40},{56,48},{64,56},{72,6... | collective-permute-start | bytes 1572872 | tf_op jit(solution)/shard_map/while/body/eval_jaxpr/ppermute | solution.py:12
  233.4 0.7 constant_dynamic-slice_fusion.4
  234.8 0.9 dynamic-slice_bitcast_fusion.2
  237.1 1.3 copy.22
  238.4 6.4 %all-to-all-start = ((f32[8,128,256]{2,1,0:T(8,128)}), f32[8,128,256]{2,1,0:T(8,128)S(1)}, u32[]{:S(2)}, u32[]{:S(2)}) async-start(f32[8,128,256]{2,1,0:T(8,128)} %copy.22), calls=%async_computation | async-start | bytes 2097152 | tf_op jit(solution)/shard_map/all_to_all | solution.py:83
  244.9 11.8 %all-to-all-done = f32[8,128,256]{2,1,0:T(8,128)S(1)} async-done(((f32[8,128,256]{2,1,0:T(8,128)}), f32[8,128,256]{2,1,0:T(8,128)S(1)}, u32[]{:S(2)}, u32[]{:S(2)}) %all-to-all-start) | async-done | bytes 1048608 | tf_op jit(solution)/shard_map/all_to_all | solution.py:83
  257.4 10.1 %all_to_all.36 = f32[8,1,8192]{2,1,0:T(1,128)S(1)} all-to-all(f32[8,1,8192]{2,1,0:T(1,128)S(1)} %all_to_all.30), channel_id=1, replica_groups=mesh['blk'=64,'rep'=8] {'rep'}, dimensions={0} | all-to-all | bytes 524288 | tf_op jit(solution)/shard_map/all_to_all | solution.py:17
  267.7 27.3 %all_to_all.37 = f32[64,1,128]{2,1,0:T(1,128)S(1)} all-to-all(f32[64,1,128]{2,1,0:T(1,128)S(1)} %bitcast.60), channel_id=1, replica_groups=mesh['blk'=64,'rep'=8] {'blk'}, dimensions={0} | all-to-all | bytes 65536 | tf_op jit(solution)/shard_map/all_to_all | solution.py:17
  295.0 17.2 %all_to_all.38 = f32[64,1,128]{2,1,0:T(1,128)S(1)} all-to-all(f32[64,1,128]{2,1,0:T(1,128)S(1)} %broadcast_in_dim.23), channel_id=1, replica_groups=mesh['blk'=64,'rep'=8] {'blk'}, dimensions={0} | all-to-all | bytes 65536 | tf_op jit(solution)/shard_map/all_to_all | solution.py:24
  312.2 0.8 broadcast_in_dim.25
  313.0 3.4 %all-to-all-start.4 = ((f32[8,1,8192]{2,1,0:T(1,128)}), f32[8,1,8192]{2,1,0:T(1,128)S(1)}, u32[]{:S(2)}, u32[]{:S(2)}) async-start(f32[8,1,8192]{2,1,0:T(1,128)} %broadcast_in_dim.25), calls=%async_computation.4 | async-start | bytes 524288 | tf_op jit(solution)/shard_map/all_to_all | solution.py:24
  316.4 0.8 convolution_convert_fusion
  317.3 7.0 %all-to-all-done.4 = f32[8,1,8192]{2,1,0:T(1,128)S(1)} async-done(((f32[8,1,8192]{2,1,0:T(1,128)}), f32[8,1,8192]{2,1,0:T(1,128)S(1)}, u32[]{:S(2)}, u32[]{:S(2)}) %all-to-all-start.4) | async-done | bytes 262176 | tf_op jit(solution)/shard_map/all_to_all | solution.py:24
  324.3 0.7 multiply_reduce_fusion
  325.0 0.7 mul.35
  (107 shorter events, 21.6 us)
Async XLA Ops:
  0.6 315.8 %copy-start = (bf16[256,256]{1,0:T(8,128)(2,1)S(1)}, bf16[256,256]{1,0:T(8,128)(2,1)}, u32[]{:S(2)}) copy-start(bf16[256,256]{1,0:T(8,128)(2,1)} %param.13) | copy-start | bytes 393220
  1.4 35.6 %copy-start.1 = (bf16[1024,256]{1,0:T(8,128)(2,1)S(1)}, bf16[1024,256]{1,0:T(8,128)(2,1)}, u32[]{:S(2)}) copy-start(bf16[1024,256]{1,0:T(8,128)(2,1)} %param.12) | copy-start | bytes 1572868
  2.7 34.3 %collective-permute-start.1 = (bf16[1024,256]{1,0:T(8,128)(2,1)S(1)}, bf16[1024,256]{1,0:T(8,128)(2,1)S(1)}, u32[]{:S(2)}, u32[]{:S(2)}) collective-permute-start(bf16[1024,256]{1,0:T(8,128)(2,1)S(1)} %multiply_convert_fusion), channel_id=1, source_target_pairs={{64,0},{72,8},{80,16},{88,24},{96,32},{104,40},{112,48},{120,56},{... | collective-permute-start | bytes 1572872 | tf_op jit(solution)/shard_map/ppermute | solution.py:12
  37.3 48.0 %collective-permute-start.2 = (bf16[1024,256]{1,0:T(8,128)(2,1)S(1)}, bf16[1024,256]{1,0:T(8,128)(2,1)S(1)}, u32[]{:S(2)}, u32[]{:S(2)}) collective-permute-start(bf16[1024,256]{1,0:T(8,128)(2,1)S(1)} %broadcast_select_fusion), channel_id=1, source_target_pairs={{128,0},{136,8},{144,16},{152,24},{160,32},{168,40},{176,48},{184,... | collective-permute-start | bytes 1572872 | tf_op jit(solution)/shard_map/ppermute | solution.py:12
  85.3 34.5 %collective-permute-start.3 = (bf16[1024,256]{1,0:T(8,128)(2,1)S(1)}, bf16[1024,256]{1,0:T(8,128)(2,1)S(1)}, u32[]{:S(2)}, u32[]{:S(2)}) collective-permute-start(bf16[1024,256]{1,0:T(8,128)(2,1)S(1)} %broadcast_select_fusion.1), channel_id=1, source_target_pairs={{256,0},{264,8},{272,16},{280,24},{288,32},{296,40},{304,48},{312,... | collective-permute-start | bytes 1572872 | tf_op jit(solution)/shard_map/ppermute | solution.py:12
  90.1 0.7 copy-start.3
  121.2 11.7 %collective-permute-start = (bf16[1024,256]{1,0:T(8,128)(2,1)S(1)}, bf16[1024,256]{1,0:T(8,128)(2,1)S(1)}, u32[]{:S(2)}, u32[]{:S(2)}) collective-permute-start(bf16[1024,256]{1,0:T(8,128)(2,1)S(1)} %get-tuple-element.304), channel_id=1, source_target_pairs={{8,0},{16,8},{24,16},{32,24},{40,32},{48,40},{56,48},{64,56},{72,6... | collective-permute-start | bytes 1572872 | tf_op jit(solution)/shard_map/while/body/eval_jaxpr/ppermute | solution.py:12
  134.4 31.0 %collective-permute-start = (bf16[1024,256]{1,0:T(8,128)(2,1)S(1)}, bf16[1024,256]{1,0:T(8,128)(2,1)S(1)}, u32[]{:S(2)}, u32[]{:S(2)}) collective-permute-start(bf16[1024,256]{1,0:T(8,128)(2,1)S(1)} %get-tuple-element.304), channel_id=1, source_target_pairs={{8,0},{16,8},{24,16},{32,24},{40,32},{48,40},{56,48},{64,56},{72,6... | collective-permute-start | bytes 1572872 | tf_op jit(solution)/shard_map/while/body/eval_jaxpr/ppermute | solution.py:12
  166.8 12.6 %collective-permute-start = (bf16[1024,256]{1,0:T(8,128)(2,1)S(1)}, bf16[1024,256]{1,0:T(8,128)(2,1)S(1)}, u32[]{:S(2)}, u32[]{:S(2)}) collective-permute-start(bf16[1024,256]{1,0:T(8,128)(2,1)S(1)} %get-tuple-element.304), channel_id=1, source_target_pairs={{8,0},{16,8},{24,16},{32,24},{40,32},{48,40},{56,48},{64,56},{72,6... | collective-permute-start | bytes 1572872 | tf_op jit(solution)/shard_map/while/body/eval_jaxpr/ppermute | solution.py:12
  180.9 12.6 %collective-permute-start = (bf16[1024,256]{1,0:T(8,128)(2,1)S(1)}, bf16[1024,256]{1,0:T(8,128)(2,1)S(1)}, u32[]{:S(2)}, u32[]{:S(2)}) collective-permute-start(bf16[1024,256]{1,0:T(8,128)(2,1)S(1)} %get-tuple-element.304), channel_id=1, source_target_pairs={{8,0},{16,8},{24,16},{32,24},{40,32},{48,40},{56,48},{64,56},{72,6... | collective-permute-start | bytes 1572872 | tf_op jit(solution)/shard_map/while/body/eval_jaxpr/ppermute | solution.py:12
  194.9 12.6 %collective-permute-start = (bf16[1024,256]{1,0:T(8,128)(2,1)S(1)}, bf16[1024,256]{1,0:T(8,128)(2,1)S(1)}, u32[]{:S(2)}, u32[]{:S(2)}) collective-permute-start(bf16[1024,256]{1,0:T(8,128)(2,1)S(1)} %get-tuple-element.304), channel_id=1, source_target_pairs={{8,0},{16,8},{24,16},{32,24},{40,32},{48,40},{56,48},{64,56},{72,6... | collective-permute-start | bytes 1572872 | tf_op jit(solution)/shard_map/while/body/eval_jaxpr/ppermute | solution.py:12
  209.0 12.6 %collective-permute-start = (bf16[1024,256]{1,0:T(8,128)(2,1)S(1)}, bf16[1024,256]{1,0:T(8,128)(2,1)S(1)}, u32[]{:S(2)}, u32[]{:S(2)}) collective-permute-start(bf16[1024,256]{1,0:T(8,128)(2,1)S(1)} %get-tuple-element.304), channel_id=1, source_target_pairs={{8,0},{16,8},{24,16},{32,24},{40,32},{48,40},{56,48},{64,56},{72,6... | collective-permute-start | bytes 1572872 | tf_op jit(solution)/shard_map/while/body/eval_jaxpr/ppermute | solution.py:12
  223.1 12.6 %collective-permute-start = (bf16[1024,256]{1,0:T(8,128)(2,1)S(1)}, bf16[1024,256]{1,0:T(8,128)(2,1)S(1)}, u32[]{:S(2)}, u32[]{:S(2)}) collective-permute-start(bf16[1024,256]{1,0:T(8,128)(2,1)S(1)} %get-tuple-element.304), channel_id=1, source_target_pairs={{8,0},{16,8},{24,16},{32,24},{40,32},{48,40},{56,48},{64,56},{72,6... | collective-permute-start | bytes 1572872 | tf_op jit(solution)/shard_map/while/body/eval_jaxpr/ppermute | solution.py:12
  238.4 18.2 %all-to-all-start = ((f32[8,128,256]{2,1,0:T(8,128)}), f32[8,128,256]{2,1,0:T(8,128)S(1)}, u32[]{:S(2)}, u32[]{:S(2)}) async-start(f32[8,128,256]{2,1,0:T(8,128)} %copy.22), calls=%async_computation | async-start | bytes 2097152 | tf_op jit(solution)/shard_map/all_to_all | solution.py:83
  244.9 11.8 %copy-start.2 = (bf16[128,256]{1,0:T(8,128)(2,1)S(1)}, bf16[128,256]{1,0:T(8,128)(2,1)}, u32[]{:S(2)}) copy-start(bf16[128,256]{1,0:T(8,128)(2,1)} %param.11) | copy-start | bytes 196612
  313.0 11.3 %all-to-all-start.4 = ((f32[8,1,8192]{2,1,0:T(1,128)}), f32[8,1,8192]{2,1,0:T(1,128)S(1)}, u32[]{:S(2)}, u32[]{:S(2)}) async-start(f32[8,1,8192]{2,1,0:T(1,128)} %broadcast_in_dim.25), calls=%async_computation.4 | async-start | bytes 524288 | tf_op jit(solution)/shard_map/all_to_all | solution.py:24

commit v2 on v1

v2 whole, which is shorter than its diff:
```python
import functools
import math

import jax
import jax.numpy as jnp
from jax import lax
from jax.experimental import pallas as pl
from jax.experimental.pallas import tpu as pltpu
from jax.sharding import PartitionSpec as P

CHUNKS = 4
MESH_ID = pl.DeviceIdType.MESH


def gather_kernel(steps, blocks, slab_ref, out_ref, send_sem, recv_sem, local_sem):
    me = lax.axis_index("blk")
    rep = lax.axis_index("rep")
    rows = slab_ref.shape[0] // CHUNKS
    far_to = lax.rem(me - steps * rep + blocks * steps, blocks)
    far_from = lax.rem(me + steps * rep, blocks)
    left = lax.rem(me + blocks - 1, blocks)
    right = lax.rem(me + 1, blocks)
    remote_first = rep != 0

    barrier = pltpu.get_barrier_semaphore()
    for partner in (left, right):
        pl.semaphore_signal(barrier, inc=1, device_id=(partner, rep), device_id_type=MESH_ID)

    @pl.when(remote_first)
    def _():
        for partner in (far_to, far_from):
            pl.semaphore_signal(barrier, inc=1, device_id=(partner, rep), device_id_type=MESH_ID)
        pl.semaphore_wait(barrier, 4)

    @pl.when(jnp.logical_not(remote_first))
    def _():
        pl.semaphore_wait(barrier, 2)

    def part(c):
        return pl.ds(c * rows, rows)

    def forward(s, c, target):
        src = slab_ref.at[part(c)] if s == 0 else out_ref.at[s - 1, part(c)]
        return pltpu.make_async_remote_copy(
            src_ref=src,
            dst_ref=out_ref.at[s, part(c)],
            send_sem=send_sem.at[s, c],
            recv_sem=recv_sem.at[s, c],
            device_id=(target, rep),
            device_id_type=MESH_ID,
        )

    @pl.when(remote_first)
    def _():
        for c in range(CHUNKS):
            forward(0, c, far_to).start()

    @pl.when(jnp.logical_not(remote_first))
    def _():
        for c in range(CHUNKS):
            local = pltpu.make_async_copy(slab_ref.at[part(c)], out_ref.at[0, part(c)], local_sem.at[c])
            local.start()
        for c in range(CHUNKS):
            pltpu.make_async_copy(slab_ref.at[part(c)], out_ref.at[0, part(c)], local_sem.at[c]).wait()

    for s in range(1, steps):
        for c in range(CHUNKS):
            if s == 1:
                @pl.when(remote_first)
                def _():
                    forward(0, c, far_to).wait_recv()
            else:
                forward(s - 1, c, left).wait_recv()
            forward(s, c, left).start()

    for c in range(CHUNKS):
        forward(steps - 1, c, left).wait_recv()

    @pl.when(remote_first)
    def _():
        for c in range(CHUNKS):
            forward(0, c, far_to).wait_send()

    for s in range(1, steps):
        for c in range(CHUNKS):
            forward(s, c, left).wait_send()


def gather_sources(scaled, steps, blocks):
    slab_rows, width = scaled.shape
    return pl.pallas_call(
        functools.partial(gather_kernel, steps, blocks),
        out_shape=jax.ShapeDtypeStruct((steps, slab_rows, width), scaled.dtype),
        in_specs=[pl.BlockSpec(memory_space=pl.ANY)],
        out_specs=pl.BlockSpec(memory_space=pl.ANY),
        scratch_shapes=[
            pltpu.SemaphoreType.DMA((steps, CHUNKS)),
            pltpu.SemaphoreType.DMA((steps, CHUNKS)),
            pltpu.SemaphoreType.DMA((CHUNKS,)),
        ],
        compiler_params=pltpu.CompilerParams(collective_id=0, has_side_effects=True),
    )(scaled)


def scatter_sum(flat, axis):
    size = lax.axis_size(axis)
    pieces = lax.all_to_all(flat.reshape(size, -1), axis, 0, 0, tiled=False)
    return pieces.sum(0)


def gather_all(piece, axis):
    size = lax.axis_size(axis)
    copies = jnp.broadcast_to(piece[None], (size,) + piece.shape)
    return lax.all_to_all(copies, axis, 0, 0, tiled=False).reshape(-1)


def all_reduce_by_exchange(term):
    flat = scatter_sum(scatter_sum(term.reshape(-1), "rep"), "blk")
    return gather_all(gather_all(flat, "blk"), "rep").reshape(term.shape)


def unpack_blocks(words):
    shifts = jnp.arange(8, dtype=jnp.int32)
    bit_values = jnp.bitwise_and(
        jnp.right_shift(words[..., :, None, :], shifts[:, None]), 1
    )
    return bit_values.reshape(words.shape[:-2] + (128, 128)).astype(jnp.bfloat16)


def per_device(features, out_grad, weight, block_words, block_coords, block_counts, degrees):
    slab_rows, width = out_grad.shape
    row_blocks = slab_rows // 128
    group_size = lax.axis_size("rep")
    blocks = lax.axis_size("blk")
    step_count = blocks // group_size
    rep_index = lax.axis_index("rep")
    inverse_root = lax.rsqrt(degrees.astype(jnp.float32))
    scaled = (out_grad.astype(jnp.float32) * inverse_root[:, None]).astype(jnp.bfloat16)

    sources = gather_sources(scaled, step_count, blocks).reshape(
        step_count, row_blocks, 128, width
    )
    coords = block_coords[0]
    slot_total = coords.shape[-1]
    picked = jnp.take_along_axis(sources, coords[:, 0, :, None, None], axis=1)
    transposed = unpack_blocks(block_words[0])
    contrib = jnp.einsum(
        "skvu,skuf->skvf", transposed, picked, preferred_element_type=jnp.float32
    )
    live = jnp.arange(slot_total, dtype=jnp.int32)[None, :] < block_counts[0][:, None]
    column_ids = jnp.arange(row_blocks, dtype=jnp.int32)
    placement = (
        (coords[:, 1, :, None] == column_ids[None, None, :]) & live[:, :, None]
    ).astype(jnp.float32)
    accumulated = jnp.einsum("skc,skvf->cvf", placement, contrib)

    partial_sums = accumulated.reshape(slab_rows, width)
    share_rows = slab_rows // group_size
    share_root = lax.dynamic_slice_in_dim(inverse_root, rep_index * share_rows, share_rows, 0)
    exchanged = lax.all_to_all(
        partial_sums.reshape(group_size, share_rows, width), "rep", 0, 0, tiled=False
    )
    own_sums = exchanged.sum(0)
    aggregated = (own_sums * share_root[:, None]).astype(jnp.bfloat16)
    input_grad = lax.dot_general(
        aggregated, weight, (((1,), (1,)), ((), ())), preferred_element_type=jnp.float32
    ).astype(jnp.bfloat16)
    weight_term = lax.dot_general(
        features, aggregated, (((0,), (0,)), ((), ())), preferred_element_type=jnp.float32
    )
    node_total = slab_rows * blocks
    weight_grad = all_reduce_by_exchange(weight_term) * (1.0 / math.sqrt(node_total))
    return (input_grad, weight_grad)


def solution(mesh):
    return jax.shard_map(
        per_device,
        mesh=mesh,
        in_specs=(
            P(("blk", "rep"), None),
            P("blk", None),
            P(),
            P("blk", "rep", None, None, None),
            P("blk", "rep", None, None),
            P("blk", "rep"),
            P("blk"),
        ),
        out_specs=(P(("blk", "rep"), None), P()),
        check_vma=False,
    )
```

time: 327 us -> 231 us (0.71)
  waiting for transfers between devices: 114 us -> 23.8 us
  Pallas kernels: 0 us -> 61.9 us
  starting transfers between devices: 114 us -> 69.4 us
  local copies, waits for them, and re-layouts: 26 us -> 9.43 us
  other arithmetic: 8.88 us -> 4.42 us
    ppermute x10 -> x0, starting transfers between devices: 104 us -> none  [from_behind(): return lax.ppermute(block, axis, route)]
    ppermute x10 -> x0, waiting for transfers between devices: 95.1 us -> none  [from_behind(): return lax.ppermute(block, axis, route)]
    pallas_call x0 -> x1, Pallas kernels: none -> 61.9 us  [gather_sources(): pl.pallas_call(functools.partial(gather_kernel, steps, blocks), out_shape...]
    all_to_all x1, starting transfers between devices: 6.35 us -> 66 us  [per_device(): lax.all_to_all(partial_sums.reshape(group_size, share_rows, width), 'rep'...]
    dynamic_slice x14 -> x0, local copies, waits for them, and re-layouts: 8.85 us -> none  [the longest x7 4.76 us: add_slot(): lax.dynamic_index_in_dim(block_coords[0], slot_index, 0, keepdims=False)]
    shift_right_arithmetic x24 -> x2, local copies, waits for them, and re-layouts: 7.51 us -> 0.1 us  [unpack_blocks(): jnp.right_shift(words[..., :, None, :], shifts[:, None])]
    all_to_all x1, waiting for transfers between devices: 11.8 us -> 16.8 us  [per_device(): lax.all_to_all(partial_sums.reshape(group_size, share_rows, width), 'rep'...]
    lt x8 -> x1, other arithmetic: 4.61 us -> 0.66 us  [per_device(): jnp.arange(slot_total, dtype=jnp.int32)[None, :] < block_counts[0][:, None]]
  transfers between devices with their start and end apart: 12 -> 2, of which waited for: 6 -> 2; matrix products, arithmetic and copies ran while one was open for 7% -> 0% of each run, Pallas kernels for 0% -> 0%
where the time goes in v2:
time: 231 us
  starting transfers between devices  69.4 us (30%)
  Pallas kernels  61.9 us (27%)
  blocking collectives  53.9 us (23%)
  waiting for transfers between devices  23.8 us (10%)
  local copies, waits for them, and re-layouts  9.43 us (4%)
  matrix products  7.14 us (3%)
  other arithmetic  4.42 us (2%)
    all_to_all x1, starting transfers between devices, per_device(): lax.all_to_all(partial_sums.reshape(group_size, share_rows, width), 'rep'...  66 us
    pallas_call x1, Pallas kernels, gather_sources(): pl.pallas_call(functools.partial(gather_kernel, steps, blocks), out_shape...  61.9 us
    all_to_all x2, blocking collectives, scatter_sum(): pieces = lax.all_to_all(flat.reshape(size, -1), axis, 0, 0, tiled=False)  36.8 us
    all_to_all x1, blocking collectives, gather_all(): return lax.all_to_all(copies, axis, 0, 0, tiled=False).reshape(-1)  17.2 us
    all_to_all x1, waiting for transfers between devices, per_device(): lax.all_to_all(partial_sums.reshape(group_size, share_rows, width), 'rep'...  16.8 us
    all_to_all x1, waiting for transfers between devices, gather_all(): return lax.all_to_all(copies, axis, 0, 0, tiled=False).reshape(-1)  7.03 us
    gather x2, local copies, waits for them, and re-layouts, per_device(): picked = jnp.take_along_axis(sources, coords[:, 0, :, None, None], axis=1)  5.11 us
  transfers between devices with their start and end apart: 2, of which 2 were waited for; matrix products, arithmetic and copies ran while one was open for 0% of the time, Pallas kernels for 0%

profile of v2, /device:TPU:1, one launch (start us, length us, event | category | flops | bytes accessed | tf_op | source)
XLA Modules:
  0.0 230.8 jit_solution(14104972537241477072)
XLA Ops:
  0.6 0.0 copy-start
  0.6 0.7 copy.39
  1.4 0.7 iota_compare_fusion.1
  2.1 0.7 convert_rsqrt_fusion
  2.8 0.1 reshape.129
  2.8 0.1 copy.27
  2.9 0.1 shift_right_arithmetic.26
  3.0 2.0 multiply_convert_fusion.slab_ref
  5.1 61.9 %shard_map.86 = bf16[8,1024,256]{2,1,0:T(8,128)(2,1)} custom-call(bf16[1024,256]{1,0:T(8,128)(2,1)} %multiply_convert_fusion.slab_ref), custom_call_target="tpu_custom_call" | custom-call | tf_op jit(solution)/shard_map/pallas_call | solution.py:91
  66.9 0.0 copy-start.2
  67.0 5.0 %gather_fusion = bf16[64,128,256]{2,1,0:T(8,128)(2,1)} fusion(bf16[8,8,128,256]{3,2,1,0:T(8,128)(2,1)} %bitcast.37, s32[64]{0:T(128)S(1)} %reshape.129), kind=kCustom, calls=%fused_computation | custom fusion | bytes 8389120 | tf_op jit(solution)/shard_map/jit(take_along_axis)/gather | solution.py:145
  72.0 0.0 copy-done.2
  72.0 3.5 %fusion.4 = bf16[8,8,128,256]{3,2,1,0:T(8,128)(2,1)S(1)} fusion(bf16[8,8,128,256]{3,2,1,0:T(8,128)(2,1)} %bitcast.38, pred[8,8]{1,0:T(8,128)(4,1)S(1)} %compare_and_fusion, s32[128]{0:T(128)S(1)} %shift_right_arithmetic.26, s32[8,8,16,128]{3,2,1,0:T(8,128)S(1)} %bitcast.45), kind=kOutput, calls=%fused_computation.6 | convolution fusion | flops 542113792 | bytes 8913472 | tf_op jit(solution)/shard_map/skvu,skuf->skvf/dot_general | solution.py:147
  75.5 0.0 copy-start.1
  75.5 2.5 %fusion.12 = f32[8,128,256]{2,0,1:T(8,128)S(1)} fusion(bf16[8,8,128,256]{3,2,1,0:T(8,128)(2,1)S(1)} %fusion.4, s32[8,8]{0,1:T(8,128)S(1)} %copy.27, pred[8,8]{0,1:T(8,128)(4,1)S(1)} %iota_compare_fusion.1), kind=kOutput, calls=%fused_computation.13 | convolution fusion | flops 33555456 | bytes 5243200 | tf_op jit(solution)/shard_map/skc,skvf->cvf/dot_general | solution.py:155
  78.0 1.3 copy.29
  79.3 66.0 %all-to-all-start = ((f32[8,128,256]{2,1,0:T(8,128)}), f32[8,128,256]{2,1,0:T(8,128)S(1)}, u32[]{:S(2)}, u32[]{:S(2)}) async-start(f32[8,128,256]{2,1,0:T(8,128)} %copy.29), calls=%async_computation | async-start | bytes 2097152 | tf_op jit(solution)/shard_map/all_to_all | solution.py:160
  145.3 0.1 dynamic_slice.3
  145.4 16.8 %all-to-all-done = f32[8,128,256]{2,1,0:T(8,128)S(1)} async-done(((f32[8,128,256]{2,1,0:T(8,128)}), f32[8,128,256]{2,1,0:T(8,128)S(1)}, u32[]{:S(2)}, u32[]{:S(2)}) %all-to-all-start) | async-done | bytes 1048608 | tf_op jit(solution)/shard_map/all_to_all | solution.py:160
  162.2 0.1 reduce_sum.27
  162.3 0.0 copy-done.1
  162.3 0.3 convolution_bitcast_fusion
  162.6 0.1 copy.30
  162.7 0.3 all_to_all.30
  163.0 10.8 %all_to_all.36 = f32[8,1,8192]{2,1,0:T(1,128)S(1)} all-to-all(f32[8,1,8192]{2,1,0:T(1,128)S(1)} %all_to_all.30), channel_id=1, replica_groups=mesh['blk'=64,'rep'=8] {'rep'}, dimensions={0} | all-to-all | bytes 524288 | tf_op jit(solution)/shard_map/all_to_all | solution.py:107
  173.8 0.2 reduce_sum.28
  174.0 25.9 %all_to_all.37 = f32[64,1,128]{2,1,0:T(1,128)S(1)} all-to-all(f32[64,1,128]{2,1,0:T(1,128)S(1)} %bitcast.39), channel_id=1, replica_groups=mesh['blk'=64,'rep'=8] {'blk'}, dimensions={0} | all-to-all | bytes 65536 | tf_op jit(solution)/shard_map/all_to_all | solution.py:107
  200.0 17.2 %all_to_all.38 = f32[64,1,128]{2,1,0:T(1,128)S(1)} all-to-all(f32[64,1,128]{2,1,0:T(1,128)S(1)} %broadcast_in_dim.28), channel_id=1, replica_groups=mesh['blk'=64,'rep'=8] {'blk'}, dimensions={0} | all-to-all | bytes 65536 | tf_op jit(solution)/shard_map/all_to_all | solution.py:114
  217.2 0.8 broadcast_in_dim.30
  218.0 3.4 %all-to-all-start.4 = ((f32[8,1,8192]{2,1,0:T(1,128)}), f32[8,1,8192]{2,1,0:T(1,128)S(1)}, u32[]{:S(2)}, u32[]{:S(2)}) async-start(f32[8,1,8192]{2,1,0:T(1,128)} %broadcast_in_dim.30), calls=%async_computation.4 | async-start | bytes 524288 | tf_op jit(solution)/shard_map/all_to_all | solution.py:114
  221.4 0.0 copy-done
  221.4 0.8 convolution_convert_fusion
  222.3 7.0 %all-to-all-done.4 = f32[8,1,8192]{2,1,0:T(1,128)S(1)} async-done(((f32[8,1,8192]{2,1,0:T(1,128)}), f32[8,1,8192]{2,1,0:T(1,128)S(1)}, u32[]{:S(2)}, u32[]{:S(2)}) %all-to-all-start.4) | async-done | bytes 262176 | tf_op jit(solution)/shard_map/all_to_all | solution.py:114
  229.3 0.7 multiply_reduce_fusion
  230.0 0.7 mul.35
  (6 shorter events, 0.1 us)
Async XLA Ops:
  0.6 220.8 %copy-start = (bf16[256,256]{1,0:T(8,128)(2,1)S(1)}, bf16[256,256]{1,0:T(8,128)(2,1)}, u32[]{:S(2)}) copy-start(bf16[256,256]{1,0:T(8,128)(2,1)} %param.9) | copy-start | bytes 393220
  66.9 5.0 %copy-start.2 = (s32[1,8,8,16,128]{4,3,2,1,0:T(8,128)S(1)}, s32[1,8,8,16,128]{4,3,2,1,0:T(8,128)}, u32[]{:S(2)}) copy-start(s32[1,8,8,16,128]{4,3,2,1,0:T(8,128)} %param.10) | copy-start | bytes 1572868
  75.5 86.8 %copy-start.1 = (bf16[128,256]{1,0:T(8,128)(2,1)S(1)}, bf16[128,256]{1,0:T(8,128)(2,1)}, u32[]{:S(2)}) copy-start(bf16[128,256]{1,0:T(8,128)(2,1)} %param.7) | copy-start | bytes 196612
  79.3 82.9 %all-to-all-start = ((f32[8,128,256]{2,1,0:T(8,128)}), f32[8,128,256]{2,1,0:T(8,128)S(1)}, u32[]{:S(2)}, u32[]{:S(2)}) async-start(f32[8,128,256]{2,1,0:T(8,128)} %copy.29), calls=%async_computation | async-start | bytes 2097152 | tf_op jit(solution)/shard_map/all_to_all | solution.py:160
  218.0 11.3 %all-to-all-start.4 = ((f32[8,1,8192]{2,1,0:T(1,128)}), f32[8,1,8192]{2,1,0:T(1,128)S(1)}, u32[]{:S(2)}, u32[]{:S(2)}) async-start(f32[8,1,8192]{2,1,0:T(1,128)} %broadcast_in_dim.30), calls=%async_computation.4 | async-start | bytes 524288 | tf_op jit(solution)/shard_map/all_to_all | solution.py:114

commit v3 on v2

--- a/solution.py
+++ b/solution.py
@@ -12,78 +12,63 @@
 MESH_ID = pl.DeviceIdType.MESH
 
 
-def gather_kernel(steps, blocks, slab_ref, out_ref, send_sem, recv_sem, local_sem):
+def gather_kernel(steps, blocks, slab_ref, out_ref, send_sem, recv_sem):
     me = lax.axis_index("blk")
     rep = lax.axis_index("rep")
     rows = slab_ref.shape[0] // CHUNKS
-    far_to = lax.rem(me - steps * rep + blocks * steps, blocks)
-    far_from = lax.rem(me + steps * rep, blocks)
+    centre = steps // 2
+    reach = steps * rep + centre
+    far_to = lax.rem(me - reach + blocks * steps, blocks)
+    far_from = lax.rem(me + reach, blocks)
     left = lax.rem(me + blocks - 1, blocks)
     right = lax.rem(me + 1, blocks)
-    remote_first = rep != 0
 
     barrier = pltpu.get_barrier_semaphore()
-    for partner in (left, right):
+    for partner in (left, right, far_to, far_from):
         pl.semaphore_signal(barrier, inc=1, device_id=(partner, rep), device_id_type=MESH_ID)
-
-    @pl.when(remote_first)
-    def _():
-        for partner in (far_to, far_from):
-            pl.semaphore_signal(barrier, inc=1, device_id=(partner, rep), device_id_type=MESH_ID)
-        pl.semaphore_wait(barrier, 4)
-
-    @pl.when(jnp.logical_not(remote_first))
-    def _():
-        pl.semaphore_wait(barrier, 2)
+    pl.semaphore_wait(barrier, 4)
 
     def part(c):
         return pl.ds(c * rows, rows)
 
-    def forward(s, c, target):
-        src = slab_ref.at[part(c)] if s == 0 else out_ref.at[s - 1, part(c)]
+    def copy(src_slot, dst_slot, c, target):
+        src = slab_ref.at[part(c)] if src_slot is None else out_ref.at[src_slot, part(c)]
         return pltpu.make_async_remote_copy(
             src_ref=src,
-            dst_ref=out_ref.at[s, part(c)],
-            send_sem=send_sem.at[s, c],
-            recv_sem=recv_sem.at[s, c],
+            dst_ref=out_ref.at[dst_slot, part(c)],
+            send_sem=send_sem.at[dst_slot, c],
+            recv_sem=recv_sem.at[dst_slot, c],
             device_id=(target, rep),
             device_id_type=MESH_ID,
         )
 
-    @pl.when(remote_first)
-    def _():
+    for c in range(CHUNKS):
+        copy(None, centre, c, far_to).start()
+
+    sent = []
+    for k in range(1, centre + 1):
         for c in range(CHUNKS):
-            forward(0, c, far_to).start()
-
-    @pl.when(jnp.logical_not(remote_first))
-    def _():
-        for c in range(CHUNKS):
-            local = pltpu.make_async_copy(slab_ref.at[part(c)], out_ref.at[0, part(c)], local_sem.at[c])
-            local.start()
-        for c in range(CHUNKS):
-            pltpu.make_async_copy(slab_ref.at[part(c)], out_ref.at[0, part(c)], local_sem.at[c]).wait()
-
-    for s in range(1, steps):
-        for c in range(CHUNKS):
-            if s == 1:
-                @pl.when(remote_first)
-                def _():
-                    forward(0, c, far_to).wait_recv()
-            else:
-                forward(s - 1, c, left).wait_recv()
-            forward(s, c, left).start()
+            up = centre + k
+            down = centre - k
+            if up < steps:
+                copy(up - 1, up - 1, c, left).wait_recv()
+                forward = copy(up - 1, up, c, left)
+                forward.start()
+                sent.append(forward)
+            if down >= 0:
+                if k > 1 or up >= steps:
+                    copy(down + 1, down + 1, c, right).wait_recv()
+                forward = copy(down + 1, down, c, right)
+                forward.start()
+                sent.append(forward)
 
     for c in range(CHUNKS):
-        forward(steps - 1, c, left).wait_recv()
-
-    @pl.when(remote_first)
-    def _():
-        for c in range(CHUNKS):
-            forward(0, c, far_to).wait_send()
-
-    for s in range(1, steps):
-        for c in range(CHUNKS):
-            forward(s, c, left).wait_send()
+        copy(None, steps - 1, c, left).wait_recv()
+        copy(None, 0, c, right).wait_recv()
+    for c in range(CHUNKS):
+        copy(None, centre, c, far_to).wait_send()
+    for forward in sent:
+        forward.wait_send()
 
 
 def gather_sources(scaled, steps, blocks):
@@ -96,7 +81,6 @@
         scratch_shapes=[
             pltpu.SemaphoreType.DMA((steps, CHUNKS)),
             pltpu.SemaphoreType.DMA((steps, CHUNKS)),
-            pltpu.SemaphoreType.DMA((CHUNKS,)),
         ],
         compiler_params=pltpu.CompilerParams(collective_id=0, has_side_effects=True),
     )(scaled)

time: 231 us -> 236 us (1.022)
  starting transfers between devices: 69.4 us -> 82.6 us
  Pallas kernels: 61.9 us -> 56.2 us
    all_to_all x1, starting transfers between devices: 66 us -> 79.2 us  [per_device(): lax.all_to_all(partial_sums.reshape(group_size, share_rows, width), 'rep'...]
    pallas_call x1, Pallas kernels: 61.9 us -> 56.2 us  [gather_sources(): pl.pallas_call(functools.partial(gather_kernel, steps, blocks), out_shape...]
where the time goes in v3:
time: 236 us; the launch traced here: 235 us
  starting transfers between devices  82.6 us (35%)
  Pallas kernels  56.2 us (24%)
  blocking collectives  52.8 us (22%)
  waiting for transfers between devices  22 us (9%)
  local copies, waits for them, and re-layouts  9.43 us (4%)
  matrix products  7.14 us (3%)
  other arithmetic  4.42 us (2%)
    all_to_all x1, starting transfers between devices, per_device(): lax.all_to_all(partial_sums.reshape(group_size, share_rows, width), 'rep'...  79.2 us
    pallas_call x1, Pallas kernels, gather_sources(): pl.pallas_call(functools.partial(gather_kernel, steps, blocks), out_shape...  56.2 us
    all_to_all x2, blocking collectives, scatter_sum(): pieces = lax.all_to_all(flat.reshape(size, -1), axis, 0, 0, tiled=False)  35.6 us
    all_to_all x1, blocking collectives, gather_all(): return lax.all_to_all(copies, axis, 0, 0, tiled=False).reshape(-1)  17.2 us
    all_to_all x1, waiting for transfers between devices, per_device(): lax.all_to_all(partial_sums.reshape(group_size, share_rows, width), 'rep'...  14.9 us
    all_to_all x1, waiting for transfers between devices, gather_all(): return lax.all_to_all(copies, axis, 0, 0, tiled=False).reshape(-1)  7.03 us
    gather x2, local copies, waits for them, and re-layouts, per_device(): picked = jnp.take_along_axis(sources, coords[:, 0, :, None, None], axis=1)  5.11 us
  transfers between devices with their start and end apart: 2, of which 2 were waited for; matrix products, arithmetic and copies ran while one was open for 0% of the time, Pallas kernels for 0%

profile of v3, /device:TPU:1, one launch (start us, length us, event | category | flops | bytes accessed | tf_op | source)
XLA Modules:
  0.0 235.3 jit_solution(11442271284528499455)
XLA Ops:
  0.6 0.0 copy-start
  0.6 0.7 copy.39
  1.4 0.7 iota_compare_fusion.1
  2.1 0.7 convert_rsqrt_fusion
  2.8 0.1 reshape.129
  2.8 0.1 copy.27
  2.9 0.1 shift_right_arithmetic.26
  3.0 2.0 multiply_convert_fusion.slab_ref
  5.1 56.2 %shard_map.86 = bf16[8,1024,256]{2,1,0:T(8,128)(2,1)} custom-call(bf16[1024,256]{1,0:T(8,128)(2,1)} %multiply_convert_fusion.slab_ref), custom_call_target="tpu_custom_call" | custom-call | tf_op jit(solution)/shard_map/pallas_call | solution.py:76
  61.3 0.0 copy-start.2
  61.3 5.0 %gather_fusion = bf16[64,128,256]{2,1,0:T(8,128)(2,1)} fusion(bf16[8,8,128,256]{3,2,1,0:T(8,128)(2,1)} %bitcast.37, s32[64]{0:T(128)S(1)} %reshape.129), kind=kCustom, calls=%fused_computation | custom fusion | bytes 8389120 | tf_op jit(solution)/shard_map/jit(take_along_axis)/gather | solution.py:129
  66.3 0.0 copy-done.2
  66.3 3.5 %fusion.4 = bf16[8,8,128,256]{3,2,1,0:T(8,128)(2,1)S(1)} fusion(bf16[8,8,128,256]{3,2,1,0:T(8,128)(2,1)} %bitcast.38, pred[8,8]{1,0:T(8,128)(4,1)S(1)} %compare_and_fusion, s32[128]{0:T(128)S(1)} %shift_right_arithmetic.26, s32[8,8,16,128]{3,2,1,0:T(8,128)S(1)} %bitcast.45), kind=kOutput, calls=%fused_computation.6 | convolution fusion | flops 542113792 | bytes 8913472 | tf_op jit(solution)/shard_map/skvu,skuf->skvf/dot_general | solution.py:131
  69.9 0.0 copy-start.1
  69.9 2.5 %fusion.12 = f32[8,128,256]{2,0,1:T(8,128)S(1)} fusion(bf16[8,8,128,256]{3,2,1,0:T(8,128)(2,1)S(1)} %fusion.4, s32[8,8]{0,1:T(8,128)S(1)} %copy.27, pred[8,8]{0,1:T(8,128)(4,1)S(1)} %iota_compare_fusion.1), kind=kOutput, calls=%fused_computation.13 | convolution fusion | flops 33555456 | bytes 5243200 | tf_op jit(solution)/shard_map/skc,skvf->cvf/dot_general | solution.py:139
  72.4 1.3 copy.29
  73.7 79.2 %all-to-all-start = ((f32[8,128,256]{2,1,0:T(8,128)}), f32[8,128,256]{2,1,0:T(8,128)S(1)}, u32[]{:S(2)}, u32[]{:S(2)}) async-start(f32[8,128,256]{2,1,0:T(8,128)} %copy.29), calls=%async_computation | async-start | bytes 2097152 | tf_op jit(solution)/shard_map/all_to_all | solution.py:144
  152.8 0.1 dynamic_slice.3
  152.9 14.9 %all-to-all-done = f32[8,128,256]{2,1,0:T(8,128)S(1)} async-done(((f32[8,128,256]{2,1,0:T(8,128)}), f32[8,128,256]{2,1,0:T(8,128)S(1)}, u32[]{:S(2)}, u32[]{:S(2)}) %all-to-all-start) | async-done | bytes 1048608 | tf_op jit(solution)/shard_map/all_to_all | solution.py:144
  167.9 0.1 reduce_sum.27
  167.9 0.0 copy-done.1
  167.9 0.3 convolution_bitcast_fusion
  168.2 0.1 copy.30
  168.4 0.3 all_to_all.30
  168.6 11.6 %all_to_all.36 = f32[8,1,8192]{2,1,0:T(1,128)S(1)} all-to-all(f32[8,1,8192]{2,1,0:T(1,128)S(1)} %all_to_all.30), channel_id=1, replica_groups=mesh['blk'=64,'rep'=8] {'rep'}, dimensions={0} | all-to-all | bytes 524288 | tf_op jit(solution)/shard_map/all_to_all | solution.py:91
  180.2 0.2 reduce_sum.28
  180.4 24.0 %all_to_all.37 = f32[64,1,128]{2,1,0:T(1,128)S(1)} all-to-all(f32[64,1,128]{2,1,0:T(1,128)S(1)} %bitcast.39), channel_id=1, replica_groups=mesh['blk'=64,'rep'=8] {'blk'}, dimensions={0} | all-to-all | bytes 65536 | tf_op jit(solution)/shard_map/all_to_all | solution.py:91
  204.5 17.2 %all_to_all.38 = f32[64,1,128]{2,1,0:T(1,128)S(1)} all-to-all(f32[64,1,128]{2,1,0:T(1,128)S(1)} %broadcast_in_dim.28), channel_id=1, replica_groups=mesh['blk'=64,'rep'=8] {'blk'}, dimensions={0} | all-to-all | bytes 65536 | tf_op jit(solution)/shard_map/all_to_all | solution.py:98
  221.7 0.8 broadcast_in_dim.30
  222.5 3.4 %all-to-all-start.4 = ((f32[8,1,8192]{2,1,0:T(1,128)}), f32[8,1,8192]{2,1,0:T(1,128)S(1)}, u32[]{:S(2)}, u32[]{:S(2)}) async-start(f32[8,1,8192]{2,1,0:T(1,128)} %broadcast_in_dim.30), calls=%async_computation.4 | async-start | bytes 524288 | tf_op jit(solution)/shard_map/all_to_all | solution.py:98
  225.9 0.0 copy-done
  225.9 0.8 convolution_convert_fusion
  226.8 7.0 %all-to-all-done.4 = f32[8,1,8192]{2,1,0:T(1,128)S(1)} async-done(((f32[8,1,8192]{2,1,0:T(1,128)}), f32[8,1,8192]{2,1,0:T(1,128)S(1)}, u32[]{:S(2)}, u32[]{:S(2)}) %all-to-all-start.4) | async-done | bytes 262176 | tf_op jit(solution)/shard_map/all_to_all | solution.py:98
  233.8 0.7 multiply_reduce_fusion
  234.5 0.7 mul.35
  (6 shorter events, 0.1 us)
Async XLA Ops:
  0.6 225.3 %copy-start = (bf16[256,256]{1,0:T(8,128)(2,1)S(1)}, bf16[256,256]{1,0:T(8,128)(2,1)}, u32[]{:S(2)}) copy-start(bf16[256,256]{1,0:T(8,128)(2,1)} %param.9) | copy-start | bytes 393220
  61.3 5.0 %copy-start.2 = (s32[1,8,8,16,128]{4,3,2,1,0:T(8,128)S(1)}, s32[1,8,8,16,128]{4,3,2,1,0:T(8,128)}, u32[]{:S(2)}) copy-start(s32[1,8,8,16,128]{4,3,2,1,0:T(8,128)} %param.10) | copy-start | bytes 1572868
  69.9 98.1 %copy-start.1 = (bf16[128,256]{1,0:T(8,128)(2,1)S(1)}, bf16[128,256]{1,0:T(8,128)(2,1)}, u32[]{:S(2)}) copy-start(bf16[128,256]{1,0:T(8,128)(2,1)} %param.7) | copy-start | bytes 196612
  73.7 94.2 %all-to-all-start = ((f32[8,128,256]{2,1,0:T(8,128)}), f32[8,128,256]{2,1,0:T(8,128)S(1)}, u32[]{:S(2)}, u32[]{:S(2)}) async-start(f32[8,128,256]{2,1,0:T(8,128)} %copy.29), calls=%async_computation | async-start | bytes 2097152 | tf_op jit(solution)/shard_map/all_to_all | solution.py:144
  222.5 11.3 %all-to-all-start.4 = ((f32[8,1,8192]{2,1,0:T(1,128)}), f32[8,1,8192]{2,1,0:T(1,128)S(1)}, u32[]{:S(2)}, u32[]{:S(2)}) async-start(f32[8,1,8192]{2,1,0:T(1,128)} %broadcast_in_dim.30), calls=%async_computation.4 | async-start | bytes 524288 | tf_op jit(solution)/shard_map/all_to_all | solution.py:98

commit v4 on v3

--- a/solution.py
+++ b/solution.py
@@ -86,6 +86,45 @@
     )(scaled)
 
 
+def butterfly_kernel(levels, term_ref, out_ref, held, send_sem, recv_sem):
+    me = lax.axis_index("blk")
+    rep = lax.axis_index("rep")
+    partners = [jnp.bitwise_xor(me, 1 << k) for k in range(levels)]
+    barrier = pltpu.get_barrier_semaphore()
+    for partner in partners:
+        pl.semaphore_signal(barrier, inc=1, device_id=(partner, rep), device_id_type=MESH_ID)
+    pl.semaphore_wait(barrier, levels)
+    out_ref[...] = term_ref[...]
+    for k, partner in enumerate(partners):
+        swap = pltpu.make_async_remote_copy(
+            src_ref=out_ref,
+            dst_ref=held.at[k],
+            send_sem=send_sem.at[k],
+            recv_sem=recv_sem.at[k],
+            device_id=(partner, rep),
+            device_id_type=MESH_ID,
+        )
+        swap.start()
+        swap.wait()
+        out_ref[...] = out_ref[...] + held[k]
+
+
+def butterfly_sum(term):
+    levels = lax.axis_size("blk").bit_length() - 1
+    return pl.pallas_call(
+        functools.partial(butterfly_kernel, levels),
+        out_shape=jax.ShapeDtypeStruct(term.shape, term.dtype),
+        in_specs=[pl.BlockSpec(memory_space=pltpu.VMEM)],
+        out_specs=pl.BlockSpec(memory_space=pltpu.VMEM),
+        scratch_shapes=[
+            pltpu.VMEM((levels,) + term.shape, term.dtype),
+            pltpu.SemaphoreType.DMA((levels,)),
+            pltpu.SemaphoreType.DMA((levels,)),
+        ],
+        compiler_params=pltpu.CompilerParams(collective_id=1, has_side_effects=True),
+    )(term)
+
+
 def scatter_sum(flat, axis):
     size = lax.axis_size(axis)
     pieces = lax.all_to_all(flat.reshape(size, -1), axis, 0, 0, tiled=False)
@@ -99,8 +138,10 @@
 
 
 def all_reduce_by_exchange(term):
-    flat = scatter_sum(scatter_sum(term.reshape(-1), "rep"), "blk")
-    return gather_all(gather_all(flat, "blk"), "rep").reshape(term.shape)
+    flat = scatter_sum(term.reshape(-1), "rep")
+    width = term.shape[-1]
+    summed = butterfly_sum(flat.reshape(-1, width)).reshape(-1)
+    return gather_all(summed, "rep").reshape(term.shape)
 
 
 def unpack_blocks(words):

time: 236 us -> 227 us (0.962); the launches traced: 235 us -> 223 us
  blocking collectives: 52.8 us -> 11.6 us
  Pallas kernels: 56.2 us -> 83.9 us
    pallas_call x0 -> x1, Pallas kernels: none -> 27.7 us  [butterfly_sum(): pl.pallas_call(functools.partial(butterfly_kernel, levels), out_shape=jax...]
    all_to_all x2 -> x1, blocking collectives: 35.6 us -> 11.6 us  [scatter_sum(): pieces = lax.all_to_all(flat.reshape(size, -1), axis, 0, 0, tiled=False)]
    all_to_all x1 -> x0, blocking collectives: 17.2 us -> none  [gather_all(): return lax.all_to_all(copies, axis, 0, 0, tiled=False).reshape(-1)]
where the time goes in v4:
time: 227 us; the launch traced here: 223 us
  Pallas kernels  83.9 us (37%)
  starting transfers between devices  82.6 us (36%)
  waiting for transfers between devices  21.7 us (10%)
  blocking collectives  11.6 us (5%)
  local copies, waits for them, and re-layouts  10.8 us (5%)
  matrix products  7.14 us (3%)
  other arithmetic  4.4 us (2%)
    all_to_all x1, starting transfers between devices, per_device(): lax.all_to_all(partial_sums.reshape(group_size, share_rows, width), 'rep'...  79.2 us
    pallas_call x1, Pallas kernels, gather_sources(): pl.pallas_call(functools.partial(gather_kernel, steps, blocks), out_shape...  56.2 us
    pallas_call x1, Pallas kernels, butterfly_sum(): pl.pallas_call(functools.partial(butterfly_kernel, levels), out_shape=jax...  27.7 us
    all_to_all x1, waiting for transfers between devices, per_device(): lax.all_to_all(partial_sums.reshape(group_size, share_rows, width), 'rep'...  14.9 us
    all_to_all x1, blocking collectives, scatter_sum(): pieces = lax.all_to_all(flat.reshape(size, -1), axis, 0, 0, tiled=False)  11.6 us
    all_to_all x1, waiting for transfers between devices, gather_all(): return lax.all_to_all(copies, axis, 0, 0, tiled=False).reshape(-1)  6.72 us
    gather x2, local copies, waits for them, and re-layouts, per_device(): picked = jnp.take_along_axis(sources, coords[:, 0, :, None, None], axis=1)  5.11 us
  transfers between devices with their start and end apart: 2, of which 2 were waited for; matrix products, arithmetic and copies ran while one was open for 0% of the time, Pallas kernels for 0%

profile of v4, /device:TPU:1, one launch (start us, length us, event | category | flops | bytes accessed | tf_op | source)
XLA Modules:
  0.0 222.9 jit_solution(5429809687977350628)
XLA Ops:
  0.6 0.0 copy-start
  0.6 0.7 copy.27
  1.4 0.7 iota_compare_fusion.1
  2.1 0.7 convert_rsqrt_fusion
  2.8 0.1 reshape.122
  2.8 0.1 copy.15
  2.9 0.1 shift_right_arithmetic.26
  3.0 2.0 multiply_convert_fusion.slab_ref
  5.1 56.2 %shard_map.86 = bf16[8,1024,256]{2,1,0:T(8,128)(2,1)} custom-call(bf16[1024,256]{1,0:T(8,128)(2,1)} %multiply_convert_fusion.slab_ref), custom_call_target="tpu_custom_call" | custom-call | tf_op jit(solution)/shard_map/pallas_call | solution.py:76
  61.3 0.0 copy-start.2
  61.3 5.0 %gather_fusion = bf16[64,128,256]{2,1,0:T(8,128)(2,1)} fusion(bf16[8,8,128,256]{3,2,1,0:T(8,128)(2,1)} %bitcast.36, s32[64]{0:T(128)S(1)} %reshape.122), kind=kCustom, calls=%fused_computation | custom fusion | bytes 8389120 | tf_op jit(solution)/shard_map/jit(take_along_axis)/gather | solution.py:170
  66.3 0.0 copy-done.2
  66.3 3.5 %fusion.4 = bf16[8,8,128,256]{3,2,1,0:T(8,128)(2,1)S(1)} fusion(bf16[8,8,128,256]{3,2,1,0:T(8,128)(2,1)} %bitcast.37, pred[8,8]{1,0:T(8,128)(4,1)S(1)} %compare_and_fusion, s32[128]{0:T(128)S(1)} %shift_right_arithmetic.26, s32[8,8,16,128]{3,2,1,0:T(8,128)S(1)} %bitcast.43), kind=kOutput, calls=%fused_computation.6 | convolution fusion | flops 542113792 | bytes 8913472 | tf_op jit(solution)/shard_map/skvu,skuf->skvf/dot_general | solution.py:172
  69.9 0.0 copy-start.1
  69.9 2.5 %fusion.12 = f32[8,128,256]{2,0,1:T(8,128)S(1)} fusion(bf16[8,8,128,256]{3,2,1,0:T(8,128)(2,1)S(1)} %fusion.4, s32[8,8]{0,1:T(8,128)S(1)} %copy.15, pred[8,8]{0,1:T(8,128)(4,1)S(1)} %iota_compare_fusion.1), kind=kOutput, calls=%fused_computation.13 | convolution fusion | flops 33555456 | bytes 5243200 | tf_op jit(solution)/shard_map/skc,skvf->cvf/dot_general | solution.py:180
  72.4 1.3 copy.17
  73.7 79.2 %all-to-all-start = ((f32[8,128,256]{2,1,0:T(8,128)}), f32[8,128,256]{2,1,0:T(8,128)S(1)}, u32[]{:S(2)}, u32[]{:S(2)}) async-start(f32[8,128,256]{2,1,0:T(8,128)} %copy.17), calls=%async_computation | async-start | bytes 2097152 | tf_op jit(solution)/shard_map/all_to_all | solution.py:185
  152.8 0.1 dynamic_slice.3
  152.9 14.9 %all-to-all-done = f32[8,128,256]{2,1,0:T(8,128)S(1)} async-done(((f32[8,128,256]{2,1,0:T(8,128)}), f32[8,128,256]{2,1,0:T(8,128)S(1)}, u32[]{:S(2)}, u32[]{:S(2)}) %all-to-all-start) | async-done | bytes 1048608 | tf_op jit(solution)/shard_map/all_to_all | solution.py:185
  167.9 0.1 reduce_sum.18
  167.9 0.0 copy-done.1
  167.9 0.3 convolution_bitcast_fusion
  168.2 0.1 copy.18
  168.4 0.3 all_to_all.17
  168.6 11.6 %all_to_all.21 = f32[8,1,8192]{2,1,0:T(1,128)S(1)} all-to-all(f32[8,1,8192]{2,1,0:T(1,128)S(1)} %all_to_all.17), channel_id=1, replica_groups=mesh['blk'=64,'rep'=8] {'rep'}, dimensions={0} | all-to-all | bytes 524288 | tf_op jit(solution)/shard_map/all_to_all | solution.py:130
  180.2 0.2 reduce_sum.19
  180.4 0.6 reshape.121.term_ref
  181.1 27.7 %shard_map.87 = f32[32,256]{1,0:T(8,128)} custom-call(f32[32,256]{1,0:T(8,128)} %reshape.121.term_ref), custom_call_target="tpu_custom_call" | custom-call | tf_op jit(solution)/shard_map/pallas_call | solution.py:114
  208.8 0.8 copy.21
  209.6 0.8 broadcast_in_dim.23
  210.4 3.4 %all-to-all-start.2 = ((f32[8,1,8192]{2,1,0:T(1,128)}), f32[8,1,8192]{2,1,0:T(1,128)S(1)}, u32[]{:S(2)}, u32[]{:S(2)}) async-start(f32[8,1,8192]{2,1,0:T(1,128)} %broadcast_in_dim.23), calls=%async_computation.2 | async-start | bytes 524288 | tf_op jit(solution)/shard_map/all_to_all | solution.py:137
  213.8 0.0 copy-done
  213.8 0.8 convolution_convert_fusion
  214.7 6.7 %all-to-all-done.2 = f32[8,1,8192]{2,1,0:T(1,128)S(1)} async-done(((f32[8,1,8192]{2,1,0:T(1,128)}), f32[8,1,8192]{2,1,0:T(1,128)S(1)}, u32[]{:S(2)}, u32[]{:S(2)}) %all-to-all-start.2) | async-done | bytes 262176 | tf_op jit(solution)/shard_map/all_to_all | solution.py:137
  221.4 0.7 multiply_reduce_fusion
  222.1 0.7 mul.35
  (4 shorter events, 0.0 us)
Async XLA Ops:
  0.6 213.2 %copy-start = (bf16[256,256]{1,0:T(8,128)(2,1)S(1)}, bf16[256,256]{1,0:T(8,128)(2,1)}, u32[]{:S(2)}) copy-start(bf16[256,256]{1,0:T(8,128)(2,1)} %param.9) | copy-start | bytes 393220
  61.3 5.0 %copy-start.2 = (s32[1,8,8,16,128]{4,3,2,1,0:T(8,128)S(1)}, s32[1,8,8,16,128]{4,3,2,1,0:T(8,128)}, u32[]{:S(2)}) copy-start(s32[1,8,8,16,128]{4,3,2,1,0:T(8,128)} %param.10) | copy-start | bytes 1572868
  69.9 98.1 %copy-start.1 = (bf16[128,256]{1,0:T(8,128)(2,1)S(1)}, bf16[128,256]{1,0:T(8,128)(2,1)}, u32[]{:S(2)}) copy-start(bf16[128,256]{1,0:T(8,128)(2,1)} %param.7) | copy-start | bytes 196612
  73.7 94.2 %all-to-all-start = ((f32[8,128,256]{2,1,0:T(8,128)}), f32[8,128,256]{2,1,0:T(8,128)S(1)}, u32[]{:S(2)}, u32[]{:S(2)}) async-start(f32[8,128,256]{2,1,0:T(8,128)} %copy.17), calls=%async_computation | async-start | bytes 2097152 | tf_op jit(solution)/shard_map/all_to_all | solution.py:185
  210.4 11.0 %all-to-all-start.2 = ((f32[8,1,8192]{2,1,0:T(1,128)}), f32[8,1,8192]{2,1,0:T(1,128)S(1)}, u32[]{:S(2)}, u32[]{:S(2)}) async-start(f32[8,1,8192]{2,1,0:T(1,128)} %broadcast_in_dim.23), calls=%async_computation.2 | async-start | bytes 524288 | tf_op jit(solution)/shard_map/all_to_all | solution.py:137

commit v5 on v4

--- a/solution.py
+++ b/solution.py
@@ -8,11 +8,26 @@
 from jax.experimental.pallas import tpu as pltpu
 from jax.sharding import PartitionSpec as P
 
-CHUNKS = 4
+CHUNKS = 8
 MESH_ID = pl.DeviceIdType.MESH
 
 
-def gather_kernel(steps, blocks, slab_ref, out_ref, send_sem, recv_sem):
+def relay_plan(steps, blocks, group):
+    plans = []
+    for rep in range(group):
+        reach = steps * rep + steps // 2
+        short = min(reach, blocks - reach)
+        if 4 * short < 5 * blocks // 4:
+            plans.append((CHUNKS, 0, 0))
+            continue
+        direct = min(CHUNKS, max(1, int(CHUNKS * (blocks - short) / blocks + 0.5)))
+        sign = 1 if reach < blocks - reach else -1
+        plans.append((direct, sign, (blocks - short) // 2))
+    return plans
+
+
+def gather_kernel(steps, blocks, plans, slab_ref, out_ref, relay_buf, send_sem, recv_sem,
+                  relay_in_sem, relay_fwd_sem):
     me = lax.axis_index("blk")
     rep = lax.axis_index("rep")
     rows = slab_ref.shape[0] // CHUNKS
@@ -23,11 +38,6 @@
     left = lax.rem(me + blocks - 1, blocks)
     right = lax.rem(me + 1, blocks)
 
-    barrier = pltpu.get_barrier_semaphore()
-    for partner in (left, right, far_to, far_from):
-        pl.semaphore_signal(barrier, inc=1, device_id=(partner, rep), device_id_type=MESH_ID)
-    pl.semaphore_wait(barrier, 4)
-
     def part(c):
         return pl.ds(c * rows, rows)
 
@@ -42,8 +52,50 @@
             device_id_type=MESH_ID,
         )
 
-    for c in range(CHUNKS):
-        copy(None, centre, c, far_to).start()
+    def relay_out(c, target):
+        return pltpu.make_async_remote_copy(
+            src_ref=slab_ref.at[part(c)],
+            dst_ref=relay_buf.at[c],
+            send_sem=send_sem.at[centre, c],
+            recv_sem=relay_in_sem.at[c],
+            device_id=(target, rep),
+            device_id_type=MESH_ID,
+        )
+
+    def relay_on(c, target):
+        return pltpu.make_async_remote_copy(
+            src_ref=relay_buf.at[c],
+            dst_ref=out_ref.at[centre, part(c)],
+            send_sem=relay_fwd_sem.at[c],
+            recv_sem=recv_sem.at[centre, c],
+            device_id=(target, rep),
+            device_id_type=MESH_ID,
+        )
+
+    barrier = pltpu.get_barrier_semaphore()
+    for partner in (left, right, far_to, far_from):
+        pl.semaphore_signal(barrier, inc=1, device_id=(partner, rep), device_id_type=MESH_ID)
+
+    for plane, (direct, sign, leg) in enumerate(plans):
+        @pl.when(rep == plane)
+        def _():
+            if direct < CHUNKS:
+                ahead = lax.rem(me + sign * leg + blocks, blocks)
+                behind = lax.rem(me - sign * leg + blocks, blocks)
+                for partner in (ahead, behind):
+                    pl.semaphore_signal(barrier, inc=1, device_id=(partner, rep), device_id_type=MESH_ID)
+                pl.semaphore_wait(barrier, 6)
+                for c in range(direct):
+                    copy(None, centre, c, far_to).start()
+                for c in range(direct, CHUNKS):
+                    relay_out(c, ahead).start()
+                for c in range(direct, CHUNKS):
+                    relay_out(c, ahead).wait_recv()
+                    relay_on(c, ahead).start()
+            else:
+                pl.semaphore_wait(barrier, 4)
+                for c in range(CHUNKS):
+                    copy(None, centre, c, far_to).start()
 
     sent = []
     for k in range(1, centre + 1):
@@ -65,22 +117,34 @@
     for c in range(CHUNKS):
         copy(None, steps - 1, c, left).wait_recv()
         copy(None, 0, c, right).wait_recv()
-    for c in range(CHUNKS):
-        copy(None, centre, c, far_to).wait_send()
+
+    for plane, (direct, sign, leg) in enumerate(plans):
+        @pl.when(rep == plane)
+        def _():
+            ahead = lax.rem(me + sign * leg + blocks, blocks)
+            for c in range(direct):
+                copy(None, centre, c, far_to).wait_send()
+            for c in range(direct, CHUNKS):
+                relay_out(c, ahead).wait_send()
+                relay_on(c, ahead).wait_send()
     for forward in sent:
         forward.wait_send()
 
 
-def gather_sources(scaled, steps, blocks):
+def gather_sources(scaled, steps, blocks, group):
     slab_rows, width = scaled.shape
+    plans = relay_plan(steps, blocks, group)
     return pl.pallas_call(
-        functools.partial(gather_kernel, steps, blocks),
+        functools.partial(gather_kernel, steps, blocks, plans),
         out_shape=jax.ShapeDtypeStruct((steps, slab_rows, width), scaled.dtype),
         in_specs=[pl.BlockSpec(memory_space=pl.ANY)],
         out_specs=pl.BlockSpec(memory_space=pl.ANY),
         scratch_shapes=[
+            pltpu.VMEM((CHUNKS, slab_rows // CHUNKS, width), scaled.dtype),
             pltpu.SemaphoreType.DMA((steps, CHUNKS)),
             pltpu.SemaphoreType.DMA((steps, CHUNKS)),
+            pltpu.SemaphoreType.DMA((CHUNKS,)),
+            pltpu.SemaphoreType.DMA((CHUNKS,)),
         ],
         compiler_params=pltpu.CompilerParams(collective_id=0, has_side_effects=True),
     )(scaled)
@@ -162,7 +226,7 @@
     inverse_root = lax.rsqrt(degrees.astype(jnp.float32))
     scaled = (out_grad.astype(jnp.float32) * inverse_root[:, None]).astype(jnp.bfloat16)
 
-    sources = gather_sources(scaled, step_count, blocks).reshape(
+    sources = gather_sources(scaled, step_count, blocks, group_size).reshape(
         step_count, row_blocks, 128, width
     )
     coords = block_coords[0]

time: 227 us -> 203 us (0.89)
  starting transfers between devices: 82.6 us -> 57.4 us
  Pallas kernels: 83.9 us -> 89.9 us
  waiting for transfers between devices: 21.7 us -> 19.4 us
    all_to_all x1, starting transfers between devices: 79.2 us -> 54 us  [per_device(): lax.all_to_all(partial_sums.reshape(group_size, share_rows, width), 'rep'...]
    pallas_call x1, Pallas kernels: 27.7 us -> 34.4 us  [butterfly_sum(): pl.pallas_call(functools.partial(butterfly_kernel, levels), out_shape=jax...]
where the time goes in v5:
time: 203 us; the launch traced here: 200 us
  Pallas kernels  89.9 us (44%)
  starting transfers between devices  57.4 us (28%)
  waiting for transfers between devices  19.4 us (10%)
  local copies, waits for them, and re-layouts  10.8 us (5%)
  blocking collectives  10.1 us (5%)
  matrix products  7.14 us (4%)
  other arithmetic  4.4 us (2%)
    pallas_call x1, Pallas kernels, gather_sources(): pl.pallas_call(functools.partial(gather_kernel, steps, blocks, plans), ou...  55.6 us
    all_to_all x1, starting transfers between devices, per_device(): lax.all_to_all(partial_sums.reshape(group_size, share_rows, width), 'rep'...  54 us
    pallas_call x1, Pallas kernels, butterfly_sum(): pl.pallas_call(functools.partial(butterfly_kernel, levels), out_shape=jax...  34.4 us
    all_to_all x1, waiting for transfers between devices, per_device(): lax.all_to_all(partial_sums.reshape(group_size, share_rows, width), 'rep'...  12.7 us
    all_to_all x1, blocking collectives, scatter_sum(): pieces = lax.all_to_all(flat.reshape(size, -1), axis, 0, 0, tiled=False)  10.1 us
    all_to_all x1, waiting for transfers between devices, gather_all(): return lax.all_to_all(copies, axis, 0, 0, tiled=False).reshape(-1)  6.72 us
    gather x2, local copies, waits for them, and re-layouts, per_device(): picked = jnp.take_along_axis(sources, coords[:, 0, :, None, None], axis=1)  5.11 us
  transfers between devices with their start and end apart: 2, of which 2 were waited for; matrix products, arithmetic and copies ran while one was open for 0% of the time, Pallas kernels for 0%

profile of v5, /device:TPU:1, one launch (start us, length us, event | category | flops | bytes accessed | tf_op | source)
XLA Modules:
  0.0 199.9 jit_solution(904180532044352627)
XLA Ops:
  0.6 0.0 copy-start
  0.6 0.7 copy.27
  1.4 0.7 iota_compare_fusion.1
  2.1 0.7 convert_rsqrt_fusion
  2.8 0.1 reshape.122
  2.8 0.1 copy.15
  2.9 0.1 shift_right_arithmetic.26
  3.0 2.0 %multiply_convert_fusion.slab_ref = bf16[1024,256]{1,0:T(8,128)(2,1)} fusion(bf16[1024,256]{1,0:T(8,128)(2,1)} %param.8, f32[1024]{0:T(1024)S(1)} %convert_rsqrt_fusion), kind=kLoop, calls=%fused_computation.16 | loop fusion | flops 786432 | bytes 1052672 | tf_op jit(solution)/shard_map/convert_element_type | solution.py:227
  5.1 55.6 %shard_map.86 = bf16[8,1024,256]{2,1,0:T(8,128)(2,1)} custom-call(bf16[1024,256]{1,0:T(8,128)(2,1)} %multiply_convert_fusion.slab_ref), custom_call_target="tpu_custom_call" | custom-call | tf_op jit(solution)/shard_map/pallas_call | solution.py:137
  60.6 0.0 copy-start.2
  60.6 5.0 %gather_fusion = bf16[64,128,256]{2,1,0:T(8,128)(2,1)} fusion(bf16[8,8,128,256]{3,2,1,0:T(8,128)(2,1)} %bitcast.36, s32[64]{0:T(128)S(1)} %reshape.122), kind=kCustom, calls=%fused_computation | custom fusion | bytes 8389120 | tf_op jit(solution)/shard_map/jit(take_along_axis)/gather | solution.py:234
  65.7 0.0 copy-done.2
  65.7 3.5 %fusion.4 = bf16[8,8,128,256]{3,2,1,0:T(8,128)(2,1)S(1)} fusion(bf16[8,8,128,256]{3,2,1,0:T(8,128)(2,1)} %bitcast.37, pred[8,8]{1,0:T(8,128)(4,1)S(1)} %compare_and_fusion, s32[128]{0:T(128)S(1)} %shift_right_arithmetic.26, s32[8,8,16,128]{3,2,1,0:T(8,128)S(1)} %bitcast.43), kind=kOutput, calls=%fused_computation.6 | convolution fusion | flops 542113792 | bytes 8913472 | tf_op jit(solution)/shard_map/skvu,skuf->skvf/dot_general | solution.py:236
  69.2 0.0 copy-start.1
  69.2 2.5 %fusion.12 = f32[8,128,256]{2,0,1:T(8,128)S(1)} fusion(bf16[8,8,128,256]{3,2,1,0:T(8,128)(2,1)S(1)} %fusion.4, s32[8,8]{0,1:T(8,128)S(1)} %copy.15, pred[8,8]{0,1:T(8,128)(4,1)S(1)} %iota_compare_fusion.1), kind=kOutput, calls=%fused_computation.13 | convolution fusion | flops 33555456 | bytes 5243200 | tf_op jit(solution)/shard_map/skc,skvf->cvf/dot_general | solution.py:244
  71.7 1.3 copy.17
  73.0 54.0 %all-to-all-start = ((f32[8,128,256]{2,1,0:T(8,128)}), f32[8,128,256]{2,1,0:T(8,128)S(1)}, u32[]{:S(2)}, u32[]{:S(2)}) async-start(f32[8,128,256]{2,1,0:T(8,128)} %copy.17), calls=%async_computation | async-start | bytes 2097152 | tf_op jit(solution)/shard_map/all_to_all | solution.py:249
  127.0 0.1 dynamic_slice.3
  127.1 12.7 %all-to-all-done = f32[8,128,256]{2,1,0:T(8,128)S(1)} async-done(((f32[8,128,256]{2,1,0:T(8,128)}), f32[8,128,256]{2,1,0:T(8,128)S(1)}, u32[]{:S(2)}, u32[]{:S(2)}) %all-to-all-start) | async-done | bytes 1048608 | tf_op jit(solution)/shard_map/all_to_all | solution.py:249
  139.8 0.1 reduce_sum.18
  139.9 0.0 copy-done.1
  139.9 0.3 convolution_bitcast_fusion
  140.2 0.1 copy.18
  140.3 0.3 all_to_all.17
  140.6 10.1 %all_to_all.21 = f32[8,1,8192]{2,1,0:T(1,128)S(1)} all-to-all(f32[8,1,8192]{2,1,0:T(1,128)S(1)} %all_to_all.17), channel_id=1, replica_groups=mesh['blk'=64,'rep'=8] {'rep'}, dimensions={0} | all-to-all | bytes 524288 | tf_op jit(solution)/shard_map/all_to_all | solution.py:194
  150.6 0.2 reduce_sum.19
  150.8 0.6 reshape.121.term_ref
  151.5 34.4 %shard_map.87 = f32[32,256]{1,0:T(8,128)} custom-call(f32[32,256]{1,0:T(8,128)} %reshape.121.term_ref), custom_call_target="tpu_custom_call" | custom-call | tf_op jit(solution)/shard_map/pallas_call | solution.py:178
  185.8 0.8 copy.21
  186.6 0.8 broadcast_in_dim.23
  187.5 3.4 %all-to-all-start.2 = ((f32[8,1,8192]{2,1,0:T(1,128)}), f32[8,1,8192]{2,1,0:T(1,128)S(1)}, u32[]{:S(2)}, u32[]{:S(2)}) async-start(f32[8,1,8192]{2,1,0:T(1,128)} %broadcast_in_dim.23), calls=%async_computation.2 | async-start | bytes 524288 | tf_op jit(solution)/shard_map/all_to_all | solution.py:201
  190.9 0.0 copy-done
  190.9 0.8 convolution_convert_fusion
  191.7 6.7 %all-to-all-done.2 = f32[8,1,8192]{2,1,0:T(1,128)S(1)} async-done(((f32[8,1,8192]{2,1,0:T(1,128)}), f32[8,1,8192]{2,1,0:T(1,128)S(1)}, u32[]{:S(2)}, u32[]{:S(2)}) %all-to-all-start.2) | async-done | bytes 262176 | tf_op jit(solution)/shard_map/all_to_all | solution.py:201
  198.4 0.7 multiply_reduce_fusion
  199.2 0.7 mul.35
  (4 shorter events, 0.0 us)
Async XLA Ops:
  0.6 190.2 %copy-start = (bf16[256,256]{1,0:T(8,128)(2,1)S(1)}, bf16[256,256]{1,0:T(8,128)(2,1)}, u32[]{:S(2)}) copy-start(bf16[256,256]{1,0:T(8,128)(2,1)} %param.9) | copy-start | bytes 393220
  60.6 5.0 %copy-start.2 = (s32[1,8,8,16,128]{4,3,2,1,0:T(8,128)S(1)}, s32[1,8,8,16,128]{4,3,2,1,0:T(8,128)}, u32[]{:S(2)}) copy-start(s32[1,8,8,16,128]{4,3,2,1,0:T(8,128)} %param.10) | copy-start | bytes 1572868
  69.2 70.7 %copy-start.1 = (bf16[128,256]{1,0:T(8,128)(2,1)S(1)}, bf16[128,256]{1,0:T(8,128)(2,1)}, u32[]{:S(2)}) copy-start(bf16[128,256]{1,0:T(8,128)(2,1)} %param.7) | copy-start | bytes 196612
  73.0 66.8 %all-to-all-start = ((f32[8,128,256]{2,1,0:T(8,128)}), f32[8,128,256]{2,1,0:T(8,128)S(1)}, u32[]{:S(2)}, u32[]{:S(2)}) async-start(f32[8,128,256]{2,1,0:T(8,128)} %copy.17), calls=%async_computation | async-start | bytes 2097152 | tf_op jit(solution)/shard_map/all_to_all | solution.py:249
  187.5 11.0 %all-to-all-start.2 = ((f32[8,1,8192]{2,1,0:T(1,128)}), f32[8,1,8192]{2,1,0:T(1,128)S(1)}, u32[]{:S(2)}, u32[]{:S(2)}) async-start(f32[8,1,8192]{2,1,0:T(1,128)} %broadcast_in_dim.23), calls=%async_computation.2 | async-start | bytes 524288 | tf_op jit(solution)/shard_map/all_to_all | solution.py:201

commit v6 on v5

--- a/solution.py
+++ b/solution.py
@@ -150,62 +150,97 @@
     )(scaled)
 
 
-def butterfly_kernel(levels, term_ref, out_ref, held, send_sem, recv_sem):
+def reduce_kernel(group, digits, term_ref, out_ref, inbox, spread, gathered, sems):
     me = lax.axis_index("blk")
     rep = lax.axis_index("rep")
-    partners = [jnp.bitwise_xor(me, 1 << k) for k in range(levels)]
+    piece = term_ref.shape[0] // group
+    rep_partners = [lax.rem(rep + j, group) for j in range(1, group)]
     barrier = pltpu.get_barrier_semaphore()
-    for partner in partners:
-        pl.semaphore_signal(barrier, inc=1, device_id=(partner, rep), device_id_type=MESH_ID)
-    pl.semaphore_wait(barrier, levels)
-    out_ref[...] = term_ref[...]
-    for k, partner in enumerate(partners):
-        swap = pltpu.make_async_remote_copy(
-            src_ref=out_ref,
-            dst_ref=held.at[k],
-            send_sem=send_sem.at[k],
-            recv_sem=recv_sem.at[k],
-            device_id=(partner, rep),
+    for partner in rep_partners:
+        pl.semaphore_signal(barrier, inc=1, device_id=(me, partner), device_id_type=MESH_ID)
+    blk_count = 0
+    for shift, width in digits:
+        for d in range(1, 1 << width):
+            pl.semaphore_signal(
+                barrier, inc=1, device_id=(jnp.bitwise_xor(me, d << shift), rep), device_id_type=MESH_ID
+            )
+            blk_count += 1
+    pl.semaphore_wait(barrier, group - 1 + blk_count)
+
+    def send(src, dst, sem_row, slot, device):
+        return pltpu.make_async_remote_copy(
+            src_ref=src,
+            dst_ref=dst,
+            send_sem=sems.at[0, sem_row, slot],
+            recv_sem=sems.at[1, sem_row, slot],
+            device_id=device,
             device_id_type=MESH_ID,
         )
-        swap.start()
-        swap.wait()
-        out_ref[...] = out_ref[...] + held[k]
-
-
-def butterfly_sum(term):
-    levels = lax.axis_size("blk").bit_length() - 1
+
+    scatter = []
+    for j, partner in enumerate(rep_partners, start=1):
+        rows = pl.ds(pl.multiple_of(partner * piece, 8), piece)
+        scatter.append(send(term_ref.at[rows], inbox.at[0, j], 0, j, (me, partner)))
+    for c in scatter:
+        c.start()
+    for c in scatter:
+        c.wait()
+    own = pl.ds(pl.multiple_of(rep * piece, 8), piece)
+    total = term_ref[own]
+    for j in range(1, group):
+        total = total + inbox[0, j]
+    spread[0, 0] = total
+
+    for level, (shift, width) in enumerate(digits):
+        members = 1 << width
+        mine = jnp.bitwise_and(jnp.right_shift(me, shift), members - 1)
+        swaps = [
+            send(spread.at[level, 0], spread.at[level + 1, d], level + 1, d,
+                 (jnp.bitwise_xor(me, d << shift), rep))
+            for d in range(1, members)
+        ]
+        for c in swaps:
+            c.start()
+        for c in swaps:
+            c.wait()
+        spread[level + 1, 0] = spread[level, 0]
+        total = spread[level + 1, jnp.bitwise_xor(mine, 0)]
+        for i in range(1, members):
+            total = total + spread[level + 1, jnp.bitwise_xor(mine, i)]
+        spread[level + 1, 0] = total
+
+    last = len(digits)
+    gathered[rep] = spread[last, 0]
+    spreads = [
+        send(spread.at[last, 0], gathered.at[rep], last + 1, j, (me, partner))
+        for j, partner in enumerate(rep_partners, start=1)
+    ]
+    for c in spreads:
+        c.start()
+    for c in spreads:
+        c.wait()
+    for r in range(group):
+        out_ref[pl.ds(r * piece, piece)] = gathered[r]
+
+
+def all_reduce_by_kernel(term):
+    group = lax.axis_size("rep")
+    bits = lax.axis_size("blk").bit_length() - 1
+    digits = [(shift, min(3, bits - shift)) for shift in range(0, bits, 3)]
+    piece = term.shape[0] // group
     return pl.pallas_call(
-        functools.partial(butterfly_kernel, levels),
+        functools.partial(reduce_kernel, group, digits),
         out_shape=jax.ShapeDtypeStruct(term.shape, term.dtype),
         in_specs=[pl.BlockSpec(memory_space=pltpu.VMEM)],
         out_specs=pl.BlockSpec(memory_space=pltpu.VMEM),
         scratch_shapes=[
-            pltpu.VMEM((levels,) + term.shape, term.dtype),
-            pltpu.SemaphoreType.DMA((levels,)),
-            pltpu.SemaphoreType.DMA((levels,)),
+            pltpu.VMEM((1, group, piece, term.shape[1]), term.dtype),
+            pltpu.VMEM((len(digits) + 1, 8, piece, term.shape[1]), term.dtype),
+            pltpu.VMEM((group, piece, term.shape[1]), term.dtype),
+            pltpu.SemaphoreType.DMA((2, len(digits) + 2, 8)),
         ],
         compiler_params=pltpu.CompilerParams(collective_id=1, has_side_effects=True),
     )(term)
-
-
-def scatter_sum(flat, axis):
-    size = lax.axis_size(axis)
-    pieces = lax.all_to_all(flat.reshape(size, -1), axis, 0, 0, tiled=False)
-    return pieces.sum(0)
-
-
-def gather_all(piece, axis):
-    size = lax.axis_size(axis)
-    copies = jnp.broadcast_to(piece[None], (size,) + piece.shape)
-    return lax.all_to_all(copies, axis, 0, 0, tiled=False).reshape(-1)
-
-
-def all_reduce_by_exchange(term):
-    flat = scatter_sum(term.reshape(-1), "rep")
-    width = term.shape[-1]
-    summed = butterfly_sum(flat.reshape(-1, width)).reshape(-1)
-    return gather_all(summed, "rep").reshape(term.shape)
 
 
 def unpack_blocks(words):
@@ -258,7 +293,7 @@
         features, aggregated, (((0,), (0,)), ((), ())), preferred_element_type=jnp.float32
     )
     node_total = slab_rows * blocks
-    weight_grad = all_reduce_by_exchange(weight_term) * (1.0 / math.sqrt(node_total))
+    weight_grad = all_reduce_by_kernel(weight_term) * (1.0 / math.sqrt(node_total))
     return (input_grad, weight_grad)
 
 

time: 203 us -> 187 us (0.921)
  blocking collectives: 10.1 us -> 0 us
  Pallas kernels: 89.9 us -> 97.2 us
  waiting for transfers between devices: 19.4 us -> 12.7 us
  starting transfers between devices: 57.4 us -> 54 us
  local copies, waits for them, and re-layouts: 10.8 us -> 7.41 us
    all_to_all x1 -> x0, blocking collectives: 10.1 us -> none  [scatter_sum(): pieces = lax.all_to_all(flat.reshape(size, -1), axis, 0, 0, tiled=False)]
    pallas_call x1, Pallas kernels: 34.4 us -> 41.7 us  [all_reduce_by_kernel(): pl.pallas_call(functools.partial(reduce_kernel, group, digits), out_shape...]
    all_to_all x1 -> x0, waiting for transfers between devices: 6.72 us -> none  [gather_all(): return lax.all_to_all(copies, axis, 0, 0, tiled=False).reshape(-1)]
    all_to_all x1 -> x0, starting transfers between devices: 3.41 us -> none  [gather_all(): return lax.all_to_all(copies, axis, 0, 0, tiled=False).reshape(-1)]
  transfers between devices with their start and end apart: 2 -> 1, of which waited for: 2 -> 1; matrix products, arithmetic and copies ran while one was open for 0% -> 0% of each run, Pallas kernels for 0% -> 0%
where the time goes in v6:
time: 187 us; the launch traced here: 185 us
  Pallas kernels  97.2 us (52%)
  starting transfers between devices  54 us (29%)
  waiting for transfers between devices  12.7 us (7%)
  matrix products  7.83 us (4%)
  local copies, waits for them, and re-layouts  7.41 us (4%)
  other arithmetic  5.15 us (3%)
    pallas_call x1, Pallas kernels, gather_sources(): pl.pallas_call(functools.partial(gather_kernel, steps, blocks, plans), ou...  55.6 us
    all_to_all x1, starting transfers between devices, per_device(): lax.all_to_all(partial_sums.reshape(group_size, share_rows, width), 'rep'...  54 us
    pallas_call x1, Pallas kernels, all_reduce_by_kernel(): pl.pallas_call(functools.partial(reduce_kernel, group, digits), out_shape...  41.7 us
    all_to_all x1, waiting for transfers between devices, per_device(): lax.all_to_all(partial_sums.reshape(group_size, share_rows, width), 'rep'...  12.7 us
    gather x2, local copies, waits for them, and re-layouts, per_device(): picked = jnp.take_along_axis(sources, coords[:, 0, :, None, None], axis=1)  5.11 us
  transfers between devices with their start and end apart: 1, of which 1 were waited for; matrix products, arithmetic and copies ran while one was open for 0% of the time, Pallas kernels for 0%

profile of v6, /device:TPU:1, one launch (start us, length us, event | category | flops | bytes accessed | tf_op | source)
XLA Modules:
  0.0 185.0 jit_solution(10154069023312969685)
XLA Ops:
  0.6 0.0 copy-start
  0.6 0.7 copy.27
  1.4 0.7 iota_compare_fusion.1
  2.1 0.7 convert_rsqrt_fusion
  2.8 0.1 reshape.104
  2.8 0.1 copy.16
  2.9 0.1 shift_right_arithmetic.26
  3.0 2.0 %multiply_convert_fusion.slab_ref = bf16[1024,256]{1,0:T(8,128)(2,1)} fusion(bf16[1024,256]{1,0:T(8,128)(2,1)} %param.8, f32[1024]{0:T(1024)S(1)} %convert_rsqrt_fusion), kind=kLoop, calls=%fused_computation.16 | loop fusion | flops 786432 | bytes 1052672 | tf_op jit(solution)/shard_map/convert_element_type | solution.py:262
  5.1 55.6 %shard_map.86 = bf16[8,1024,256]{2,1,0:T(8,128)(2,1)} custom-call(bf16[1024,256]{1,0:T(8,128)(2,1)} %multiply_convert_fusion.slab_ref), custom_call_target="tpu_custom_call" | custom-call | tf_op jit(solution)/shard_map/pallas_call | solution.py:137
  60.6 0.0 copy-start.2
  60.6 5.0 %gather_fusion = bf16[64,128,256]{2,1,0:T(8,128)(2,1)} fusion(bf16[8,8,128,256]{3,2,1,0:T(8,128)(2,1)} %bitcast.34, s32[64]{0:T(128)S(1)} %reshape.104), kind=kCustom, calls=%fused_computation | custom fusion | bytes 8389120 | tf_op jit(solution)/shard_map/jit(take_along_axis)/gather | solution.py:269
  65.7 0.0 copy-done.2
  65.7 3.5 %fusion.4 = bf16[8,8,128,256]{3,2,1,0:T(8,128)(2,1)S(1)} fusion(bf16[8,8,128,256]{3,2,1,0:T(8,128)(2,1)} %bitcast.35, pred[8,8]{1,0:T(8,128)(4,1)S(1)} %compare_and_fusion, s32[128]{0:T(128)S(1)} %shift_right_arithmetic.26, s32[8,8,16,128]{3,2,1,0:T(8,128)S(1)} %bitcast.39), kind=kOutput, calls=%fused_computation.6 | convolution fusion | flops 542113792 | bytes 8913472 | tf_op jit(solution)/shard_map/skvu,skuf->skvf/dot_general | solution.py:271
  69.2 2.5 %fusion.12 = f32[8,128,256]{2,0,1:T(8,128)S(1)} fusion(bf16[8,8,128,256]{3,2,1,0:T(8,128)(2,1)S(1)} %fusion.4, s32[8,8]{0,1:T(8,128)S(1)} %copy.16, pred[8,8]{0,1:T(8,128)(4,1)S(1)} %iota_compare_fusion.1), kind=kOutput, calls=%fused_computation.13 | convolution fusion | flops 33555456 | bytes 5243200 | tf_op jit(solution)/shard_map/skc,skvf->cvf/dot_general | solution.py:279
  71.7 0.0 copy-start.1
  71.7 1.3 copy.18
  73.0 54.0 %all-to-all-start = ((f32[8,128,256]{2,1,0:T(8,128)}), f32[8,128,256]{2,1,0:T(8,128)S(1)}, u32[]{:S(2)}, u32[]{:S(2)}) async-start(f32[8,128,256]{2,1,0:T(8,128)} %copy.18), calls=%async_computation | async-start | bytes 2097152 | tf_op jit(solution)/shard_map/all_to_all | solution.py:284
  127.0 0.1 dynamic_slice.3
  127.1 12.7 %all-to-all-done = f32[8,128,256]{2,1,0:T(8,128)S(1)} async-done(((f32[8,128,256]{2,1,0:T(8,128)}), f32[8,128,256]{2,1,0:T(8,128)S(1)}, u32[]{:S(2)}, u32[]{:S(2)}) %all-to-all-start) | async-done | bytes 1048608 | tf_op jit(solution)/shard_map/all_to_all | solution.py:284
  139.8 0.1 reduce_sum.9
  139.9 0.0 copy-done
  139.9 0.8 convolution_convert_fusion
  140.7 0.0 copy-done.1
  140.7 1.0 convolution_bitcast_fusion.term_ref
  141.7 41.7 %shard_map.87 = f32[256,256]{1,0:T(8,128)} custom-call(f32[256,256]{1,0:T(8,128)} %convolution_bitcast_fusion.term_ref), custom_call_target="tpu_custom_call" | custom-call | tf_op jit(solution)/shard_map/pallas_call | solution.py:231
  183.4 1.7 broadcast_multiply_fusion
  (4 shorter events, 0.0 us)
Async XLA Ops:
  0.6 139.3 %copy-start = (bf16[256,256]{1,0:T(8,128)(2,1)S(1)}, bf16[256,256]{1,0:T(8,128)(2,1)}, u32[]{:S(2)}) copy-start(bf16[256,256]{1,0:T(8,128)(2,1)} %param.9) | copy-start | bytes 393220
  60.6 5.0 %copy-start.2 = (s32[1,8,8,16,128]{4,3,2,1,0:T(8,128)S(1)}, s32[1,8,8,16,128]{4,3,2,1,0:T(8,128)}, u32[]{:S(2)}) copy-start(s32[1,8,8,16,128]{4,3,2,1,0:T(8,128)} %param.10) | copy-start | bytes 1572868
  71.7 69.0 %copy-start.1 = (bf16[128,256]{1,0:T(8,128)(2,1)S(1)}, bf16[128,256]{1,0:T(8,128)(2,1)}, u32[]{:S(2)}) copy-start(bf16[128,256]{1,0:T(8,128)(2,1)} %param.7) | copy-start | bytes 196612
  73.0 66.8 %all-to-all-start = ((f32[8,128,256]{2,1,0:T(8,128)}), f32[8,128,256]{2,1,0:T(8,128)S(1)}, u32[]{:S(2)}, u32[]{:S(2)}) async-start(f32[8,128,256]{2,1,0:T(8,128)} %copy.18), calls=%async_computation | async-start | bytes 2097152 | tf_op jit(solution)/shard_map/all_to_all | solution.py:284

commit v7 on v6

--- a/solution.py
+++ b/solution.py
@@ -150,10 +150,12 @@
     )(scaled)
 
 
-def reduce_kernel(group, digits, term_ref, out_ref, inbox, spread, gathered, sems):
+def finish_kernel(group, digits, partial_ref, root_ref, feat_t_ref, weight_t_ref, grad_ref, out_ref,
+                  sums_in, inbox, spread, gathered, sems):
     me = lax.axis_index("blk")
     rep = lax.axis_index("rep")
-    piece = term_ref.shape[0] // group
+    share = grad_ref.shape[0]
+    piece = out_ref.shape[0] // group
     rep_partners = [lax.rem(rep + j, group) for j in range(1, group)]
     barrier = pltpu.get_barrier_semaphore()
     for partner in rep_partners:
@@ -177,42 +179,61 @@
             device_id_type=MESH_ID,
         )
 
+    shares = []
+    for j, partner in enumerate(rep_partners, start=1):
+        rows = pl.ds(pl.multiple_of(partner * share, 8), share)
+        shares.append(send(partial_ref.at[rows], sums_in.at[j], 0, j, (me, partner)))
+    for c in shares:
+        c.start()
+    for c in shares:
+        c.wait()
+    own_rows = pl.ds(pl.multiple_of(rep * share, 8), share)
+    summed = partial_ref[own_rows]
+    for j in range(1, group):
+        summed = summed + sums_in[j]
+    aggregated = (summed * root_ref[...]).astype(jnp.bfloat16)
+    grad_ref[...] = jnp.dot(
+        aggregated, weight_t_ref[...], preferred_element_type=jnp.float32
+    ).astype(grad_ref.dtype)
+    term = jnp.dot(feat_t_ref[...], aggregated, preferred_element_type=jnp.float32)
+    spread[0, 0] = term
+
     scatter = []
     for j, partner in enumerate(rep_partners, start=1):
         rows = pl.ds(pl.multiple_of(partner * piece, 8), piece)
-        scatter.append(send(term_ref.at[rows], inbox.at[0, j], 0, j, (me, partner)))
+        scatter.append(send(spread.at[0, 0, rows], inbox.at[j], 1, j, (me, partner)))
     for c in scatter:
         c.start()
     for c in scatter:
         c.wait()
     own = pl.ds(pl.multiple_of(rep * piece, 8), piece)
-    total = term_ref[own]
+    total = spread[0, 0, own]
     for j in range(1, group):
-        total = total + inbox[0, j]
-    spread[0, 0] = total
-
-    for level, (shift, width) in enumerate(digits):
+        total = total + inbox[j]
+    spread[1, 0, pl.ds(0, piece)] = total
+
+    for level, (shift, width) in enumerate(digits, start=1):
         members = 1 << width
         mine = jnp.bitwise_and(jnp.right_shift(me, shift), members - 1)
         swaps = [
-            send(spread.at[level, 0], spread.at[level + 1, d], level + 1, d,
-                 (jnp.bitwise_xor(me, d << shift), rep))
+            send(spread.at[level, 0, pl.ds(0, piece)], spread.at[level + 1, d, pl.ds(0, piece)],
+                 level + 1, d, (jnp.bitwise_xor(me, d << shift), rep))
             for d in range(1, members)
         ]
         for c in swaps:
             c.start()
         for c in swaps:
             c.wait()
-        spread[level + 1, 0] = spread[level, 0]
-        total = spread[level + 1, jnp.bitwise_xor(mine, 0)]
+        spread[level + 1, 0, pl.ds(0, piece)] = spread[level, 0, pl.ds(0, piece)]
+        total = spread[level + 1, mine, pl.ds(0, piece)]
         for i in range(1, members):
-            total = total + spread[level + 1, jnp.bitwise_xor(mine, i)]
-        spread[level + 1, 0] = total
-
-    last = len(digits)
-    gathered[rep] = spread[last, 0]
+            total = total + spread[level + 1, jnp.bitwise_xor(mine, i), pl.ds(0, piece)]
+        spread[level + 1, 0, pl.ds(0, piece)] = total
+
+    last = len(digits) + 1
+    gathered[rep] = spread[last, 0, pl.ds(0, piece)]
     spreads = [
-        send(spread.at[last, 0], gathered.at[rep], last + 1, j, (me, partner))
+        send(spread.at[last, 0, pl.ds(0, piece)], gathered.at[rep], last + 1, j, (me, partner))
         for j, partner in enumerate(rep_partners, start=1)
     ]
     for c in spreads:
@@ -223,24 +244,32 @@
         out_ref[pl.ds(r * piece, piece)] = gathered[r]
 
 
-def all_reduce_by_kernel(term):
+def finish(partial_sums, share_root, features, weight):
     group = lax.axis_size("rep")
     bits = lax.axis_size("blk").bit_length() - 1
     digits = [(shift, min(3, bits - shift)) for shift in range(0, bits, 3)]
-    piece = term.shape[0] // group
+    slab_rows, width = partial_sums.shape
+    share = slab_rows // group
+    fan = weight.shape[1]
+    piece = fan // group
+    vmem = pl.BlockSpec(memory_space=pltpu.VMEM)
     return pl.pallas_call(
-        functools.partial(reduce_kernel, group, digits),
-        out_shape=jax.ShapeDtypeStruct(term.shape, term.dtype),
-        in_specs=[pl.BlockSpec(memory_space=pltpu.VMEM)],
-        out_specs=pl.BlockSpec(memory_space=pltpu.VMEM),
+        functools.partial(finish_kernel, group, digits),
+        out_shape=(
+            jax.ShapeDtypeStruct((share, weight.shape[0]), jnp.bfloat16),
+            jax.ShapeDtypeStruct((fan, width), jnp.float32),
+        ),
+        in_specs=[vmem] * 4,
+        out_specs=(vmem, vmem),
         scratch_shapes=[
-            pltpu.VMEM((1, group, piece, term.shape[1]), term.dtype),
-            pltpu.VMEM((len(digits) + 1, 8, piece, term.shape[1]), term.dtype),
-            pltpu.VMEM((group, piece, term.shape[1]), term.dtype),
-            pltpu.SemaphoreType.DMA((2, len(digits) + 2, 8)),
+            pltpu.VMEM((group, share, width), jnp.float32),
+            pltpu.VMEM((group, piece, width), jnp.float32),
+            pltpu.VMEM((len(digits) + 2, 8, fan, width), jnp.float32),
+            pltpu.VMEM((group, piece, width), jnp.float32),
+            pltpu.SemaphoreType.DMA((2, len(digits) + 3, 8)),
         ],
         compiler_params=pltpu.CompilerParams(collective_id=1, has_side_effects=True),
-    )(term)
+    )(partial_sums, share_root[:, None], features.T, weight.T)
 
 
 def unpack_blocks(words):
@@ -281,19 +310,9 @@
     partial_sums = accumulated.reshape(slab_rows, width)
     share_rows = slab_rows // group_size
     share_root = lax.dynamic_slice_in_dim(inverse_root, rep_index * share_rows, share_rows, 0)
-    exchanged = lax.all_to_all(
-        partial_sums.reshape(group_size, share_rows, width), "rep", 0, 0, tiled=False
-    )
-    own_sums = exchanged.sum(0)
-    aggregated = (own_sums * share_root[:, None]).astype(jnp.bfloat16)
-    input_grad = lax.dot_general(
-        aggregated, weight, (((1,), (1,)), ((), ())), preferred_element_type=jnp.float32
-    ).astype(jnp.bfloat16)
-    weight_term = lax.dot_general(
-        features, aggregated, (((0,), (0,)), ((), ())), preferred_element_type=jnp.float32
-    )
+    input_grad, weight_sum = finish(partial_sums, share_root, features, weight)
     node_total = slab_rows * blocks
-    weight_grad = all_reduce_by_kernel(weight_term) * (1.0 / math.sqrt(node_total))
+    weight_grad = weight_sum * (1.0 / math.sqrt(node_total))
     return (input_grad, weight_grad)
 
 

time: 187 us -> 189 us (1.011)
  Pallas kernels: 97.2 us -> 162 us
  starting transfers between devices: 54 us -> 0 us
  waiting for transfers between devices: 12.7 us -> 0 us
  local copies, waits for them, and re-layouts: 7.41 us -> 11.1 us
  matrix products: 7.83 us -> 10.2 us
    pallas_call x1, Pallas kernels: 41.7 us -> 106 us  [finish(): pl.pallas_call(functools.partial(finish_kernel, group, digits), out_shape...]
    all_to_all x1 -> x0, starting transfers between devices: 54 us -> none  [per_device(): lax.all_to_all(partial_sums.reshape(group_size, share_rows, width), 'rep'...]
    all_to_all x1 -> x0, waiting for transfers between devices: 12.7 us -> none  [per_device(): lax.all_to_all(partial_sums.reshape(group_size, share_rows, width), 'rep'...]
    unnamed x7 -> x12, local copies, waits for them, and re-layouts: 0.75 us -> 3.68 us
    dot_general x1, matrix products: 2.49 us -> 4.69 us  [per_device(): accumulated = jnp.einsum('skc,skvf->cvf', placement, contrib)]
    dot_general x1, matrix products: 3.55 us -> 5.49 us  [per_device(): jnp.einsum('skvu,skuf->skvf', transposed, picked, preferred_element_type=...]
  transfers between devices with their start and end apart: 1 -> 0, of which waited for: 1 -> 0; matrix products, arithmetic and copies ran while one was open for 0% -> 0% of each run, Pallas kernels for 0% -> 0%
where the time goes in v7:
time: 189 us; the launch traced here: 188 us
  Pallas kernels  162 us (86%)
  local copies, waits for them, and re-layouts  11.1 us (6%)
  matrix products  10.2 us (5%)
  other arithmetic  4.46 us (2%)
    pallas_call x1, Pallas kernels, finish(): pl.pallas_call(functools.partial(finish_kernel, group, digits), out_shape...  106 us
    pallas_call x1, Pallas kernels, gather_sources(): pl.pallas_call(functools.partial(gather_kernel, steps, blocks, plans), ou...  55.6 us
    dot_general x1, matrix products, per_device(): jnp.einsum('skvu,skuf->skvf', transposed, picked, preferred_element_type=...  5.49 us
    gather x2, local copies, waits for them, and re-layouts, per_device(): picked = jnp.take_along_axis(sources, coords[:, 0, :, None, None], axis=1)  5.11 us
    dot_general x1, matrix products, per_device(): accumulated = jnp.einsum('skc,skvf->cvf', placement, contrib)  4.69 us

profile of v7, /device:TPU:1, one launch (start us, length us, event | category | flops | bytes accessed | tf_op | source)
XLA Modules:
  0.0 188.2 jit_solution(11426964728266909324)
XLA Ops:
  0.6 0.7 copy.28
  1.3 0.1 reshape.107
  1.4 0.7 convert_rsqrt_fusion
  2.1 2.1 %multiply_convert_fusion.slab_ref = bf16[1024,256]{1,0:T(8,128)(2,1)} fusion(bf16[1024,256]{1,0:T(8,128)(2,1)} %param.8, f32[1024]{0:T(1024)S(1)} %convert_rsqrt_fusion), kind=kLoop, calls=%fused_computation.14 | loop fusion | flops 786432 | bytes 1052672 | tf_op jit(solution)/shard_map/convert_element_type | solution.py:291
  4.2 55.6 %shard_map.86 = bf16[8,1024,256]{2,1,0:T(8,128)(2,1)} custom-call(bf16[1024,256]{1,0:T(8,128)(2,1)} %multiply_convert_fusion.slab_ref), custom_call_target="tpu_custom_call" | custom-call | tf_op jit(solution)/shard_map/pallas_call | solution.py:137
  59.7 0.0 copy-start.2
  59.8 5.0 %gather_fusion = bf16[64,128,256]{2,1,0:T(8,128)(2,1)} fusion(bf16[8,8,128,256]{3,2,1,0:T(8,128)(2,1)} %bitcast.35, s32[64]{0:T(128)S(1)} %reshape.107), kind=kCustom, calls=%fused_computation | custom fusion | bytes 8389120 | tf_op jit(solution)/shard_map/jit(take_along_axis)/gather | solution.py:298
  64.8 0.1 shift_right_arithmetic.26
  64.9 0.0 copy-done.2
  64.9 0.0 copy-start.3
  64.9 5.5 %fusion.4 = bf16[8,8,128,256]{3,2,1,0:T(8,128)(2,1)} fusion(bf16[8,8,128,256]{3,2,1,0:T(8,128)(2,1)} %bitcast.37, pred[8,8]{1,0:T(8,128)(4,1)S(1)} %compare_and_fusion, s32[128]{0:T(128)S(1)} %shift_right_arithmetic.26, s32[8,8,16,128]{3,2,1,0:T(8,128)S(1)} %bitcast.43), kind=kOutput, calls=%fused_computation.6 | convolution fusion | flops 542113792 | bytes 8913472 | tf_op jit(solution)/shard_map/skvu,skuf->skvf/dot_general | solution.py:300
  70.4 0.0 copy-start
  70.4 0.0 copy-start.1
  70.4 0.1 copy.16
  70.5 0.0 copy-done.3
  70.5 4.7 %fusion.12 = f32[8,128,256]{2,0,1:T(8,128)S(1)} fusion(bf16[8,8,128,256]{3,2,1,0:T(8,128)(2,1)} %fusion.4, s32[8,8]{0,1:T(8,128)S(1)} %copy.16, pred[8,8]{0,1:T(8,128)(4,1)S(1)} %iota_compare_fusion.1), kind=kOutput, calls=%fused_computation.13 | convolution fusion | flops 33555456 | bytes 5243200 | tf_op jit(solution)/shard_map/skc,skvf->cvf/dot_general | solution.py:308
  75.2 1.3 copy.17
  76.5 0.1 dynamic-slice_bitcast_fusion
  76.5 0.7 copy.20.root_ref
  77.3 0.0 copy-done
  77.3 0.8 copy.19
  78.0 0.0 copy-done.1
  78.0 0.7 copy.18
  78.8 106.3 %shard_map.87 = (bf16[128,256]{1,0:T(8,128)(2,1)}, f32[256,256]{1,0:T(8,128)}) custom-call(f32[1024,256]{1,0:T(8,128)} %bitcast.36, f32[128,1]{1,0:T(8,128)} %copy.20.root_ref, bf16[256,128]{1,0:T(8,128)(2,1)} %bitcast.39, bf16[256,256]{1,0:T(8,128)(2,1)} %bitcast.38), custom_call_target="tpu_custom_call" | custom-call | tf_op jit(solution)/shard_map/pallas_call | solution.py:256
  185.0 1.7 broadcast_multiply_fusion
  186.7 1.5 copy.30
  (5 shorter events, 0.0 us)
Async XLA Ops:
  59.7 5.1 %copy-start.2 = (s32[1,8,8,16,128]{4,3,2,1,0:T(8,128)S(1)}, s32[1,8,8,16,128]{4,3,2,1,0:T(8,128)}, u32[]{:S(2)}) copy-start(s32[1,8,8,16,128]{4,3,2,1,0:T(8,128)} %param.10) | copy-start | bytes 1572868
  64.9 5.6 %copy-start.3 = (s32[1,8]{1,0:T(1,128)S(1)}, s32[1,8]{1,0:T(1,128)}, u32[]{:S(2)}) copy-start(s32[1,8]{1,0:T(1,128)} %param.12) | copy-start | bytes 100
  70.4 6.9 %copy-start = (bf16[256,256]{1,0:T(8,128)(2,1)S(1)}, bf16[256,256]{1,0:T(8,128)(2,1)}, u32[]{:S(2)}) copy-start(bf16[256,256]{1,0:T(8,128)(2,1)} %param.9) | copy-start | bytes 393220
  70.4 7.7 %copy-start.1 = (bf16[128,256]{1,0:T(8,128)(2,1)S(1)}, bf16[128,256]{1,0:T(8,128)(2,1)}, u32[]{:S(2)}) copy-start(bf16[128,256]{1,0:T(8,128)(2,1)} %param.7) | copy-start | bytes 196612

commit v8 on v7

--- a/solution.py
+++ b/solution.py
@@ -8,7 +8,7 @@
 from jax.experimental.pallas import tpu as pltpu
 from jax.sharding import PartitionSpec as P
 
-CHUNKS = 8
+CHUNKS = 16
 MESH_ID = pl.DeviceIdType.MESH
 
 
@@ -17,7 +17,7 @@
     for rep in range(group):
         reach = steps * rep + steps // 2
         short = min(reach, blocks - reach)
-        if 4 * short < 5 * blocks // 4:
+        if 16 * short < 3 * blocks:
             plans.append((CHUNKS, 0, 0))
             continue
         direct = min(CHUNKS, max(1, int(CHUNKS * (blocks - short) / blocks + 0.5)))
@@ -188,9 +188,9 @@
     for c in shares:
         c.wait()
     own_rows = pl.ds(pl.multiple_of(rep * share, 8), share)
-    summed = partial_ref[own_rows]
+    summed = partial_ref[own_rows].astype(jnp.float32)
     for j in range(1, group):
-        summed = summed + sums_in[j]
+        summed = summed + sums_in[j].astype(jnp.float32)
     aggregated = (summed * root_ref[...]).astype(jnp.bfloat16)
     grad_ref[...] = jnp.dot(
         aggregated, weight_t_ref[...], preferred_element_type=jnp.float32
@@ -262,7 +262,7 @@
         in_specs=[vmem] * 4,
         out_specs=(vmem, vmem),
         scratch_shapes=[
-            pltpu.VMEM((group, share, width), jnp.float32),
+            pltpu.VMEM((group, share, width), partial_sums.dtype),
             pltpu.VMEM((group, piece, width), jnp.float32),
             pltpu.VMEM((len(digits) + 2, 8, fan, width), jnp.float32),
             pltpu.VMEM((group, piece, width), jnp.float32),
@@ -310,7 +310,7 @@
     partial_sums = accumulated.reshape(slab_rows, width)
     share_rows = slab_rows // group_size
     share_root = lax.dynamic_slice_in_dim(inverse_root, rep_index * share_rows, share_rows, 0)
-    input_grad, weight_sum = finish(partial_sums, share_root, features, weight)
+    input_grad, weight_sum = finish(partial_sums.astype(jnp.bfloat16), share_root, features, weight)
     node_total = slab_rows * blocks
     weight_grad = weight_sum * (1.0 / math.sqrt(node_total))
     return (input_grad, weight_grad)

time: 189 us -> 181 us (0.958)
  Pallas kernels: 162 us -> 154 us
    pallas_call x1, Pallas kernels: 106 us -> 97.6 us  [finish(): pl.pallas_call(functools.partial(finish_kernel, group, digits), out_shape...]
where the time goes in v8:
time: 181 us; the launch traced here: 180 us
  Pallas kernels  154 us (85%)
  local copies, waits for them, and re-layouts  10.7 us (6%)
  matrix products  10.2 us (6%)
  other arithmetic  4.46 us (2%)
    pallas_call x1, Pallas kernels, finish(): pl.pallas_call(functools.partial(finish_kernel, group, digits), out_shape...  97.6 us
    pallas_call x1, Pallas kernels, gather_sources(): pl.pallas_call(functools.partial(gather_kernel, steps, blocks, plans), ou...  56.6 us
    dot_general x1, matrix products, per_device(): jnp.einsum('skvu,skuf->skvf', transposed, picked, preferred_element_type=...  5.49 us
    gather x2, local copies, waits for them, and re-layouts, per_device(): picked = jnp.take_along_axis(sources, coords[:, 0, :, None, None], axis=1)  5.11 us
    dot_general x1, matrix products, per_device(): accumulated = jnp.einsum('skc,skvf->cvf', placement, contrib)  4.68 us
    unnamed x12, local copies, waits for them, and re-layouts  3.68 us

profile of v8, /device:TPU:1, one launch (start us, length us, event | category | flops | bytes accessed | tf_op | source)
XLA Modules:
  0.0 180.2 jit_solution(6666474076586439962)
XLA Ops:
  0.6 0.7 copy.30
  1.3 0.1 reshape.105
  1.4 0.7 convert_rsqrt_fusion
  2.1 2.1 %multiply_convert_fusion.slab_ref = bf16[1024,256]{1,0:T(8,128)(2,1)} fusion(bf16[1024,256]{1,0:T(8,128)(2,1)} %param.8, f32[1024]{0:T(1024)S(1)} %convert_rsqrt_fusion), kind=kLoop, calls=%fused_computation.15 | loop fusion | flops 786432 | bytes 1052672 | tf_op jit(solution)/shard_map/convert_element_type | solution.py:291
  4.2 56.6 %shard_map.86 = bf16[8,1024,256]{2,1,0:T(8,128)(2,1)} custom-call(bf16[1024,256]{1,0:T(8,128)(2,1)} %multiply_convert_fusion.slab_ref), custom_call_target="tpu_custom_call" | custom-call | tf_op jit(solution)/shard_map/pallas_call | solution.py:137
  60.8 0.0 copy-start.2
  60.8 5.0 %gather_fusion = bf16[64,128,256]{2,1,0:T(8,128)(2,1)} fusion(bf16[8,8,128,256]{3,2,1,0:T(8,128)(2,1)} %bitcast.37, s32[64]{0:T(128)S(1)} %reshape.105), kind=kCustom, calls=%fused_computation | custom fusion | bytes 8389120 | tf_op jit(solution)/shard_map/jit(take_along_axis)/gather | solution.py:298
  65.9 0.1 shift_right_arithmetic.26
  66.0 0.0 copy-done.2
  66.0 0.0 copy-start.3
  66.0 5.5 %fusion.4 = bf16[8,8,128,256]{3,2,1,0:T(8,128)(2,1)} fusion(bf16[8,8,128,256]{3,2,1,0:T(8,128)(2,1)} %bitcast.38, pred[8,8]{1,0:T(8,128)(4,1)S(1)} %compare_and_fusion, s32[128]{0:T(128)S(1)} %shift_right_arithmetic.26, s32[8,8,16,128]{3,2,1,0:T(8,128)S(1)} %bitcast.45), kind=kOutput, calls=%fused_computation.6 | convolution fusion | flops 542113792 | bytes 8913472 | tf_op jit(solution)/shard_map/skvu,skuf->skvf/dot_general | solution.py:300
  71.5 0.0 copy-start
  71.5 0.0 copy-start.1
  71.5 0.1 copy.16
  71.6 0.0 copy-done.3
  71.6 4.7 %fusion.15 = bf16[8,128,256]{2,0,1:T(8,128)(2,1)S(1)} fusion(bf16[8,8,128,256]{3,2,1,0:T(8,128)(2,1)} %fusion.4, s32[8,8]{0,1:T(8,128)S(1)} %copy.16, pred[8,8]{0,1:T(8,128)(4,1)S(1)} %iota_compare_fusion.1), kind=kOutput, calls=%fused_computation.14 | convolution fusion | flops 33555456 | bytes 4718912 | tf_op jit(solution)/shard_map/skc,skvf->cvf/dot_general | solution.py:308
  76.3 0.9 copy.17
  77.2 0.1 dynamic-slice_bitcast_fusion
  77.2 0.7 copy.20.root_ref
  78.0 0.0 copy-done
  78.0 0.8 copy.19
  78.7 0.0 copy-done.1
  78.7 0.7 copy.18
  79.5 97.6 %shard_map.87 = (bf16[128,256]{1,0:T(8,128)(2,1)}, f32[256,256]{1,0:T(8,128)}) custom-call(bf16[1024,256]{1,0:T(8,128)(2,1)} %bitcast.39, f32[128,1]{1,0:T(8,128)} %copy.20.root_ref, bf16[256,128]{1,0:T(8,128)(2,1)} %bitcast.41, bf16[256,256]{1,0:T(8,128)(2,1)} %bitcast.40), custom_call_target="tpu_custom_call" | custom-call | tf_op jit(solution)/shard_map/pallas_call | solution.py:256
  177.1 1.7 broadcast_multiply_fusion
  178.8 1.5 copy.32
  (5 shorter events, 0.0 us)
Async XLA Ops:
  60.8 5.1 %copy-start.2 = (s32[1,8,8,16,128]{4,3,2,1,0:T(8,128)S(1)}, s32[1,8,8,16,128]{4,3,2,1,0:T(8,128)}, u32[]{:S(2)}) copy-start(s32[1,8,8,16,128]{4,3,2,1,0:T(8,128)} %param.10) | copy-start | bytes 1572868
  66.0 5.6 %copy-start.3 = (s32[1,8]{1,0:T(1,128)S(1)}, s32[1,8]{1,0:T(1,128)}, u32[]{:S(2)}) copy-start(s32[1,8]{1,0:T(1,128)} %param.12) | copy-start | bytes 100
  71.5 6.5 %copy-start = (bf16[256,256]{1,0:T(8,128)(2,1)S(1)}, bf16[256,256]{1,0:T(8,128)(2,1)}, u32[]{:S(2)}) copy-start(bf16[256,256]{1,0:T(8,128)(2,1)} %param.9) | copy-start | bytes 393220
  71.5 7.3 %copy-start.1 = (bf16[128,256]{1,0:T(8,128)(2,1)S(1)}, bf16[128,256]{1,0:T(8,128)(2,1)}, u32[]{:S(2)}) copy-start(bf16[128,256]{1,0:T(8,128)(2,1)} %param.7) | copy-start | bytes 196612

commit v9 on v8

--- a/solution.py
+++ b/solution.py
@@ -26,8 +26,8 @@
     return plans
 
 
-def gather_kernel(steps, blocks, plans, slab_ref, out_ref, relay_buf, send_sem, recv_sem,
-                  relay_in_sem, relay_fwd_sem):
+def gather_kernel(steps, blocks, plans, group, slab_ref, feat_ref, out_ref, feats_ref, relay_buf,
+                  send_sem, recv_sem, relay_in_sem, relay_fwd_sem, feat_sem):
     me = lax.axis_index("blk")
     rep = lax.axis_index("rep")
     rows = slab_ref.shape[0] // CHUNKS
@@ -72,9 +72,25 @@
             device_id_type=MESH_ID,
         )
 
+    rep_partners = [lax.rem(rep + j, group) for j in range(1, group)]
+
+    def feat_copy(j, partner):
+        return pltpu.make_async_remote_copy(
+            src_ref=feat_ref,
+            dst_ref=feats_ref.at[rep],
+            send_sem=feat_sem.at[0, j],
+            recv_sem=feat_sem.at[1, j],
+            device_id=(me, partner),
+            device_id_type=MESH_ID,
+        )
+
     barrier = pltpu.get_barrier_semaphore()
     for partner in (left, right, far_to, far_from):
         pl.semaphore_signal(barrier, inc=1, device_id=(partner, rep), device_id_type=MESH_ID)
+    for partner in rep_partners:
+        pl.semaphore_signal(barrier, inc=1, device_id=(me, partner), device_id_type=MESH_ID)
+    own_feat = pltpu.make_async_copy(feat_ref, feats_ref.at[rep], feat_sem.at[0, 0])
+    own_feat.start()
 
     for plane, (direct, sign, leg) in enumerate(plans):
         @pl.when(rep == plane)
@@ -84,18 +100,22 @@
                 behind = lax.rem(me - sign * leg + blocks, blocks)
                 for partner in (ahead, behind):
                     pl.semaphore_signal(barrier, inc=1, device_id=(partner, rep), device_id_type=MESH_ID)
-                pl.semaphore_wait(barrier, 6)
+                pl.semaphore_wait(barrier, 6 + group - 1)
                 for c in range(direct):
                     copy(None, centre, c, far_to).start()
+                for j, partner in enumerate(rep_partners, start=1):
+                    feat_copy(j, partner).start()
                 for c in range(direct, CHUNKS):
                     relay_out(c, ahead).start()
                 for c in range(direct, CHUNKS):
                     relay_out(c, ahead).wait_recv()
                     relay_on(c, ahead).start()
             else:
-                pl.semaphore_wait(barrier, 4)
+                pl.semaphore_wait(barrier, 4 + group - 1)
                 for c in range(CHUNKS):
                     copy(None, centre, c, far_to).start()
+                for j, partner in enumerate(rep_partners, start=1):
+                    feat_copy(j, partner).start()
 
     sent = []
     for k in range(1, centre + 1):
@@ -129,28 +149,35 @@
                 relay_on(c, ahead).wait_send()
     for forward in sent:
         forward.wait_send()
-
-
-def gather_sources(scaled, steps, blocks, group):
+    own_feat.wait()
+    for j, partner in enumerate(rep_partners, start=1):
+        feat_copy(j, partner).wait()
+
+
+def gather_sources(scaled, features, steps, blocks, group):
     slab_rows, width = scaled.shape
     plans = relay_plan(steps, blocks, group)
     return pl.pallas_call(
-        functools.partial(gather_kernel, steps, blocks, plans),
-        out_shape=jax.ShapeDtypeStruct((steps, slab_rows, width), scaled.dtype),
-        in_specs=[pl.BlockSpec(memory_space=pl.ANY)],
-        out_specs=pl.BlockSpec(memory_space=pl.ANY),
+        functools.partial(gather_kernel, steps, blocks, plans, group),
+        out_shape=(
+            jax.ShapeDtypeStruct((steps, slab_rows, width), scaled.dtype),
+            jax.ShapeDtypeStruct((group,) + features.shape, features.dtype),
+        ),
+        in_specs=[pl.BlockSpec(memory_space=pl.ANY)] * 2,
+        out_specs=(pl.BlockSpec(memory_space=pl.ANY), pl.BlockSpec(memory_space=pl.ANY)),
         scratch_shapes=[
             pltpu.VMEM((CHUNKS, slab_rows // CHUNKS, width), scaled.dtype),
             pltpu.SemaphoreType.DMA((steps, CHUNKS)),
             pltpu.SemaphoreType.DMA((steps, CHUNKS)),
             pltpu.SemaphoreType.DMA((CHUNKS,)),
             pltpu.SemaphoreType.DMA((CHUNKS,)),
+            pltpu.SemaphoreType.DMA((2, group)),
         ],
         compiler_params=pltpu.CompilerParams(collective_id=0, has_side_effects=True),
-    )(scaled)
-
-
-def finish_kernel(group, digits, partial_ref, root_ref, feat_t_ref, weight_t_ref, grad_ref, out_ref,
+    )(scaled, features)
+
+
+def finish_kernel(group, digits, partial_ref, root_ref, term_ref, weight_t_ref, grad_ref, out_ref,
                   sums_in, inbox, spread, gathered, sems):
     me = lax.axis_index("blk")
     rep = lax.axis_index("rep")
@@ -179,13 +206,15 @@
             device_id_type=MESH_ID,
         )
 
-    shares = []
+    first = []
     for j, partner in enumerate(rep_partners, start=1):
         rows = pl.ds(pl.multiple_of(partner * share, 8), share)
-        shares.append(send(partial_ref.at[rows], sums_in.at[j], 0, j, (me, partner)))
-    for c in shares:
+        first.append(send(partial_ref.at[rows], sums_in.at[j], 0, j, (me, partner)))
+        rows = pl.ds(pl.multiple_of(partner * piece, 8), piece)
+        first.append(send(term_ref.at[rows], inbox.at[j], 1, j, (me, partner)))
+    for c in first:
         c.start()
-    for c in shares:
+    for c in first:
         c.wait()
     own_rows = pl.ds(pl.multiple_of(rep * share, 8), share)
     summed = partial_ref[own_rows].astype(jnp.float32)
@@ -195,45 +224,34 @@
     grad_ref[...] = jnp.dot(
         aggregated, weight_t_ref[...], preferred_element_type=jnp.float32
     ).astype(grad_ref.dtype)
-    term = jnp.dot(feat_t_ref[...], aggregated, preferred_element_type=jnp.float32)
-    spread[0, 0] = term
-
-    scatter = []
-    for j, partner in enumerate(rep_partners, start=1):
-        rows = pl.ds(pl.multiple_of(partner * piece, 8), piece)
-        scatter.append(send(spread.at[0, 0, rows], inbox.at[j], 1, j, (me, partner)))
-    for c in scatter:
-        c.start()
-    for c in scatter:
-        c.wait()
     own = pl.ds(pl.multiple_of(rep * piece, 8), piece)
-    total = spread[0, 0, own]
+    total = term_ref[own]
     for j in range(1, group):
         total = total + inbox[j]
-    spread[1, 0, pl.ds(0, piece)] = total
+    spread[1, 0] = total
 
     for level, (shift, width) in enumerate(digits, start=1):
         members = 1 << width
         mine = jnp.bitwise_and(jnp.right_shift(me, shift), members - 1)
         swaps = [
-            send(spread.at[level, 0, pl.ds(0, piece)], spread.at[level + 1, d, pl.ds(0, piece)],
-                 level + 1, d, (jnp.bitwise_xor(me, d << shift), rep))
+            send(spread.at[level, 0], spread.at[level + 1, d], level + 1, d,
+                 (jnp.bitwise_xor(me, d << shift), rep))
             for d in range(1, members)
         ]
         for c in swaps:
             c.start()
         for c in swaps:
             c.wait()
-        spread[level + 1, 0, pl.ds(0, piece)] = spread[level, 0, pl.ds(0, piece)]
-        total = spread[level + 1, mine, pl.ds(0, piece)]
+        spread[level + 1, 0] = spread[level, 0]
+        total = spread[level + 1, mine]
         for i in range(1, members):
-            total = total + spread[level + 1, jnp.bitwise_xor(mine, i), pl.ds(0, piece)]
-        spread[level + 1, 0, pl.ds(0, piece)] = total
+            total = total + spread[level + 1, jnp.bitwise_xor(mine, i)]
+        spread[level + 1, 0] = total
 
     last = len(digits) + 1
-    gathered[rep] = spread[last, 0, pl.ds(0, piece)]
+    gathered[rep] = spread[last, 0]
     spreads = [
-        send(spread.at[last, 0, pl.ds(0, piece)], gathered.at[rep], last + 1, j, (me, partner))
+        send(spread.at[last, 0], gathered.at[rep], last + 1, j, (me, partner))
         for j, partner in enumerate(rep_partners, start=1)
     ]
     for c in spreads:
@@ -244,32 +262,32 @@
         out_ref[pl.ds(r * piece, piece)] = gathered[r]
 
 
-def finish(partial_sums, share_root, features, weight):
+def finish(partial_sums, share_root, term, weight):
     group = lax.axis_size("rep")
     bits = lax.axis_size("blk").bit_length() - 1
     digits = [(shift, min(3, bits - shift)) for shift in range(0, bits, 3)]
     slab_rows, width = partial_sums.shape
     share = slab_rows // group
-    fan = weight.shape[1]
+    fan = term.shape[0]
     piece = fan // group
     vmem = pl.BlockSpec(memory_space=pltpu.VMEM)
     return pl.pallas_call(
         functools.partial(finish_kernel, group, digits),
         out_shape=(
             jax.ShapeDtypeStruct((share, weight.shape[0]), jnp.bfloat16),
-            jax.ShapeDtypeStruct((fan, width), jnp.float32),
+            jax.ShapeDtypeStruct(term.shape, jnp.float32),
         ),
         in_specs=[vmem] * 4,
         out_specs=(vmem, vmem),
         scratch_shapes=[
             pltpu.VMEM((group, share, width), partial_sums.dtype),
-            pltpu.VMEM((group, piece, width), jnp.float32),
-            pltpu.VMEM((len(digits) + 2, 8, fan, width), jnp.float32),
-            pltpu.VMEM((group, piece, width), jnp.float32),
+            pltpu.VMEM((group, piece, term.shape[1]), jnp.float32),
+            pltpu.VMEM((len(digits) + 2, 8, piece, term.shape[1]), jnp.float32),
+            pltpu.VMEM((group, piece, term.shape[1]), jnp.float32),
             pltpu.SemaphoreType.DMA((2, len(digits) + 3, 8)),
         ],
         compiler_params=pltpu.CompilerParams(collective_id=1, has_side_effects=True),
-    )(partial_sums, share_root[:, None], features.T, weight.T)
+    )(partial_sums, share_root[:, None], term, weight.T)
 
 
 def unpack_blocks(words):
@@ -290,9 +308,8 @@
     inverse_root = lax.rsqrt(degrees.astype(jnp.float32))
     scaled = (out_grad.astype(jnp.float32) * inverse_root[:, None]).astype(jnp.bfloat16)
 
-    sources = gather_sources(scaled, step_count, blocks, group_size).reshape(
-        step_count, row_blocks, 128, width
-    )
+    sources, feature_slab = gather_sources(scaled, features, step_count, blocks, group_size)
+    sources = sources.reshape(step_count, row_blocks, 128, width)
     coords = block_coords[0]
     slot_total = coords.shape[-1]
     picked = jnp.take_along_axis(sources, coords[:, 0, :, None, None], axis=1)
@@ -310,7 +327,12 @@
     partial_sums = accumulated.reshape(slab_rows, width)
     share_rows = slab_rows // group_size
     share_root = lax.dynamic_slice_in_dim(inverse_root, rep_index * share_rows, share_rows, 0)
-    input_grad, weight_sum = finish(partial_sums.astype(jnp.bfloat16), share_root, features, weight)
+    scaled_sums = (partial_sums * inverse_root[:, None]).astype(jnp.bfloat16)
+    term = lax.dot_general(
+        feature_slab.reshape(slab_rows, -1), scaled_sums, (((0,), (0,)), ((), ())),
+        preferred_element_type=jnp.float32,
+    )
+    input_grad, weight_sum = finish(partial_sums.astype(jnp.bfloat16), share_root, term, weight)
     node_total = slab_rows * blocks
     weight_grad = weight_sum * (1.0 / math.sqrt(node_total))
     return (input_grad, weight_grad)

time: 181 us -> 178 us (0.983)
  Pallas kernels: 154 us -> 152 us
    pallas_call x1, Pallas kernels: 97.6 us -> 90.2 us  [finish(): pl.pallas_call(functools.partial(finish_kernel, group, digits), out_shape...]
    pallas_call x1, Pallas kernels: 56.6 us -> 61.3 us  [gather_sources(): pl.pallas_call(functools.partial(gather_kernel, steps, blocks, plans, gro...]
    unnamed x12 -> x11, local copies, waits for them, and re-layouts: 3.68 us -> 2.96 us
where the time goes in v9:
time: 178 us
  Pallas kernels  152 us (85%)
  matrix products  11.3 us (6%)
  local copies, waits for them, and re-layouts  10.1 us (6%)
  other arithmetic  4.44 us (2%)
    pallas_call x1, Pallas kernels, finish(): pl.pallas_call(functools.partial(finish_kernel, group, digits), out_shape...  90.2 us
    pallas_call x1, Pallas kernels, gather_sources(): pl.pallas_call(functools.partial(gather_kernel, steps, blocks, plans, gro...  61.3 us
    dot_general x1, matrix products, per_device(): jnp.einsum('skvu,skuf->skvf', transposed, picked, preferred_element_type=...  5.46 us
    gather x2, local copies, waits for them, and re-layouts, per_device(): picked = jnp.take_along_axis(sources, coords[:, 0, :, None, None], axis=1)  5.13 us
    dot_general x1, matrix products, per_device(): accumulated = jnp.einsum('skc,skvf->cvf', placement, contrib)  4.75 us

profile of v9, /device:TPU:1, one launch (start us, length us, event | category | flops | bytes accessed | tf_op | source)
XLA Modules:
  0.0 178.0 jit_solution(12969261500616983951)
XLA Ops:
  0.6 0.7 fusion.26
  1.3 2.0 %multiply_convert_fusion.1.slab_ref = bf16[1024,256]{1,0:T(8,128)(2,1)} fusion(bf16[1024,256]{1,0:T(8,128)(2,1)} %param.8, f32[1024]{0:T(1024)S(1)} %get-tuple-element.13), kind=kLoop, calls=%fused_computation.16 | loop fusion | flops 786432 | bytes 1052672 | tf_op jit(solution)/shard_map/convert_element_type | solution.py:309
  3.4 61.3 %shard_map.86 = (bf16[8,1024,256]{2,1,0:T(8,128)(2,1)}, bf16[8,128,256]{2,1,0:T(8,128)(2,1)}) custom-call(bf16[1024,256]{1,0:T(8,128)(2,1)} %multiply_convert_fusion.1.slab_ref, bf16[128,256]{1,0:T(8,128)(2,1)} %feat_ref.1), custom_call_target="tpu_custom_call" | custom-call | tf_op jit(solution)/shard_map/pallas_call | solution.py:160
  64.7 0.7 copy.36
  65.4 0.1 reshape.111
  65.5 0.0 copy-start.1
  65.5 5.0 %gather_fusion = bf16[64,128,256]{2,1,0:T(8,128)(2,1)} fusion(bf16[8,8,128,256]{3,2,1,0:T(8,128)(2,1)} %bitcast.41, s32[64]{0:T(128)S(1)} %reshape.111), kind=kCustom, calls=%fused_computation | custom fusion | bytes 8389120 | tf_op jit(solution)/shard_map/jit(take_along_axis)/gather | solution.py:315
  70.5 0.1 shift_right_arithmetic.26
  70.6 0.0 copy-done.1
  70.6 0.0 copy-start.3
  70.6 5.5 %fusion.4 = bf16[8,8,128,256]{3,2,1,0:T(8,128)(2,1)} fusion(bf16[8,8,128,256]{3,2,1,0:T(8,128)(2,1)} %bitcast.42, pred[8,8]{1,0:T(8,128)(4,1)S(1)} %compare_and_fusion, s32[128]{0:T(128)S(1)} %shift_right_arithmetic.26, s32[8,8,16,128]{3,2,1,0:T(8,128)S(1)} %bitcast.48), kind=kOutput, calls=%fused_computation.6 | convolution fusion | flops 542113792 | bytes 8913472 | tf_op jit(solution)/shard_map/skvu,skuf->skvf/dot_general | solution.py:317
  76.1 0.0 copy-start.2
  76.1 0.1 copy.17
  76.2 0.1 copy.19
  76.3 0.0 copy-done.3
  76.3 0.0 copy-start
  76.3 4.8 %multiply_convert_fusion = (bf16[8,128,256]{2,0,1:T(8,128)(2,1)S(1)}, bf16[8,128,256]{2,0,1:T(8,128)(2,1)S(1)}) fusion(f32[8,128]{0,1:T(8,128)S(1)} %copy.19, bf16[8,8,128,256]{3,2,1,0:T(8,128)(2,1)} %fusion.4, s32[8,8]{0,1:T(8,128)S(1)} %copy.17, pred[8,8]{0,1:T(8,128)(4,1)S(1)} %iota_compare_fusion.1), kind=kOutput, calls=%fused_computation.15 | convolution fusion | flops 34341888 | bytes 5247296 | tf_op jit(solution)/shard_map/skc,skvf->cvf/dot_general | solution.py:325
  81.1 0.0 copy-done.2
  81.1 1.1 convolution_bitcast_fusion.term_ref
  82.1 0.9 copy.18
  83.0 0.1 dynamic-slice_bitcast_fusion
  83.1 0.7 copy.23.root_ref
  83.8 0.0 copy-done
  83.8 0.8 copy.22
  84.6 90.2 %shard_map.87 = (bf16[128,256]{1,0:T(8,128)(2,1)}, f32[256,256]{1,0:T(8,128)}) custom-call(bf16[1024,256]{1,0:T(8,128)(2,1)} %bitcast.43, f32[128,1]{1,0:T(8,128)} %copy.23.root_ref, f32[256,256]{1,0:T(8,128)} %convolution_bitcast_fusion.term_ref, bf16[256,256]{1,0:T(8,128)(2,1)} %bitcast.44), custom_call_target="tpu_custom_call" | custom-call | tf_op jit(solution)/shard_map/pallas_call | solution.py:274
  174.8 1.7 broadcast_multiply_fusion
  176.5 1.5 copy.38
  (5 shorter events, 0.0 us)
Async XLA Ops:
  65.5 5.2 %copy-start.1 = (s32[1,8,8,16,128]{4,3,2,1,0:T(8,128)S(1)}, s32[1,8,8,16,128]{4,3,2,1,0:T(8,128)}, u32[]{:S(2)}) copy-start(s32[1,8,8,16,128]{4,3,2,1,0:T(8,128)} %param.10) | copy-start | bytes 1572868
  70.6 5.7 %copy-start.3 = (s32[1,8]{1,0:T(1,128)S(1)}, s32[1,8]{1,0:T(1,128)}, u32[]{:S(2)}) copy-start(s32[1,8]{1,0:T(1,128)} %param.12) | copy-start | bytes 100
  76.1 5.0 %copy-start.2 = (bf16[8,128,256]{2,1,0:T(8,128)(2,1)S(1)}, bf16[8,128,256]{2,1,0:T(8,128)(2,1)}, u32[]{:S(2)}) copy-start(bf16[8,128,256]{2,1,0:T(8,128)(2,1)} %get-tuple-element.7) | copy-start | bytes 1572868
  76.3 7.5 %copy-start = (bf16[256,256]{1,0:T(8,128)(2,1)S(1)}, bf16[256,256]{1,0:T(8,128)(2,1)}, u32[]{:S(2)}) copy-start(bf16[256,256]{1,0:T(8,128)(2,1)} %param.9) | copy-start | bytes 393220

commit v10 on v9

--- a/solution.py
+++ b/solution.py
@@ -290,12 +290,45 @@
     )(partial_sums, share_root[:, None], term, weight.T)
 
 
-def unpack_blocks(words):
-    shifts = jnp.arange(8, dtype=jnp.int32)
-    bit_values = jnp.bitwise_and(
-        jnp.right_shift(words[..., :, None, :], shifts[:, None]), 1
+def slot_kernel(slots, coords_ref, counts_ref, src_ref, words_ref, out_ref):
+    s = pl.program_id(0)
+
+    @pl.when(s == 0)
+    def _():
+        out_ref[...] = jnp.zeros_like(out_ref)
+
+    shifts = lax.broadcasted_iota(jnp.int32, (1, 8, 1), 1)
+    for k in range(slots):
+        @pl.when(k < counts_ref[s])
+        def _():
+            p = coords_ref[s, 0, k]
+            q = coords_ref[s, 1, k]
+            picked = src_ref[0, pl.ds(pl.multiple_of(p * 128, 128), 128), :]
+            words = words_ref[0, k]
+            bits = jnp.bitwise_and(jnp.right_shift(words[:, None, :], shifts), 1)
+            transposed = bits.reshape(128, 128).astype(jnp.bfloat16)
+            rows = pl.ds(pl.multiple_of(q * 128, 128), 128)
+            out_ref[rows, :] += jnp.dot(transposed, picked, preferred_element_type=jnp.float32)
+
+
+def slot_sums(sources, words, coords, counts):
+    steps, slab_rows, width = sources.shape
+    slots = words.shape[1]
+    grid_spec = pltpu.PrefetchScalarGridSpec(
+        num_scalar_prefetch=2,
+        grid=(steps,),
+        in_specs=[
+            pl.BlockSpec((1, slab_rows, width), lambda s, c, n: (s, 0, 0)),
+            pl.BlockSpec((1,) + words.shape[1:], lambda s, c, n: (s, 0, 0, 0)),
+        ],
+        out_specs=pl.BlockSpec((slab_rows, width), lambda s, c, n: (0, 0)),
     )
-    return bit_values.reshape(words.shape[:-2] + (128, 128)).astype(jnp.bfloat16)
+    return pl.pallas_call(
+        functools.partial(slot_kernel, slots),
+        out_shape=jax.ShapeDtypeStruct((slab_rows, width), jnp.float32),
+        grid_spec=grid_spec,
+        compiler_params=pltpu.CompilerParams(dimension_semantics=("arbitrary",)),
+    )(coords, counts, sources, words)
 
 
 def per_device(features, out_grad, weight, block_words, block_coords, block_counts, degrees):
@@ -309,22 +342,7 @@
     scaled = (out_grad.astype(jnp.float32) * inverse_root[:, None]).astype(jnp.bfloat16)
 
     sources, feature_slab = gather_sources(scaled, features, step_count, blocks, group_size)
-    sources = sources.reshape(step_count, row_blocks, 128, width)
-    coords = block_coords[0]
-    slot_total = coords.shape[-1]
-    picked = jnp.take_along_axis(sources, coords[:, 0, :, None, None], axis=1)
-    transposed = unpack_blocks(block_words[0])
-    contrib = jnp.einsum(
-        "skvu,skuf->skvf", transposed, picked, preferred_element_type=jnp.float32
-    )
-    live = jnp.arange(slot_total, dtype=jnp.int32)[None, :] < block_counts[0][:, None]
-    column_ids = jnp.arange(row_blocks, dtype=jnp.int32)
-    placement = (
-        (coords[:, 1, :, None] == column_ids[None, None, :]) & live[:, :, None]
-    ).astype(jnp.float32)
-    accumulated = jnp.einsum("skc,skvf->cvf", placement, contrib)
-
-    partial_sums = accumulated.reshape(slab_rows, width)
+    partial_sums = slot_sums(sources, block_words[0], block_coords[0], block_counts[0])
     share_rows = slab_rows // group_size
     share_root = lax.dynamic_slice_in_dim(inverse_root, rep_index * share_rows, share_rows, 0)
     scaled_sums = (partial_sums * inverse_root[:, None]).astype(jnp.bfloat16)

time: 178 us -> 175 us (0.983)
  Pallas kernels: 152 us -> 162 us
  matrix products: 11.3 us -> 2.42 us
  local copies, waits for them, and re-layouts: 10.1 us -> 3.05 us
  other arithmetic: 4.44 us -> 6.48 us
    dot_general x2 -> x0, matrix products: 10.2 us -> none  [the longest x1 5.46 us: per_device(): jnp.einsum('skvu,skuf->skvf', transposed, picked, preferred_element_type=...]
    pallas_call x0 -> x1, Pallas kernels: none -> 9.76 us  [slot_sums(): pl.pallas_call(functools.partial(slot_kernel, slots), out_shape=jax.Shape...]
    gather x2 -> x0, local copies, waits for them, and re-layouts: 5.13 us -> none  [per_device(): picked = jnp.take_along_axis(sources, coords[:, 0, :, None, None], axis=1)]
    convert_element_type x0 -> x1, other arithmetic: none -> 2.06 us  [per_device(): partial_sums.astype(jnp.bfloat16)]
where the time goes in v10:
time: 175 us
  Pallas kernels  162 us (93%)
  other arithmetic  6.48 us (4%)
  local copies, waits for them, and re-layouts  3.05 us (2%)
  matrix products  2.42 us (1%)
    pallas_call x1, Pallas kernels, finish(): pl.pallas_call(functools.partial(finish_kernel, group, digits), out_shape...  90.8 us
    pallas_call x1, Pallas kernels, gather_sources(): pl.pallas_call(functools.partial(gather_kernel, steps, blocks, plans, gro...  61.3 us
    pallas_call x1, Pallas kernels, slot_sums(): pl.pallas_call(functools.partial(slot_kernel, slots), out_shape=jax.Shape...  9.76 us

profile of v10, /device:TPU:1, one launch (start us, length us, event | category | flops | bytes accessed | tf_op | source)
XLA Modules:
  0.0 174.5 jit_solution(12626028046774242446)
XLA Ops:
  0.6 0.7 convert_rsqrt_fusion
  1.3 2.1 %multiply_convert_fusion.1.slab_ref = bf16[1024,256]{1,0:T(8,128)(2,1)} fusion(bf16[1024,256]{1,0:T(8,128)(2,1)} %param.8, f32[1024]{0:T(1024)S(1)} %convert_rsqrt_fusion), kind=kLoop, calls=%fused_computation.1 | loop fusion | flops 786432 | bytes 1052672 | tf_op jit(solution)/shard_map/convert_element_type | solution.py:342
  3.4 61.3 %shard_map.86 = (bf16[8,1024,256]{2,1,0:T(8,128)(2,1)}, bf16[8,128,256]{2,1,0:T(8,128)(2,1)}) custom-call(bf16[1024,256]{1,0:T(8,128)(2,1)} %multiply_convert_fusion.1.slab_ref, bf16[128,256]{1,0:T(8,128)(2,1)} %feat_ref.1), custom_call_target="tpu_custom_call" | custom-call | tf_op jit(solution)/shard_map/pallas_call | solution.py:160
  64.7 0.0 copy-start
  64.7 0.0 copy-start.1
  64.7 9.8 %shard_map.87 = f32[1024,256]{1,0:T(8,128)} custom-call(s32[8,2,8]{2,1,0:T(2,128)} %bitcast.11, s32[8]{0:T(128)} %bitcast.12, bf16[8,1024,256]{2,1,0:T(8,128)(2,1)} %get-tuple-element.6.src_ref, s32[8,8,16,128]{3,2,1,0:T(8,128)} %bitcast.8), custom_call_target="tpu_custom_call" | custom-call | tf_op jit(solution)/shard_map/pallas_call | solution.py:326
  74.5 0.0 copy-done
  74.5 2.4 %fusion.term_ref = f32[256,256]{1,0:T(8,128)} fusion(bf16[1024,256]{1,0:T(8,128)(2,1)S(1)} %bitcast.9, f32[1024,256]{1,0:T(8,128)} %shard_map.87, f32[1024]{0:T(1024)S(1)} %convert_rsqrt_fusion), kind=kOutput, calls=%fused_computation.2 | convolution fusion | flops 134742016 | bytes 1839104 | tf_op jit(solution)/shard_map/dot_general | solution.py:349
  76.9 0.1 dynamic-slice_bitcast_fusion
  77.0 0.7 copy.12.root_ref
  77.7 2.1 %convert_element_type.18.partial_ref = bf16[1024,256]{1,0:T(8,128)(2,1)} convert(f32[1024,256]{1,0:T(8,128)} %shard_map.87) | non-fusion elementwise | flops 262144 | bytes 1572864 | tf_op jit(solution)/shard_map/convert_element_type | solution.py:353
  79.8 0.0 copy-done.1
  79.8 0.7 copy.11
  80.5 90.8 %shard_map.88 = (bf16[128,256]{1,0:T(8,128)(2,1)}, f32[256,256]{1,0:T(8,128)}) custom-call(bf16[1024,256]{1,0:T(8,128)(2,1)} %convert_element_type.18.partial_ref, f32[128,1]{1,0:T(8,128)} %copy.12.root_ref, f32[256,256]{1,0:T(8,128)} %fusion.term_ref, bf16[256,256]{1,0:T(8,128)(2,1)} %bitcast.10), custom_call_target="tpu_custom_call" | custom-call | tf_op jit(solution)/shard_map/pallas_call | solution.py:274
  171.4 1.7 broadcast_multiply_fusion
  173.0 1.5 copy.15
Async XLA Ops:
  64.7 9.8 %copy-start = (bf16[8,128,256]{2,1,0:T(8,128)(2,1)S(1)}, bf16[8,128,256]{2,1,0:T(8,128)(2,1)}, u32[]{:S(2)}) copy-start(bf16[8,128,256]{2,1,0:T(8,128)(2,1)} %get-tuple-element.7) | copy-start | bytes 1572868
  64.7 15.1 %copy-start.1 = (bf16[256,256]{1,0:T(8,128)(2,1)S(1)}, bf16[256,256]{1,0:T(8,128)(2,1)}, u32[]{:S(2)}) copy-start(bf16[256,256]{1,0:T(8,128)(2,1)} %param.9) | copy-start | bytes 393220

commit v11 on v10

--- a/solution.py
+++ b/solution.py
@@ -177,8 +177,8 @@
     )(scaled, features)
 
 
-def finish_kernel(group, digits, partial_ref, root_ref, term_ref, weight_t_ref, grad_ref, out_ref,
-                  sums_in, inbox, spread, gathered, sems):
+def finish_kernel(group, digits, partial_ref, root_ref, feat_ref, scaled_ref, weight_t_ref, grad_ref,
+                  out_ref, term_ref, sums_in, inbox, spread, gathered, sems):
     me = lax.axis_index("blk")
     rep = lax.axis_index("rep")
     share = grad_ref.shape[0]
@@ -194,6 +194,9 @@
                 barrier, inc=1, device_id=(jnp.bitwise_xor(me, d << shift), rep), device_id_type=MESH_ID
             )
             blk_count += 1
+    term_ref[...] = lax.dot_general(
+        feat_ref[...], scaled_ref[...], (((0,), (0,)), ((), ())), preferred_element_type=jnp.float32
+    )
     pl.semaphore_wait(barrier, group - 1 + blk_count)
 
     def send(src, dst, sem_row, slot, device):
@@ -262,35 +265,37 @@
         out_ref[pl.ds(r * piece, piece)] = gathered[r]
 
 
-def finish(partial_sums, share_root, term, weight):
+def finish(partial_sums, share_root, feature_slab, scaled_sums, weight):
     group = lax.axis_size("rep")
     bits = lax.axis_size("blk").bit_length() - 1
     digits = [(shift, min(3, bits - shift)) for shift in range(0, bits, 3)]
     slab_rows, width = partial_sums.shape
     share = slab_rows // group
-    fan = term.shape[0]
+    fan = feature_slab.shape[1]
     piece = fan // group
     vmem = pl.BlockSpec(memory_space=pltpu.VMEM)
     return pl.pallas_call(
         functools.partial(finish_kernel, group, digits),
         out_shape=(
             jax.ShapeDtypeStruct((share, weight.shape[0]), jnp.bfloat16),
-            jax.ShapeDtypeStruct(term.shape, jnp.float32),
+            jax.ShapeDtypeStruct((fan, width), jnp.float32),
         ),
-        in_specs=[vmem] * 4,
+        in_specs=[vmem] * 5,
         out_specs=(vmem, vmem),
         scratch_shapes=[
+            pltpu.VMEM((fan, width), jnp.float32),
             pltpu.VMEM((group, share, width), partial_sums.dtype),
-            pltpu.VMEM((group, piece, term.shape[1]), jnp.float32),
-            pltpu.VMEM((len(digits) + 2, 8, piece, term.shape[1]), jnp.float32),
-            pltpu.VMEM((group, piece, term.shape[1]), jnp.float32),
+            pltpu.VMEM((group, piece, width), jnp.float32),
+            pltpu.VMEM((len(digits) + 2, 8, piece, width), jnp.float32),
+            pltpu.VMEM((group, piece, width), jnp.float32),
             pltpu.SemaphoreType.DMA((2, len(digits) + 3, 8)),
         ],
         compiler_params=pltpu.CompilerParams(collective_id=1, has_side_effects=True),
-    )(partial_sums, share_root[:, None], term, weight.T)
-
-
-def slot_kernel(slots, coords_ref, counts_ref, src_ref, words_ref, out_ref):
+    )(partial_sums, share_root[:, None], feature_slab, scaled_sums, weight.T)
+
+
+def slot_kernel(slots, coords_ref, counts_ref, src_ref, words_ref, root_ref, out_ref, sums_ref,
+                scaled_ref):
     s = pl.program_id(0)
 
     @pl.when(s == 0)
@@ -310,8 +315,13 @@
             rows = pl.ds(pl.multiple_of(q * 128, 128), 128)
             out_ref[rows, :] += jnp.dot(transposed, picked, preferred_element_type=jnp.float32)
 
-
-def slot_sums(sources, words, coords, counts):
+    @pl.when(s == pl.num_programs(0) - 1)
+    def _():
+        sums_ref[...] = out_ref[...].astype(sums_ref.dtype)
+        scaled_ref[...] = (out_ref[...] * root_ref[...]).astype(scaled_ref.dtype)
+
+
+def slot_sums(sources, words, coords, counts, inverse_root):
     steps, slab_rows, width = sources.shape
     slots = words.shape[1]
     grid_spec = pltpu.PrefetchScalarGridSpec(
@@ -320,15 +330,25 @@
         in_specs=[
             pl.BlockSpec((1, slab_rows, width), lambda s, c, n: (s, 0, 0)),
             pl.BlockSpec((1,) + words.shape[1:], lambda s, c, n: (s, 0, 0, 0)),
-        ],
-        out_specs=pl.BlockSpec((slab_rows, width), lambda s, c, n: (0, 0)),
-    )
-    return pl.pallas_call(
+            pl.BlockSpec((slab_rows, 1), lambda s, c, n: (0, 0)),
+        ],
+        out_specs=[
+            pl.BlockSpec((slab_rows, width), lambda s, c, n: (0, 0)),
+            pl.BlockSpec((slab_rows, width), lambda s, c, n: (0, 0)),
+            pl.BlockSpec((slab_rows, width), lambda s, c, n: (0, 0)),
+        ],
+    )
+    _, sums, scaled_sums = pl.pallas_call(
         functools.partial(slot_kernel, slots),
-        out_shape=jax.ShapeDtypeStruct((slab_rows, width), jnp.float32),
+        out_shape=[
+            jax.ShapeDtypeStruct((slab_rows, width), jnp.float32),
+            jax.ShapeDtypeStruct((slab_rows, width), jnp.bfloat16),
+            jax.ShapeDtypeStruct((slab_rows, width), jnp.bfloat16),
+        ],
         grid_spec=grid_spec,
         compiler_params=pltpu.CompilerParams(dimension_semantics=("arbitrary",)),
-    )(coords, counts, sources, words)
+    )(coords, counts, sources, words, inverse_root[:, None])
+    return sums, scaled_sums
 
 
 def per_device(features, out_grad, weight, block_words, block_coords, block_counts, degrees):
@@ -342,15 +362,14 @@
     scaled = (out_grad.astype(jnp.float32) * inverse_root[:, None]).astype(jnp.bfloat16)
 
     sources, feature_slab = gather_sources(scaled, features, step_count, blocks, group_size)
-    partial_sums = slot_sums(sources, block_words[0], block_coords[0], block_counts[0])
+    partial_sums, scaled_sums = slot_sums(
+        sources, block_words[0], block_coords[0], block_counts[0], inverse_root
+    )
     share_rows = slab_rows // group_size
     share_root = lax.dynamic_slice_in_dim(inverse_root, rep_index * share_rows, share_rows, 0)
-    scaled_sums = (partial_sums * inverse_root[:, None]).astype(jnp.bfloat16)
-    term = lax.dot_general(
-        feature_slab.reshape(slab_rows, -1), scaled_sums, (((0,), (0,)), ((), ())),
-        preferred_element_type=jnp.float32,
-    )
-    input_grad, weight_sum = finish(partial_sums.astype(jnp.bfloat16), share_root, term, weight)
+    input_grad, weight_sum = finish(
+        partial_sums, share_root, feature_slab.reshape(slab_rows, -1), scaled_sums, weight
+    )
     node_total = slab_rows * blocks
     weight_grad = weight_sum * (1.0 / math.sqrt(node_total))
     return (input_grad, weight_grad)

time: 175 us -> 174 us (level)
  Pallas kernels: 162 us -> 165 us
  matrix products: 2.42 us -> 0 us
  other arithmetic: 6.48 us -> 4.45 us
    dot_general x1 -> x0, matrix products: 2.42 us -> none  [per_device(): lax.dot_general(feature_slab.reshape(slab_rows, -1), scaled_sums, (((0,),...]
    convert_element_type x1 -> x0, other arithmetic: 2.06 us -> none  [per_device(): partial_sums.astype(jnp.bfloat16)]
    pallas_call x1, Pallas kernels: 90.8 us -> 92.9 us  [finish(): pl.pallas_call(functools.partial(finish_kernel, group, digits), out_shape...]
where the time goes in v11:
time: 174 us
  Pallas kernels  165 us (95%)
  other arithmetic  4.45 us (3%)
  local copies, waits for them, and re-layouts  4.1 us (2%)
    pallas_call x1, Pallas kernels, finish(): pl.pallas_call(functools.partial(finish_kernel, group, digits), out_shape...  92.9 us
    pallas_call x1, Pallas kernels, gather_sources(): pl.pallas_call(functools.partial(gather_kernel, steps, blocks, plans, gro...  61.3 us
    pallas_call x1, Pallas kernels, slot_sums(): pl.pallas_call(functools.partial(slot_kernel, slots), out_shape=[jax.Shap...  10.7 us

profile of v11, /device:TPU:1, one launch (start us, length us, event | category | flops | bytes accessed | tf_op | source)
XLA Modules:
  0.0 174.1 jit_solution(7241223959242046402)
XLA Ops:
  0.6 0.0 copy-start
  0.6 0.7 convert_rsqrt_fusion
  1.4 2.1 %multiply_convert_fusion.slab_ref = bf16[1024,256]{1,0:T(8,128)(2,1)} fusion(bf16[1024,256]{1,0:T(8,128)(2,1)} %param.8, f32[1024]{0:T(1024)S(1)} %convert_rsqrt_fusion), kind=kLoop, calls=%fused_computation | loop fusion | flops 786432 | bytes 1052672 | tf_op jit(solution)/shard_map/convert_element_type | solution.py:362
  3.4 61.3 %shard_map.86 = (bf16[8,1024,256]{2,1,0:T(8,128)(2,1)}, bf16[8,128,256]{2,1,0:T(8,128)(2,1)}) custom-call(bf16[1024,256]{1,0:T(8,128)(2,1)} %multiply_convert_fusion.slab_ref, bf16[128,256]{1,0:T(8,128)(2,1)} %feat_ref.1), custom_call_target="tpu_custom_call" | custom-call | tf_op jit(solution)/shard_map/pallas_call | solution.py:160
  64.7 1.0 copy.15.root_ref
  65.8 10.7 %shard_map.87 = (f32[1024,256]{1,0:T(8,128)}, bf16[1024,256]{1,0:T(8,128)(2,1)}, bf16[1024,256]{1,0:T(8,128)(2,1)}) custom-call(s32[8,2,8]{2,1,0:T(2,128)} %bitcast.12, s32[8]{0:T(128)} %bitcast.13, bf16[8,1024,256]{2,1,0:T(8,128)(2,1)} %get-tuple-element.8.src_ref, s32[8,8,16,128]{3,2,1,0:T(8,128)} %bitcast.10, f32[1024,1]{1,0:T(8,128)} %copy.15.root_ref), custom_call_target="tpu_custom_call" | custom-call | tf_op jit(solution)/shard_map/pallas_call | solution.py:341
  76.5 0.1 dynamic-slice_bitcast_fusion
  76.6 0.7 copy.17.root_ref
  77.3 0.0 copy-done
  77.3 0.8 copy.16
  78.1 92.9 %shard_map.88 = (bf16[128,256]{1,0:T(8,128)(2,1)}, f32[256,256]{1,0:T(8,128)}) custom-call(bf16[1024,256]{1,0:T(8,128)(2,1)} %get-tuple-element.9.partial_ref, f32[128,1]{1,0:T(8,128)} %copy.17.root_ref, bf16[1024,256]{1,0:T(8,128)(2,1)} %bitcast.8, bf16[1024,256]{1,0:T(8,128)(2,1)} %get-tuple-element.11.scaled_ref, bf16[256,256]{1,0:T(8,128)(2,1)} %bitcast.9), custom_call_target="tpu_custom_call" | custom-call | tf_op jit(solution)/shard_map/pallas_call | solution.py:277
  170.9 1.7 broadcast_multiply_fusion
  172.6 1.5 copy.20
Async XLA Ops:
  0.6 76.7 %copy-start = (bf16[256,256]{1,0:T(8,128)(2,1)S(1)}, bf16[256,256]{1,0:T(8,128)(2,1)}, u32[]{:S(2)}) copy-start(bf16[256,256]{1,0:T(8,128)(2,1)} %param.9) | copy-start | bytes 393220

commit v12 on v11

--- a/solution.py
+++ b/solution.py
@@ -107,9 +107,6 @@
                     feat_copy(j, partner).start()
                 for c in range(direct, CHUNKS):
                     relay_out(c, ahead).start()
-                for c in range(direct, CHUNKS):
-                    relay_out(c, ahead).wait_recv()
-                    relay_on(c, ahead).start()
             else:
                 pl.semaphore_wait(barrier, 4 + group - 1)
                 for c in range(CHUNKS):
@@ -120,6 +117,14 @@
     sent = []
     for k in range(1, centre + 1):
         for c in range(CHUNKS):
+            if k == 1:
+                for plane, (direct, sign, leg) in enumerate(plans):
+                    if c >= direct:
+                        @pl.when(rep == plane)
+                        def _():
+                            ahead = lax.rem(me + sign * leg + blocks, blocks)
+                            relay_out(c, ahead).wait_recv()
+                            relay_on(c, ahead).start()
             up = centre + k
             down = centre - k
             if up < steps:

time: 174 us -> 207 us (1.19)
  Pallas kernels: 165 us -> 197 us
    pallas_call x1, Pallas kernels: 92.9 us -> 126 us  [finish(): pl.pallas_call(functools.partial(finish_kernel, group, digits), out_shape...]
where the time goes in v12:
time: 207 us
  Pallas kernels  197 us (95%)
  other arithmetic  4.45 us (2%)
  local copies, waits for them, and re-layouts  4.1 us (2%)
    pallas_call x1, Pallas kernels, finish(): pl.pallas_call(functools.partial(finish_kernel, group, digits), out_shape...  126 us
    pallas_call x1, Pallas kernels, gather_sources(): pl.pallas_call(functools.partial(gather_kernel, steps, blocks, plans, gro...  61.3 us
    pallas_call x1, Pallas kernels, slot_sums(): pl.pallas_call(functools.partial(slot_kernel, slots), out_shape=[jax.Shap...  9.95 us

profile of v12, /device:TPU:1, one launch (start us, length us, event | category | flops | bytes accessed | tf_op | source)
XLA Modules:
  0.0 206.6 jit_solution(58292377396606124)
XLA Ops:
  0.6 0.0 copy-start
  0.6 0.7 convert_rsqrt_fusion
  1.4 2.1 multiply_convert_fusion.slab_ref
  3.4 61.3 %shard_map.86 = (bf16[8,1024,256]{2,1,0:T(8,128)(2,1)}, bf16[8,128,256]{2,1,0:T(8,128)(2,1)}) custom-call(bf16[1024,256]{1,0:T(8,128)(2,1)} %multiply_convert_fusion.slab_ref, bf16[128,256]{1,0:T(8,128)(2,1)} %feat_ref.1), custom_call_target="tpu_custom_call" | custom-call | tf_op jit(solution)/shard_map/pallas_call | solution.py:165
  64.7 1.0 copy.15.root_ref
  65.8 9.9 %shard_map.87 = (f32[1024,256]{1,0:T(8,128)}, bf16[1024,256]{1,0:T(8,128)(2,1)}, bf16[1024,256]{1,0:T(8,128)(2,1)}) custom-call(s32[8,2,8]{2,1,0:T(2,128)} %bitcast.12, s32[8]{0:T(128)} %bitcast.13, bf16[8,1024,256]{2,1,0:T(8,128)(2,1)} %get-tuple-element.8.src_ref, s32[8,8,16,128]{3,2,1,0:T(8,128)} %bitcast.10, f32[1024,1]{1,0:T(8,128)} %copy.15.root_ref), custom_call_target="tpu_custom_call" | custom-call | tf_op jit(solution)/shard_map/pallas_call | solution.py:346
  75.7 0.1 dynamic-slice_bitcast_fusion
  75.8 0.7 copy.17.root_ref
  76.5 0.0 copy-done
  76.5 0.8 copy.16
  77.3 126.2 %shard_map.88 = (bf16[128,256]{1,0:T(8,128)(2,1)}, f32[256,256]{1,0:T(8,128)}) custom-call(bf16[1024,256]{1,0:T(8,128)(2,1)} %get-tuple-element.9.partial_ref, f32[128,1]{1,0:T(8,128)} %copy.17.root_ref, bf16[1024,256]{1,0:T(8,128)(2,1)} %bitcast.8, bf16[1024,256]{1,0:T(8,128)(2,1)} %get-tuple-element.11.scaled_ref, bf16[256,256]{1,0:T(8,128)(2,1)} %bitcast.9), custom_call_target="tpu_custom_call" | custom-call | tf_op jit(solution)/shard_map/pallas_call | solution.py:282
  203.5 1.7 broadcast_multiply_fusion
  205.1 1.5 copy.20
Async XLA Ops:
  0.6 75.9 %copy-start = (bf16[256,256]{1,0:T(8,128)(2,1)S(1)}, bf16[256,256]{1,0:T(8,128)(2,1)}, u32[]{:S(2)}) copy-start(bf16[256,256]{1,0:T(8,128)(2,1)} %param.9) | copy-start | bytes 393220

commit v13 on v11

--- a/solution.py
+++ b/solution.py
@@ -8,7 +8,7 @@
 from jax.experimental.pallas import tpu as pltpu
 from jax.sharding import PartitionSpec as P
 
-CHUNKS = 16
+CHUNKS = 8
 MESH_ID = pl.DeviceIdType.MESH
 
 
@@ -17,7 +17,7 @@
     for rep in range(group):
         reach = steps * rep + steps // 2
         short = min(reach, blocks - reach)
-        if 16 * short < 3 * blocks:
+        if 4 * short < 5 * blocks // 4:
             plans.append((CHUNKS, 0, 0))
             continue
         direct = min(CHUNKS, max(1, int(CHUNKS * (blocks - short) / blocks + 0.5)))

time: 174 us -> 178 us (1.023)
  Pallas kernels: 165 us -> 168 us
    pallas_call x1, Pallas kernels: 92.9 us -> 97.7 us  [finish(): pl.pallas_call(functools.partial(finish_kernel, group, digits), out_shape...]
where the time goes in v13:
time: 178 us
  Pallas kernels  168 us (94%)
  other arithmetic  4.45 us (2%)
  local copies, waits for them, and re-layouts  4.1 us (2%)
    pallas_call x1, Pallas kernels, finish(): pl.pallas_call(functools.partial(finish_kernel, group, digits), out_shape...  97.7 us
    pallas_call x1, Pallas kernels, gather_sources(): pl.pallas_call(functools.partial(gather_kernel, steps, blocks, plans, gro...  60.1 us
    pallas_call x1, Pallas kernels, slot_sums(): pl.pallas_call(functools.partial(slot_kernel, slots), out_shape=[jax.Shap...  10.6 us

profile of v13, /device:TPU:1, one launch (start us, length us, event | category | flops | bytes accessed | tf_op | source)
XLA Modules:
  0.0 177.6 jit_solution(16476485832646719278)
XLA Ops:
  0.6 0.0 copy-start
  0.6 0.7 convert_rsqrt_fusion
  1.4 2.1 %multiply_convert_fusion.slab_ref = bf16[1024,256]{1,0:T(8,128)(2,1)} fusion(bf16[1024,256]{1,0:T(8,128)(2,1)} %param.8, f32[1024]{0:T(1024)S(1)} %convert_rsqrt_fusion), kind=kLoop, calls=%fused_computation | loop fusion | flops 786432 | bytes 1052672 | tf_op jit(solution)/shard_map/convert_element_type | solution.py:362
  3.4 60.1 %shard_map.86 = (bf16[8,1024,256]{2,1,0:T(8,128)(2,1)}, bf16[8,128,256]{2,1,0:T(8,128)(2,1)}) custom-call(bf16[1024,256]{1,0:T(8,128)(2,1)} %multiply_convert_fusion.slab_ref, bf16[128,256]{1,0:T(8,128)(2,1)} %feat_ref.1), custom_call_target="tpu_custom_call" | custom-call | tf_op jit(solution)/shard_map/pallas_call | solution.py:160
  63.5 1.0 copy.15.root_ref
  64.6 10.6 %shard_map.87 = (f32[1024,256]{1,0:T(8,128)}, bf16[1024,256]{1,0:T(8,128)(2,1)}, bf16[1024,256]{1,0:T(8,128)(2,1)}) custom-call(s32[8,2,8]{2,1,0:T(2,128)} %bitcast.12, s32[8]{0:T(128)} %bitcast.13, bf16[8,1024,256]{2,1,0:T(8,128)(2,1)} %get-tuple-element.8.src_ref, s32[8,8,16,128]{3,2,1,0:T(8,128)} %bitcast.10, f32[1024,1]{1,0:T(8,128)} %copy.15.root_ref), custom_call_target="tpu_custom_call" | custom-call | tf_op jit(solution)/shard_map/pallas_call | solution.py:341
  75.1 0.1 dynamic-slice_bitcast_fusion
  75.2 0.7 copy.17.root_ref
  75.9 0.0 copy-done
  76.0 0.8 copy.16
  76.7 97.7 %shard_map.88 = (bf16[128,256]{1,0:T(8,128)(2,1)}, f32[256,256]{1,0:T(8,128)}) custom-call(bf16[1024,256]{1,0:T(8,128)(2,1)} %get-tuple-element.9.partial_ref, f32[128,1]{1,0:T(8,128)} %copy.17.root_ref, bf16[1024,256]{1,0:T(8,128)(2,1)} %bitcast.8, bf16[1024,256]{1,0:T(8,128)(2,1)} %get-tuple-element.11.scaled_ref, bf16[256,256]{1,0:T(8,128)(2,1)} %bitcast.9), custom_call_target="tpu_custom_call" | custom-call | tf_op jit(solution)/shard_map/pallas_call | solution.py:277
  174.5 1.7 broadcast_multiply_fusion
  176.1 1.5 copy.20
Async XLA Ops:
  0.6 75.3 %copy-start = (bf16[256,256]{1,0:T(8,128)(2,1)S(1)}, bf16[256,256]{1,0:T(8,128)(2,1)}, u32[]{:S(2)}) copy-start(bf16[256,256]{1,0:T(8,128)(2,1)} %param.9) | copy-start | bytes 393220

commit v14 on v11

--- a/solution.py
+++ b/solution.py
@@ -177,7 +177,7 @@
     )(scaled, features)
 
 
-def finish_kernel(group, digits, partial_ref, root_ref, feat_ref, scaled_ref, weight_t_ref, grad_ref,
+def finish_kernel(group, digits, scale, partial_ref, root_ref, feat_ref, scaled_ref, weight_t_ref, grad_ref,
                   out_ref, term_ref, sums_in, inbox, spread, gathered, sems):
     me = lax.axis_index("blk")
     rep = lax.axis_index("rep")
@@ -262,10 +262,10 @@
     for c in spreads:
         c.wait()
     for r in range(group):
-        out_ref[pl.ds(r * piece, piece)] = gathered[r]
-
-
-def finish(partial_sums, share_root, feature_slab, scaled_sums, weight):
+        out_ref[pl.ds(r * piece, piece)] = gathered[r] * scale
+
+
+def finish(partial_sums, share_root, feature_slab, scaled_sums, weight, scale):
     group = lax.axis_size("rep")
     bits = lax.axis_size("blk").bit_length() - 1
     digits = [(shift, min(3, bits - shift)) for shift in range(0, bits, 3)]
@@ -275,7 +275,7 @@
     piece = fan // group
     vmem = pl.BlockSpec(memory_space=pltpu.VMEM)
     return pl.pallas_call(
-        functools.partial(finish_kernel, group, digits),
+        functools.partial(finish_kernel, group, digits, scale),
         out_shape=(
             jax.ShapeDtypeStruct((share, weight.shape[0]), jnp.bfloat16),
             jax.ShapeDtypeStruct((fan, width), jnp.float32),
@@ -367,11 +367,11 @@
     )
     share_rows = slab_rows // group_size
     share_root = lax.dynamic_slice_in_dim(inverse_root, rep_index * share_rows, share_rows, 0)
-    input_grad, weight_sum = finish(
-        partial_sums, share_root, feature_slab.reshape(slab_rows, -1), scaled_sums, weight
-    )
     node_total = slab_rows * blocks
-    weight_grad = weight_sum * (1.0 / math.sqrt(node_total))
+    input_grad, weight_grad = finish(
+        partial_sums, share_root, feature_slab.reshape(slab_rows, -1), scaled_sums, weight,
+        1.0 / math.sqrt(node_total),
+    )
     return (input_grad, weight_grad)
 
 

time: 174 us -> 173 us (level)
  Pallas kernels: 165 us -> 163 us
    unnamed x4 -> x5, local copies, waits for them, and re-layouts: 2.24 us -> 3.91 us
where the time goes in v14:
time: 173 us; the launch traced here: 172 us
  Pallas kernels  163 us (94%)
  local copies, waits for them, and re-layouts  5.77 us (3%)
  other arithmetic  2.78 us (2%)
    pallas_call x1, Pallas kernels, finish(): pl.pallas_call(functools.partial(finish_kernel, group, digits, scale), ou...  91.7 us
    pallas_call x1, Pallas kernels, gather_sources(): pl.pallas_call(functools.partial(gather_kernel, steps, blocks, plans, gro...  61.3 us
    pallas_call x1, Pallas kernels, slot_sums(): pl.pallas_call(functools.partial(slot_kernel, slots), out_shape=[jax.Shap...  10.1 us
    unnamed x5, local copies, waits for them, and re-layouts  3.91 us

profile of v14, /device:TPU:1, one launch (start us, length us, event | category | flops | bytes accessed | tf_op | source)
XLA Modules:
  0.0 172.3 jit_solution(6060970966298772649)
XLA Ops:
  0.6 0.0 copy-start
  0.6 0.7 convert_rsqrt_fusion
  1.4 2.1 %multiply_convert_fusion.slab_ref = bf16[1024,256]{1,0:T(8,128)(2,1)} fusion(bf16[1024,256]{1,0:T(8,128)(2,1)} %param.8, f32[1024]{0:T(1024)S(1)} %convert_rsqrt_fusion), kind=kLoop, calls=%fused_computation | loop fusion | flops 786432 | bytes 1052672 | tf_op jit(solution)/shard_map/convert_element_type | solution.py:362
  3.4 61.3 %shard_map.86 = (bf16[8,1024,256]{2,1,0:T(8,128)(2,1)}, bf16[8,128,256]{2,1,0:T(8,128)(2,1)}) custom-call(bf16[1024,256]{1,0:T(8,128)(2,1)} %multiply_convert_fusion.slab_ref, bf16[128,256]{1,0:T(8,128)(2,1)} %feat_ref.1), custom_call_target="tpu_custom_call" | custom-call | tf_op jit(solution)/shard_map/pallas_call | solution.py:160
  64.7 1.0 copy.15.root_ref
  65.8 10.1 %shard_map.87 = (f32[1024,256]{1,0:T(8,128)}, bf16[1024,256]{1,0:T(8,128)(2,1)}, bf16[1024,256]{1,0:T(8,128)(2,1)}) custom-call(s32[8,2,8]{2,1,0:T(2,128)} %bitcast.12, s32[8]{0:T(128)} %bitcast.13, bf16[8,1024,256]{2,1,0:T(8,128)(2,1)} %get-tuple-element.6.src_ref, s32[8,8,16,128]{3,2,1,0:T(8,128)} %bitcast.10, f32[1024,1]{1,0:T(8,128)} %copy.15.root_ref), custom_call_target="tpu_custom_call" | custom-call | tf_op jit(solution)/shard_map/pallas_call | solution.py:341
  75.9 0.1 dynamic-slice_bitcast_fusion
  76.0 0.7 copy.17.root_ref
  76.7 0.0 copy-done
  76.7 0.8 copy.16
  77.5 91.7 %shard_map.88 = (bf16[128,256]{1,0:T(8,128)(2,1)}, f32[256,256]{1,0:T(8,128)}) custom-call(bf16[1024,256]{1,0:T(8,128)(2,1)} %get-tuple-element.7.partial_ref, f32[128,1]{1,0:T(8,128)} %copy.17.root_ref, bf16[1024,256]{1,0:T(8,128)(2,1)} %bitcast.8, bf16[1024,256]{1,0:T(8,128)(2,1)} %get-tuple-element.9.scaled_ref, bf16[256,256]{1,0:T(8,128)(2,1)} %bitcast.9), custom_call_target="tpu_custom_call" | custom-call | tf_op jit(solution)/shard_map/pallas_call | solution.py:277
  169.2 1.5 copy.21
  170.6 1.7 copy.22
Async XLA Ops:
  0.6 76.1 %copy-start = (bf16[256,256]{1,0:T(8,128)(2,1)S(1)}, bf16[256,256]{1,0:T(8,128)(2,1)}, u32[]{:S(2)}) copy-start(bf16[256,256]{1,0:T(8,128)(2,1)} %param.9) | copy-start | bytes 393220
